TPU v7x, 32 devices: a whole 2x2x4 slice. The times are simulated.
32 devices in a mesh: dp: 8 (over y, x, core), tensor: 4 (over z).
Axes of the slice: x: 2, y: 2, z: 4, core: 2. Of those that a mesh axis runs over, the one named last changes fastest.
Arguments:
- tokens: bfloat16 [2, 8192, 2048], P(None, ('dp', 'tensor')), may hold values from -6 to 6
- segments: int32 [2, 8, 1024], P(None, 'dp'), may hold values from 0 to 15, never falling along the last dimension, each value on 1 to 512 neighbouring positions
- query_weight: bfloat16 [2048, 2048], P('dp', 'tensor'), may hold values from -0.125 to 0.125
- key_weight: bfloat16 [2048, 2048], P('dp', 'tensor'), may hold values from -0.125 to 0.125
- value_weight: bfloat16 [2048, 2048], P('dp', 'tensor'), may hold values from -0.125 to 0.125
- output_weight: bfloat16 [2048, 2048], P('tensor', 'dp'), may hold values from -0.75 to 0.75
- expand_weight: bfloat16 [2048, 8192], P('dp', 'tensor'), may hold values from -0.125 to 0.125
- contract_weight: bfloat16 [8192, 2048], P('tensor', 'dp'), may hold values from -0.09375 to 0.09375
- norm_gains: bfloat16 [2, 2048], P(None, 'dp'), may hold values from 0.099609375 to 1.8984375
- norm_shifts: bfloat16 [2, 2048], P(None, 'dp'), may hold values from -1.75 to 1.75
- cotangent: bfloat16 [2, 8192, 2048], P(None, ('dp', 'tensor')), may hold values from -6 to 6
Outputs:
- result: bfloat16 [2, 8192, 2048], P(None, ('dp', 'tensor'))
- tokens_grad: float32 [2, 8192, 2048], P(None, ('dp', 'tensor'))
- query_grad: float32 [2048, 2048], P('dp', 'tensor')
- key_grad: float32 [2048, 2048], P('dp', 'tensor')
- value_grad: float32 [2048, 2048], P('dp', 'tensor')
- output_grad: float32 [2048, 2048], P('tensor', 'dp')
- expand_grad: float32 [2048, 8192], P('dp', 'tensor')
- contract_grad: float32 [8192, 2048], P('tensor', 'dp')
- gains_grad: float32 [2, 2048], P(None, 'dp')
- shifts_grad: float32 [2, 2048], P(None, 'dp')
Inputs may be any that keep to these rules, and one draw needn't show every extreme that they name: `segments`: along each packed row of 1024 tokens the numbers never fall; each document has 1 to 512 tokens. Numbers only compare tokens of the same row.
All inputs are finite; a program needn't handle non-finite values.
Results may differ from a plain program's by a relative error of at most 0.019.
Values may be sent and summed in bfloat16 or wider, within the bound.
No kernel may reach another device: no remote copies, remote signals or barrier semaphores. Data moves between devices by JAX's collectives and lax.ppermute only.
A program may use at most 256 MiB of HBM per device.

v0:
```python
import jax
import jax.numpy as jnp
from jax import lax
from jax.sharding import PartitionSpec as P

DH = 128


EPSILON = 1e-06
NEGATIVE = -1e30


def layer_norm(values, gain, shift):
    average = jnp.mean(values, axis=-1, keepdims=True)
    centered = values - average
    variance = jnp.mean(centered * centered, axis=-1, keepdims=True)
    return centered * lax.rsqrt(variance + EPSILON) * gain + shift


def gelu_tanh(values):
    return jax.nn.gelu(values, approximate=True)


def plain_dot(left, right):
    return jnp.dot(left, right, preferred_element_type=jnp.float32)


def inner_dot(left, right):
    return lax.dot_general(
        left, right, (((0,), (0,)), ((), ())), preferred_element_type=jnp.float32
    )


def outer_dot(left, right):
    return lax.dot_general(
        left, right, (((1,), (1,)), ((), ())), preferred_element_type=jnp.float32
    )


def masked_scores(query_block, key_row, segment_block, segment_row):
    scores = jnp.einsum(
        "qhd,khd->hqk", query_block, key_row, preferred_element_type=jnp.float32
    ) * DH ** (-0.5)
    matching = segment_block[:, None] == segment_row[None, :]
    return jnp.where(matching[None], scores, NEGATIVE)


def attention_forward(query, keys, values, segment_rows):
    seq_length = query.shape[1]
    block = min(512, seq_length)
    count = seq_length // block

    def one_row(inputs):
        query_row, key_row, value_row, segment_row = inputs
        query_blocks = query_row.reshape(count, block, query_row.shape[1], query_row.shape[2])
        segment_blocks = segment_row.reshape(count, block)

        def one_block(pair):
            query_block, segment_block = pair
            scores = masked_scores(query_block, key_row, segment_block, segment_row)
            row_top = jnp.max(scores, axis=-1, keepdims=True)
            exponent = jnp.exp(scores - row_top)
            total = jnp.sum(exponent, axis=-1, keepdims=True)
            probs = (exponent / total).astype(jnp.bfloat16)
            context = jnp.einsum(
                "hqk,khd->qhd", probs, value_row, preferred_element_type=jnp.float32
            )
            return (context.astype(jnp.bfloat16), (row_top + jnp.log(total))[..., 0])

        contexts, logsums = lax.map(one_block, (query_blocks, segment_blocks))
        return (contexts.reshape(query_row.shape), logsums)

    return lax.map(one_row, (query, keys, values, segment_rows))


def attention_backward(query, keys, values, context_grad, logsums, segment_rows):
    seq_length = query.shape[1]
    block = min(512, seq_length)
    count = seq_length // block

    def one_row(inputs):
        query_row, key_row, value_row, grad_row, logsum_row, segment_row = inputs
        shape = (count, block, query_row.shape[1], query_row.shape[2])

        def one_block(carry, pieces):
            key_total, value_total = carry
            query_block, grad_block, logsum_block, segment_block = pieces
            scores = masked_scores(query_block, key_row, segment_block, segment_row)
            probs = jnp.exp(scores - logsum_block[..., None])
            value_total = value_total + jnp.einsum(
                "hqk,qhd->khd",
                probs.astype(jnp.bfloat16),
                grad_block,
                preferred_element_type=jnp.float32,
            )
            prob_grad = jnp.einsum(
                "qhd,khd->hqk", grad_block, value_row, preferred_element_type=jnp.float32
            )
            weighted = jnp.sum(probs * prob_grad, axis=-1, keepdims=True)
            score_grad = (probs * (prob_grad - weighted)).astype(jnp.bfloat16)
            query_part = jnp.einsum(
                "hqk,khd->qhd", score_grad, key_row, preferred_element_type=jnp.float32
            ) * DH ** (-0.5)
            key_total = key_total + jnp.einsum(
                "hqk,qhd->khd", score_grad, query_block, preferred_element_type=jnp.float32
            ) * DH ** (-0.5)
            return ((key_total, value_total), query_part)

        starting = (jnp.zeros(key_row.shape, jnp.float32), jnp.zeros(value_row.shape, jnp.float32))
        (key_total, value_total), query_parts = lax.scan(
            one_block,
            starting,
            (
                query_row.reshape(shape),
                grad_row.reshape(shape),
                logsum_row,
                segment_row.reshape(count, block),
            ),
        )
        return (
            query_parts.reshape(query_row.shape).astype(jnp.bfloat16),
            key_total.astype(jnp.bfloat16),
            value_total.astype(jnp.bfloat16),
        )

    return lax.map(one_row, (query, keys, values, context_grad, logsums, segment_rows))


def fetch(
    query_weight,
    key_weight,
    value_weight,
    expand_weight,
    output_weight,
    contract_weight,
    norm_gains,
    norm_shifts,
):
    by_rows = (
        lax.all_gather(query_weight, "dp", axis=0, tiled=True),
        lax.all_gather(key_weight, "dp", axis=0, tiled=True),
        lax.all_gather(value_weight, "dp", axis=0, tiled=True),
        lax.all_gather(expand_weight, "dp", axis=0, tiled=True),
    )
    by_columns = (
        lax.all_gather(output_weight, "dp", axis=1, tiled=True),
        lax.all_gather(contract_weight, "dp", axis=1, tiled=True),
        lax.all_gather(norm_gains, "dp", axis=1, tiled=True),
        lax.all_gather(norm_shifts, "dp", axis=1, tiled=True),
    )
    return (
        by_rows[0],
        by_rows[1],
        by_rows[2],
        by_rows[3],
        by_columns[0],
        by_columns[1],
        by_columns[2],
        by_columns[3],
    )


def per_device(
    tokens,
    segments,
    query_weight,
    key_weight,
    value_weight,
    output_weight,
    expand_weight,
    contract_weight,
    norm_gains,
    norm_shifts,
    cotangent,
):
    shards = (
        query_weight,
        key_weight,
        value_weight,
        expand_weight,
        output_weight,
        contract_weight,
        norm_gains,
        norm_shifts,
    )
    micro_count = tokens.shape[0]
    width = tokens.shape[2]
    row_count = segments.shape[1]
    seq_length = segments.shape[2]
    local_width = query_weight.shape[1]
    local_heads = local_width // DH
    hidden_width = expand_weight.shape[1]
    query_sum = jnp.zeros((width, local_width), jnp.float32)
    key_sum = jnp.zeros((width, local_width), jnp.float32)
    value_sum = jnp.zeros((width, local_width), jnp.float32)
    expand_sum = jnp.zeros((width, hidden_width), jnp.float32)
    output_sum = jnp.zeros((local_width, width), jnp.float32)
    contract_sum = jnp.zeros((hidden_width, width), jnp.float32)
    gain_sum = jnp.zeros((2, width), jnp.float32)
    shift_sum = jnp.zeros((2, width), jnp.float32)
    outputs = []
    input_grads = []

    def heads_view(matrix):
        return matrix.reshape(row_count, seq_length, local_heads, DH)

    for micro in range(micro_count):
        ahead = fetch(*shards)
        (
            full_query,
            full_key,
            full_value,
            full_expand,
            full_output,
            full_contract,
            full_gains,
            full_shifts,
        ) = ahead
        gains = full_gains.astype(jnp.float32)
        shifts = full_shifts.astype(jnp.float32)
        block_tokens = tokens[micro]
        block_segments = segments[micro]
        gathered = lax.all_gather(block_tokens, "tensor", axis=0, tiled=True)
        query = plain_dot(gathered, full_query).astype(jnp.bfloat16)
        keys = plain_dot(gathered, full_key).astype(jnp.bfloat16)
        values = plain_dot(gathered, full_value).astype(jnp.bfloat16)
        context, logsums = attention_forward(
            heads_view(query), heads_view(keys), heads_view(values), block_segments
        )
        context = context.reshape(row_count * seq_length, local_width)
        attended = lax.psum_scatter(
            plain_dot(context, full_output), "tensor", scatter_dimension=0, tiled=True
        )
        first_in = block_tokens.astype(jnp.float32) + attended
        normed = layer_norm(first_in, gains[0], shifts[0])
        normed_all = lax.all_gather(normed.astype(jnp.bfloat16), "tensor", axis=0, tiled=True)
        hidden = plain_dot(normed_all, full_expand)
        active = gelu_tanh(hidden).astype(jnp.bfloat16)
        branch = lax.psum_scatter(
            plain_dot(active, full_contract), "tensor", scatter_dimension=0, tiled=True
        )
        second_in = normed + branch
        outcome, second_pull = jax.vjp(layer_norm, second_in, gains[1], shifts[1])
        outputs.append(outcome.astype(jnp.bfloat16))
        behind = fetch(*shards)
        (
            back_query,
            back_key,
            back_value,
            back_expand,
            back_output,
            back_contract,
            back_gains,
            back_shifts,
        ) = behind
        back_gain = back_gains.astype(jnp.float32)
        second_grad, second_gain_grad, second_shift_grad = second_pull(
            cotangent[micro].astype(jnp.float32)
        )
        branch_all = lax.all_gather(second_grad.astype(jnp.bfloat16), "tensor", axis=0, tiled=True)
        contract_sum = contract_sum + inner_dot(active, branch_all)
        active_grad = outer_dot(branch_all, back_contract)
        gelu_pull = jax.vjp(gelu_tanh, hidden)[1]
        hidden_grad = gelu_pull(active_grad)[0].astype(jnp.bfloat16)
        expand_sum = expand_sum + inner_dot(normed_all, hidden_grad)
        normed_grad = second_grad + lax.psum_scatter(
            outer_dot(hidden_grad, back_expand), "tensor", scatter_dimension=0, tiled=True
        )
        first_pull = jax.vjp(layer_norm, first_in, back_gain[0], shifts[0])[1]
        first_grad, first_gain_grad, first_shift_grad = first_pull(normed_grad)
        gain_sum = gain_sum + jnp.stack([first_gain_grad, second_gain_grad])
        shift_sum = shift_sum + jnp.stack([first_shift_grad, second_shift_grad])
        attention_all = lax.all_gather(
            first_grad.astype(jnp.bfloat16), "tensor", axis=0, tiled=True
        )
        output_sum = output_sum + inner_dot(context, attention_all)
        context_grad = outer_dot(attention_all, back_output).astype(jnp.bfloat16)
        query_grad, key_grad, value_grad = attention_backward(
            heads_view(query),
            heads_view(keys),
            heads_view(values),
            heads_view(context_grad),
            logsums,
            block_segments,
        )
        query_grad = query_grad.reshape(row_count * seq_length, local_width)
        key_grad = key_grad.reshape(row_count * seq_length, local_width)
        value_grad = value_grad.reshape(row_count * seq_length, local_width)
        query_sum = query_sum + inner_dot(gathered, query_grad)
        key_sum = key_sum + inner_dot(gathered, key_grad)
        value_sum = value_sum + inner_dot(gathered, value_grad)
        total = outer_dot(query_grad, back_query)
        total = total + outer_dot(key_grad, back_key)
        input_grads.append(
            first_grad
            + lax.psum_scatter(
                (total + outer_dot(value_grad, back_value)).astype(jnp.bfloat16),
                "tensor",
                scatter_dimension=0,
                tiled=True,
            ).astype(jnp.float32)
        )
    norm_totals = (
        lax.psum(gain_sum.astype(jnp.bfloat16), "tensor").astype(jnp.float32),
        lax.psum(shift_sum.astype(jnp.bfloat16), "tensor").astype(jnp.float32),
    )
    row_grads = (
        lax.psum_scatter(
            query_sum.astype(jnp.bfloat16), "dp", scatter_dimension=0, tiled=True
        ).astype(jnp.float32),
        lax.psum_scatter(
            key_sum.astype(jnp.bfloat16), "dp", scatter_dimension=0, tiled=True
        ).astype(jnp.float32),
        lax.psum_scatter(
            value_sum.astype(jnp.bfloat16), "dp", scatter_dimension=0, tiled=True
        ).astype(jnp.float32),
        lax.psum_scatter(
            expand_sum.astype(jnp.bfloat16), "dp", scatter_dimension=0, tiled=True
        ).astype(jnp.float32),
    )
    column_grads = (
        lax.psum_scatter(
            output_sum.astype(jnp.bfloat16), "dp", scatter_dimension=1, tiled=True
        ).astype(jnp.float32),
        lax.psum_scatter(
            contract_sum.astype(jnp.bfloat16), "dp", scatter_dimension=1, tiled=True
        ).astype(jnp.float32),
        lax.psum_scatter(
            norm_totals[0].astype(jnp.bfloat16), "dp", scatter_dimension=1, tiled=True
        ).astype(jnp.float32),
        lax.psum_scatter(
            norm_totals[1].astype(jnp.bfloat16), "dp", scatter_dimension=1, tiled=True
        ).astype(jnp.float32),
    )
    return (
        jnp.stack(outputs),
        jnp.stack(input_grads),
        row_grads[0],
        row_grads[1],
        row_grads[2],
        column_grads[0],
        row_grads[3],
        column_grads[1],
        column_grads[2],
        column_grads[3],
    )


def solution(mesh):
    in_specs = (
        P(None, ("dp", "tensor"), None),
        P(None, "dp", None),
        P("dp", "tensor"),
        P("dp", "tensor"),
        P("dp", "tensor"),
        P("tensor", "dp"),
        P("dp", "tensor"),
        P("tensor", "dp"),
        P(None, "dp"),
        P(None, "dp"),
        P(None, ("dp", "tensor"), None),
    )
    out_specs = (
        P(None, ("dp", "tensor"), None),
        P(None, ("dp", "tensor"), None),
        P("dp", "tensor"),
        P("dp", "tensor"),
        P("dp", "tensor"),
        P("tensor", "dp"),
        P("dp", "tensor"),
        P("tensor", "dp"),
        P(None, "dp"),
        P(None, "dp"),
    )
    return jax.shard_map(
        per_device, mesh=mesh, in_specs=in_specs, out_specs=out_specs, check_vma=False
    )
```

profile of v0, /device:TPU:0, one launch (start us, length us, event | category | flops | bytes accessed | tf_op | source)
XLA Modules:
  0.0 2413.9 jit_solution(9187912460696633784)
XLA Ops:
  13.7 26.7 %all-gather.17.cloned.1.call-done = bf16[2048,512]{1,0:T(8,128)(2,1)} async-done(((bf16[256,512]{1,0:T(8,128)(2,1)}), bf16[2048,512]{1,0:T(8,128)(2,1)}) %all-gather.17.cloned.1.call-update) | async-done | bytes 2097168 | tf_op jit(solution)/shard_map/all_gather | solution.py:140
  40.4 82.9 %all-gather.43.cloned.1.call-done = bf16[1,1024,2048]{2,1,0:T(8,128)(2,1)} async-done(((bf16[1,256,2048]{2,1,0:T(8,128)(2,1)}), bf16[1,1024,2048]{2,1,0:T(8,128)(2,1)}) %all-gather.43.cloned.1.call-update) | async-done | bytes 4194320 | tf_op jit(solution)/shard_map/all_gather | solution.py:223
  129.0 22.6 all-gather.19.cloned.1.call-done
  157.4 23.6 all-gather.21.cloned.1.call-done
  218.6 75.1 %all-gather.41.cloned.1.call-done = bf16[1,1024,2048]{2,1,0:T(8,128)(2,1)} async-done(((bf16[1,256,2048]{2,1,0:T(8,128)(2,1)}), bf16[1,1024,2048]{2,1,0:T(8,128)(2,1)}) %all-gather.41.cloned.1.call-update) | async-done | bytes 4194320 | tf_op jit(solution)/shard_map/all_gather | solution.py:223
  361.0 78.2 %reduce-scatter.25.cloned.1.call-done = f32[256,2048]{1,0:T(8,128)} async-done(((f32[1024,2048]{1,0:T(8,128)}), f32[256,2048]{1,0:T(8,128)}) %reduce-scatter.25.cloned.1.call-update) | async-done | bytes 2097168 | tf_op jit(solution)/shard_map/reduce_scatter | solution.py:231
  439.2 147.6 %reduce-scatter.21.cloned.1.call-done = f32[256,2048]{1,0:T(8,128)} async-done(((f32[1024,2048]{1,0:T(8,128)}), f32[256,2048]{1,0:T(8,128)}) %reduce-scatter.21.cloned.1.call-update) | async-done | bytes 2097168 | tf_op jit(solution)/shard_map/reduce_scatter | solution.py:231
  594.0 49.6 %all-gather.27.cloned.1.call-done = bf16[2048,2048]{1,0:T(8,128)(2,1)} async-done(((bf16[256,2048]{1,0:T(8,128)(2,1)}), bf16[2048,2048]{1,0:T(8,128)(2,1)}) %all-gather.27.cloned.1.call-update) | async-done | bytes 8388624 | tf_op jit(solution)/shard_map/all_gather | solution.py:143
  643.6 82.8 %all-gather.25.cloned.1.call-done = bf16[1024,2048]{1,0:T(8,128)(2,1)} async-done(((bf16[256,2048]{1,0:T(8,128)(2,1)}), bf16[1024,2048]{1,0:T(8,128)(2,1)}) %all-gather.25.cloned.1.call-update) | async-done | bytes 4194320 | tf_op jit(solution)/shard_map/all_gather | solution.py:236
  740.8 41.8 %all-gather.29.cloned.1.call-done = bf16[2048,2048]{1,0:T(8,128)(2,1)} async-done(((bf16[2048,256]{1,0:T(8,128)(2,1)}), bf16[2048,2048]{1,0:T(8,128)(2,1)}) %all-gather.29.cloned.1.call-update) | async-done | bytes 8388624 | tf_op jit(solution)/shard_map/all_gather | solution.py:147
  801.0 142.8 %reduce-scatter.23.cloned.1.call-done = f32[256,2048]{1,0:T(8,128)} async-done(((f32[1024,2048]{1,0:T(8,128)}), f32[256,2048]{1,0:T(8,128)}) %reduce-scatter.23.cloned.1.call-update) | async-done | bytes 2097168 | tf_op jit(solution)/shard_map/reduce_scatter | solution.py:239
  948.5 81.2 %all-gather.31.cloned.1.call-done = bf16[1024,2048]{1,0:T(8,128)(2,1)} async-done(((bf16[256,2048]{1,0:T(8,128)(2,1)}), bf16[1024,2048]{1,0:T(8,128)(2,1)}) %all-gather.31.cloned.1.call-update) | async-done | bytes 4194320 | tf_op jit(solution)/shard_map/all_gather | solution.py:236
  1061.8 141.2 %reduce-scatter.27.cloned.1.call-done = f32[256,2048]{1,0:T(8,128)} async-done(((f32[1024,2048]{1,0:T(8,128)}), f32[256,2048]{1,0:T(8,128)}) %reduce-scatter.27.cloned.1.call-update) | async-done | bytes 2097168 | tf_op jit(solution)/shard_map/reduce_scatter | solution.py:239
  1217.5 78.2 %all-gather.37.cloned.1.call-done = bf16[1024,2048]{1,0:T(8,128)(2,1)} async-done(((bf16[256,2048]{1,0:T(8,128)(2,1)}), bf16[1024,2048]{1,0:T(8,128)(2,1)}) %all-gather.37.cloned.1.call-update) | async-done | bytes 4194320 | tf_op jit(solution)/shard_map/all_gather | solution.py:260
  1295.7 18.0 fusion.77
  1329.4 47.5 %all-gather.33.cloned.1.call-done = bf16[1024,2048]{1,0:T(8,128)(2,1)} async-done(((bf16[256,2048]{1,0:T(8,128)(2,1)}), bf16[1024,2048]{1,0:T(8,128)(2,1)}) %all-gather.33.cloned.1.call-update) | async-done | bytes 4194320 | tf_op jit(solution)/shard_map/all_gather | solution.py:260
  1377.0 18.0 fusion.70
  1410.6 111.8 %reduce-scatter.33.cloned.1.call-done = f32[256,2048]{1,0:T(8,128)} async-done(((f32[1024,2048]{1,0:T(8,128)}), f32[256,2048]{1,0:T(8,128)}) %reduce-scatter.33.cloned.1.call-update) | async-done | bytes 2097168 | tf_op jit(solution)/shard_map/reduce_scatter | solution.py:266
  1522.3 147.5 %reduce-scatter.29.cloned.1.call-done = f32[256,2048]{1,0:T(8,128)} async-done(((f32[1024,2048]{1,0:T(8,128)}), f32[256,2048]{1,0:T(8,128)}) %reduce-scatter.29.cloned.1.call-update) | async-done | bytes 2097168 | tf_op jit(solution)/shard_map/reduce_scatter | solution.py:266
  1698.3 20.3 add_convert_fusion
  1771.1 45.2 %while.96 = (s32[]{:T(128)}, f32[1024,4,128]{0,2,1:T(8,128)}, f32[1024,4,128]{0,2,1:T(8,128)}, bf16[2,512,4,128]{3,1,2,0:T(8,128)(2,1)}, bf16[2,512,4,128]{3,1,2...) while((s32[]{:T(128)}, f32[1024,4,128]{0,2,1:T(8,128)}, ...), condition=%wide.region_27.28_spmd.clone, body=%wide.region_25.27_spmd.clone.sunk | while | flops 2719217664 | bytes 181473200 | solution.py:110
  1823.2 19.0 all-gather.39.cloned.1.call-done
  1860.0 43.7 %while.97 = (s32[]{:T(128)}, f32[1024,4,128]{0,2,1:T(8,128)S(1)}, f32[1024,4,128]{0,2,1:T(8,128)}, bf16[2,512,4,128]{3,1,2,0:T(8,128)(2,1)}, bf16[2,512,4,128]{3...) while((s32[]{:T(128)}, f32[1024,4,128]{0,2,1:T(8,128)S(1)}, ...), condition=%wide.region_36.37_spmd.clone, body=%wide.region_34.36_spmd.clone.sunk | while | flops 2719217664 | bytes 181473200 | solution.py:110
  1963.4 27.0 %reduce-scatter.45.cloned.1.call-done = bf16[256,2048]{1,0:T(8,128)(2,1)} async-done(((bf16[2048,2048]{1,0:T(8,128)(2,1)}), bf16[256,2048]{1,0:T(8,128)(2,1)}) %reduce-scatter.45.cloned.1.call-update) | async-done | bytes 1048592 | tf_op jit(solution)/shard_map/reduce_scatter | solution.py:317
  1993.2 35.0 %reduce-scatter.49.cloned.1.call-done = bf16[256,2]{1,0:T(8,128)(2,1)} async-done(((bf16[2048,2]{1,0:T(8,128)(2,1)}), bf16[256,2]{1,0:T(8,128)(2,1)}) %reduce-scatter.49.cloned.1.call-update) | async-done | bytes 1040
  2029.1 36.7 %reduce-scatter.51.cloned.1.call-done = bf16[256,2]{1,0:T(8,128)(2,1)} async-done(((bf16[2048,2]{1,0:T(8,128)(2,1)}), bf16[256,2]{1,0:T(8,128)(2,1)}) %reduce-scatter.51.cloned.1.call-update) | async-done | bytes 1040
  2079.6 30.7 %reduce-scatter.43.cloned.1.call-done = bf16[512,256]{1,0:T(8,128)(2,1)} async-done(((bf16[512,2048]{1,0:T(8,128)(2,1)}), bf16[512,256]{1,0:T(8,128)(2,1)}) %reduce-scatter.43.cloned.1.call-update) | async-done | bytes 262160 | tf_op jit(solution)/shard_map/reduce_scatter | solution.py:322
  2112.1 42.5 %reduce-scatter.41.cloned.1.call-done = bf16[256,512]{0,1:T(8,128)(2,1)} async-done(((bf16[2048,512]{0,1:T(8,128)(2,1)}), bf16[256,512]{0,1:T(8,128)(2,1)}) %reduce-scatter.41.cloned.1.call-update) | async-done | bytes 262160 | tf_op jit(solution)/shard_map/reduce_scatter | solution.py:314
  2156.4 42.4 %reduce-scatter.39.cloned.1.call-done = bf16[256,512]{0,1:T(8,128)(2,1)} async-done(((bf16[2048,512]{0,1:T(8,128)(2,1)}), bf16[256,512]{0,1:T(8,128)(2,1)}) %reduce-scatter.39.cloned.1.call-update) | async-done | bytes 262160 | tf_op jit(solution)/shard_map/reduce_scatter | solution.py:311
  2200.7 42.5 %reduce-scatter.37.cloned.1.call-done = bf16[256,512]{0,1:T(8,128)(2,1)} async-done(((bf16[2048,512]{0,1:T(8,128)(2,1)}), bf16[256,512]{0,1:T(8,128)(2,1)}) %reduce-scatter.37.cloned.1.call-update) | async-done | bytes 262160 | tf_op jit(solution)/shard_map/reduce_scatter | solution.py:308
  2245.1 77.2 %reduce-scatter.31.cloned.1.call-done = bf16[256,2048]{1,0:T(8,128)(2,1)} async-done(((bf16[1024,2048]{1,0:T(8,128)(2,1)}), bf16[256,2048]{1,0:T(8,128)(2,1)}) %reduce-scatter.31.cloned.1.call-update) | async-done | bytes 1048592 | tf_op jit(solution)/shard_map/reduce_scatter | solution.py:296
  2325.9 76.5 %reduce-scatter.35.cloned.1.call-done = bf16[256,2048]{1,0:T(8,128)(2,1)} async-done(((bf16[1024,2048]{1,0:T(8,128)(2,1)}), bf16[256,2048]{1,0:T(8,128)(2,1)}) %reduce-scatter.35.cloned.1.call-update) | async-done | bytes 1048592 | tf_op jit(solution)/shard_map/reduce_scatter | solution.py:296
  (455 shorter events, 565.3 us)
Async XLA Ops:
  7.2 33.2 %all-gather.17.cloned.1.call-start = ((), (), s32[]{:S(2)}) async-start(), calls=%async_computation.16 | async-start | bytes 2359296 | tf_op jit(solution)/shard_map/all_gather | solution.py:140
  7.9 115.4 %all-gather.43.cloned.1.call-start = ((), (), s32[]{:S(2)}) async-start(), calls=%async_computation.43 | async-start | bytes 5242880 | tf_op jit(solution)/shard_map/all_gather | solution.py:223
  11.1 140.4 %all-gather.19.cloned.1.call-start = ((), (), s32[]{:S(2)}) async-start(), calls=%async_computation.17 | async-start | bytes 2359296 | tf_op jit(solution)/shard_map/all_gather | solution.py:141
  11.8 169.2 %all-gather.21.cloned.1.call-start = ((), (), s32[]{:S(2)}) async-start(), calls=%async_computation.18 | async-start | bytes 2359296 | tf_op jit(solution)/shard_map/all_gather | solution.py:142
  12.4 198.5 %all-gather.23.cloned.1.call-start = ((), (), s32[]{:S(2)}) async-start(), calls=%async_computation.19 | async-start | bytes 2359296 | tf_op jit(solution)/shard_map/all_gather | solution.py:146
  13.0 280.7 %all-gather.41.cloned.1.call-start = ((), (), s32[]{:S(2)}) async-start(), calls=%async_computation.42 | async-start | bytes 5242880 | tf_op jit(solution)/shard_map/all_gather | solution.py:223
  13.6 425.6 %reduce-scatter.25.cloned.1.call-start = ((), (), s32[]{:S(2)}) async-start(), calls=%async_computation.25 | async-start | bytes 10485760 | tf_op jit(solution)/shard_map/reduce_scatter | solution.py:231
  218.5 368.3 %reduce-scatter.21.cloned.1.call-start = ((), (), s32[]{:S(2)}) async-start(), calls=%async_computation.20 | async-start | bytes 10485760 | tf_op jit(solution)/shard_map/reduce_scatter | solution.py:231
  342.1 301.5 %all-gather.27.cloned.1.call-start = ((), (), s32[]{:S(2)}) async-start(), calls=%async_computation.22 | async-start | bytes 9437184 | tf_op jit(solution)/shard_map/all_gather | solution.py:143
  342.8 383.5 %all-gather.25.cloned.1.call-start = ((), (), s32[]{:S(2)}) async-start(), calls=%async_computation.21 | async-start | bytes 5242880 | tf_op jit(solution)/shard_map/all_gather | solution.py:236
  593.2 189.4 %all-gather.29.cloned.1.call-start = ((), (), s32[]{:S(2)}) async-start(), calls=%async_computation.23 | async-start | bytes 9437184 | tf_op jit(solution)/shard_map/all_gather | solution.py:147
  594.0 349.7 %reduce-scatter.23.cloned.1.call-start = ((), (), s32[]{:S(2)}) async-start(), calls=%async_computation.24 | async-start | bytes 10485760 | tf_op jit(solution)/shard_map/reduce_scatter | solution.py:239
  798.9 230.8 %all-gather.31.cloned.1.call-start = ((), (), s32[]{:S(2)}) async-start(), calls=%async_computation.26 | async-start | bytes 5242880 | tf_op jit(solution)/shard_map/all_gather | solution.py:236
  948.3 254.8 %reduce-scatter.27.cloned.1.call-start = ((), (), s32[]{:S(2)}) async-start(), calls=%async_computation.27 | async-start | bytes 10485760 | tf_op jit(solution)/shard_map/reduce_scatter | solution.py:239
  1059.8 235.9 %all-gather.37.cloned.1.call-start = ((), (), s32[]{:S(2)}) async-start(), calls=%async_computation.32 | async-start | bytes 5242880 | tf_op jit(solution)/shard_map/all_gather | solution.py:260
  1214.2 162.8 %all-gather.33.cloned.1.call-start = ((), (), s32[]{:S(2)}) async-start(), calls=%async_computation.28 | async-start | bytes 5242880 | tf_op jit(solution)/shard_map/all_gather | solution.py:260
  1217.0 305.3 %reduce-scatter.33.cloned.1.call-start = ((), (), s32[]{:S(2)}) async-start(), calls=%async_computation.33 | async-start | bytes 10485760 | tf_op jit(solution)/shard_map/reduce_scatter | solution.py:266
  1329.2 340.6 %reduce-scatter.29.cloned.1.call-start = ((), (), s32[]{:S(2)}) async-start(), calls=%async_computation.29 | async-start | bytes 10485760 | tf_op jit(solution)/shard_map/reduce_scatter | solution.py:266
  1410.5 351.0 %all-gather.35.cloned.1.call-start = ((), (), s32[]{:S(2)}) async-start(), calls=%async_computation.30 | async-start | bytes 5242880 | tf_op jit(solution)/shard_map/all_gather | solution.py:273
  1680.0 162.2 %all-gather.39.cloned.1.call-start = ((), (), s32[]{:S(2)}) async-start(), calls=%async_computation.34 | async-start | bytes 5242880 | tf_op jit(solution)/shard_map/all_gather | solution.py:273
  1681.2 279.4 %reduce-scatter.47.cloned.1.call-start = ((), (), s32[]{:S(2)}) async-start(), calls=%async_computation.41 | async-start | bytes 9437184 | tf_op jit(solution)/shard_map/reduce_scatter | solution.py:325
  1718.7 271.7 %reduce-scatter.45.cloned.1.call-start = ((), (), s32[]{:S(2)}) async-start(), calls=%async_computation.40 | async-start | bytes 9437184 | tf_op jit(solution)/shard_map/reduce_scatter | solution.py:317
  1749.3 278.9 %reduce-scatter.49.cloned.1.call-start = ((), (), s32[]{:S(2)}) async-start(), calls=%async_computation.44 | async-start | bytes 589824
  1752.4 313.4 %reduce-scatter.51.cloned.1.call-start = ((), (), s32[]{:S(2)}) async-start(), calls=%async_computation.45 | async-start | bytes 589824
  1753.7 356.6 %reduce-scatter.43.cloned.1.call-start = ((), (), s32[]{:S(2)}) async-start(), calls=%async_computation.39 | async-start | bytes 2359296 | tf_op jit(solution)/shard_map/reduce_scatter | solution.py:322
  1858.8 295.7 %reduce-scatter.41.cloned.1.call-start = ((), (), s32[]{:S(2)}) async-start(), calls=%async_computation.38 | async-start | bytes 2359296 | tf_op jit(solution)/shard_map/reduce_scatter | solution.py:314
  1914.2 284.6 %reduce-scatter.39.cloned.1.call-start = ((), (), s32[]{:S(2)}) async-start(), calls=%async_computation.37 | async-start | bytes 2359296 | tf_op jit(solution)/shard_map/reduce_scatter | solution.py:311
  1923.5 319.8 %reduce-scatter.37.cloned.1.call-start = ((), (), s32[]{:S(2)}) async-start(), calls=%async_computation.36 | async-start | bytes 2359296 | tf_op jit(solution)/shard_map/reduce_scatter | solution.py:308
  1933.8 388.6 %reduce-scatter.31.cloned.1.call-start = ((), (), s32[]{:S(2)}) async-start(), calls=%async_computation.31 | async-start | bytes 5242880 | tf_op jit(solution)/shard_map/reduce_scatter | solution.py:296
  1944.7 457.7 %reduce-scatter.35.cloned.1.call-start = ((), (), s32[]{:S(2)}) async-start(), calls=%async_computation.35 | async-start | bytes 5242880 | tf_op jit(solution)/shard_map/reduce_scatter | solution.py:296
  1960.7 361.7 %copy-start.69 = (f32[256]{0:T(256)S(1)}, f32[256]{0:T(256)}, u32[]{:S(2)}) copy-start(f32[256]{0:T(256)} %copy-done.68) | copy-start | bytes 3076
  2079.6 322.8 %copy-start.71 = (f32[256]{0:T(256)S(1)}, f32[256]{0:T(256)}, u32[]{:S(2)}) copy-start(f32[256]{0:T(256)} %copy-done.70) | copy-start | bytes 3076
  (100 other events, 1255.6 us)
Sparse Core Ops, SparseCore 0:
  9.9 30.4 all-gather.16
  42.6 80.7 all-gather.42
  125.2 26.2 all-gather.18
  153.3 27.7 all-gather.20
  182.8 28.0 all-gather.22
  212.9 80.7 all-gather.40
  296.1 143.0 reduce-scatter.24
  441.5 145.2 reduce-scatter.20
  588.7 54.8 all-gather.26
  645.6 80.7 all-gather.24
  728.2 54.3 all-gather.28
  799.1 144.6 reduce-scatter.22
  948.4 81.3 all-gather.30
  1059.9 143.0 reduce-scatter.26
  1214.3 81.3 all-gather.36
  1297.7 79.2 all-gather.32
  1379.2 143.0 reduce-scatter.32
  1524.5 145.2 reduce-scatter.28
  1680.1 81.3 all-gather.34
  1762.9 79.2 all-gather.38
  1845.6 69.7 reduce-scatter.46
  1918.9 71.5 reduce-scatter.44
  1994.1 34.0 reduce-scatter.48
  2031.7 34.0 reduce-scatter.50
  2069.1 41.1 reduce-scatter.42
  2113.4 41.0 reduce-scatter.40
  2157.7 41.1 reduce-scatter.38
  2202.1 41.0 reduce-scatter.36
  2245.6 76.7 reduce-scatter.30
  2325.1 77.2 reduce-scatter.34
where the time goes:
time: 2430 us; the launch traced here: 2410 us
  waiting for transfers between devices  1830 us (75%)
  matrix products  394 us (16%)
  other arithmetic  90 us (4%)
  local copies, waits for them, and re-layouts  53.6 us (2%)
  blocking collectives  29.7 us (1%)
    reduce_scatter x2, waiting for transfers between devices, per_device(): lax.psum_scatter(plain_dot(active, full_contract), 'tensor', scatter_dime...  284 us
    reduce_scatter x2, waiting for transfers between devices, per_device(): lax.psum_scatter(outer_dot(hidden_grad, back_expand), 'tensor', scatter_d...  259 us
    reduce_scatter x2, waiting for transfers between devices, per_device(): lax.psum_scatter(plain_dot(context, full_output), 'tensor', scatter_dimen...  226 us
    all_gather x2, waiting for transfers between devices, per_device(): lax.all_gather(normed.astype(jnp.bfloat16), 'tensor', axis=0, tiled=True)  164 us
    all_gather x2, waiting for transfers between devices, per_device(): gathered = lax.all_gather(block_tokens, 'tensor', axis=0, tiled=True)  158 us
    reduce_scatter x2, waiting for transfers between devices, per_device(): lax.psum_scatter((total + outer_dot(value_grad, back_value)).astype(jnp.b...  154 us
    all_gather x2, waiting for transfers between devices, per_device(): lax.all_gather(second_grad.astype(jnp.bfloat16), 'tensor', axis=0, tiled=...  126 us
    dot_general x12, matrix products, plain_dot(): return jnp.dot(left, right, preferred_element_type=jnp.float32)  108 us
  transfers between devices with their start and end apart: 30, of which 29 were waited for; matrix products, arithmetic and copies ran while one was open for 19% of the time, Pallas kernels for 0%

commit v1 on v0

v1 whole, which is shorter than its diff:
```python
import functools

import jax
import jax.numpy as jnp
from jax import lax
from jax.experimental import pallas as pl
from jax.experimental.pallas import tpu as pltpu
from jax.sharding import PartitionSpec as P

DH = 128
EPSILON = 1e-06
NEGATIVE = -1e30
AXES = ("dp", "tensor")
F32 = jnp.float32
BF16 = jnp.bfloat16


def dot_nn(left, right):
    return jnp.dot(left, right, preferred_element_type=F32)


def dot_tn(left, right):
    return lax.dot_general(left, right, (((0,), (0,)), ((), ())), preferred_element_type=F32)


def dot_nt(left, right):
    return lax.dot_general(left, right, (((1,), (1,)), ((), ())), preferred_element_type=F32)


def attention_forward_kernel(qkv_ref, seg_col_ref, seg_row_ref, out_ref, *, block):
    length = qkv_ref.shape[0]
    keys = qkv_ref[:, DH : 2 * DH]
    values = qkv_ref[:, 2 * DH :]
    seg_row = seg_row_ref[...]
    for start in range(0, length, block):
        rows = slice(start, start + block)
        scores = dot_nt(qkv_ref[rows, :DH], keys)
        scores = jnp.where(seg_col_ref[rows, :] == seg_row, scores, NEGATIVE)
        top = jnp.max(scores, axis=1, keepdims=True)
        exponent = jnp.exp((scores - top) * DH**-0.5)
        total = jnp.sum(exponent, axis=1, keepdims=True)
        context = dot_nn(exponent.astype(BF16), values)
        out_ref[rows, :] = (context / total).astype(BF16)


def attention_backward_kernel(
    qkv_ref, grad_ref, seg_col_ref, seg_row_ref, out_ref, key_total, value_total, *, block
):
    length = qkv_ref.shape[0]
    keys = qkv_ref[:, DH : 2 * DH]
    values = qkv_ref[:, 2 * DH :]
    seg_col = seg_col_ref[...]
    for start in range(0, length, block):
        rows = slice(start, start + block)
        query = qkv_ref[rows, :DH]
        grad = grad_ref[rows, :]
        scores = dot_nt(keys, query)
        scores = jnp.where(seg_col == seg_row_ref[:, rows], scores, NEGATIVE)
        top = jnp.max(scores, axis=0, keepdims=True)
        exponent = jnp.exp((scores - top) * DH**-0.5)
        probs = exponent * (1.0 / jnp.sum(exponent, axis=0, keepdims=True))
        prob_grad = dot_nt(values, grad)
        weighted = jnp.sum(probs * prob_grad, axis=0, keepdims=True)
        score_grad = (probs * (prob_grad - weighted)).astype(BF16)
        value_part = dot_nn(probs.astype(BF16), grad)
        key_part = dot_nn(score_grad, query)
        if start == 0:
            value_total[...] = value_part
            key_total[...] = key_part
        else:
            value_total[...] += value_part
            key_total[...] += key_part
        out_ref[rows, :DH] = (dot_tn(score_grad, keys) * DH**-0.5).astype(BF16)
    out_ref[:, DH : 2 * DH] = (key_total[...] * DH**-0.5).astype(BF16)
    out_ref[:, 2 * DH :] = value_total[...].astype(BF16)


def attention_forward(qkv, seg_col, seg_row):
    length, width = qkv.shape
    heads = width // (3 * DH)
    return pl.pallas_call(
        functools.partial(attention_forward_kernel, block=min(256, length)),
        out_shape=jax.ShapeDtypeStruct((length, heads * DH), BF16),
        grid=(heads,),
        in_specs=[
            pl.BlockSpec((length, 3 * DH), lambda i: (0, i)),
            pl.BlockSpec((length, 1), lambda i: (0, 0)),
            pl.BlockSpec((1, length), lambda i: (0, 0)),
        ],
        out_specs=pl.BlockSpec((length, DH), lambda i: (0, i)),
        cost_estimate=pl.CostEstimate(
            flops=4 * heads * length * length * DH,
            transcendentals=heads * length * length,
            bytes_accessed=2 * length * heads * DH * 4,
        ),
        name="attention_forward",
    )(qkv, seg_col, seg_row)


def attention_backward(qkv, grad, seg_col, seg_row):
    length, width = qkv.shape
    heads = width // (3 * DH)
    return pl.pallas_call(
        functools.partial(attention_backward_kernel, block=min(256, length)),
        out_shape=jax.ShapeDtypeStruct((length, width), BF16),
        grid=(heads,),
        in_specs=[
            pl.BlockSpec((length, 3 * DH), lambda i: (0, i)),
            pl.BlockSpec((length, DH), lambda i: (0, i)),
            pl.BlockSpec((length, 1), lambda i: (0, 0)),
            pl.BlockSpec((1, length), lambda i: (0, 0)),
        ],
        out_specs=pl.BlockSpec((length, 3 * DH), lambda i: (0, i)),
        scratch_shapes=[pltpu.VMEM((length, DH), F32), pltpu.VMEM((length, DH), F32)],
        cost_estimate=pl.CostEstimate(
            flops=10 * heads * length * length * DH,
            transcendentals=heads * length * length,
            bytes_accessed=2 * length * heads * DH * 7,
        ),
        name="attention_backward",
    )(qkv, grad, seg_col, seg_row)


def reorder_kernel(mask_ref, in_ref, out_ref):
    out_ref[...] = in_ref[...]


def reorder(array, mask, count):
    rows, width = array.shape
    return pl.pallas_call(
        reorder_kernel,
        out_shape=jax.ShapeDtypeStruct(array.shape, array.dtype),
        grid_spec=pltpu.PrefetchScalarGridSpec(
            num_scalar_prefetch=1,
            grid=(count,),
            in_specs=[pl.BlockSpec((rows, width // count), lambda i, m: (0, i ^ m[0]))],
            out_specs=pl.BlockSpec((rows, width // count), lambda i, m: (0, i)),
        ),
        cost_estimate=pl.CostEstimate(
            flops=0, transcendentals=0, bytes_accessed=4 * rows * width
        ),
        name="reorder",
    )(mask, array)


def norm_forward(values, gain, shift):
    average = jnp.mean(values, axis=-1, keepdims=True)
    centered = values - average
    inverse = lax.rsqrt(jnp.mean(centered * centered, axis=-1, keepdims=True) + EPSILON)
    unit = centered * inverse
    return unit * gain + shift, unit, inverse


def norm_backward(grad, unit, inverse, gain):
    scaled = grad * gain
    first = jnp.mean(scaled, axis=-1, keepdims=True)
    second = jnp.mean(scaled * unit, axis=-1, keepdims=True)
    terms = (jnp.sum(grad * unit, axis=0), jnp.sum(grad, axis=0))
    return (scaled - first - unit * second) * inverse, terms


def gelu_pair(values):
    root = 0.7978845608028654
    square = values * values
    inner = jnp.tanh(root * values * (1.0 + 0.044715 * square))
    half = 0.5 * (1.0 + inner)
    slope = half + 0.5 * values * (1.0 - inner * inner) * root * (1.0 + 3 * 0.044715 * square)
    return values * half, slope


def per_device(
    tokens,
    segments,
    query_weight,
    key_weight,
    value_weight,
    output_weight,
    expand_weight,
    contract_weight,
    norm_gains,
    norm_shifts,
    cotangent,
):
    dp_size = lax.axis_size("dp")
    tensor_size = lax.axis_size("tensor")
    halves = tokens.shape[0]
    tp = tensor_size // halves
    total = dp_size * tensor_size
    block_tokens, width = tokens.shape[1], tokens.shape[2]
    blocks = dp_size
    chips = dp_size // 2
    local_width = query_weight.shape[1]
    heads = local_width // DH
    core_bit, half_bit = tensor_size, tp
    t_bits = [1 << i for i in range(tp.bit_length() - 1)]
    p_bits = [1 << i for i in range(chips.bit_length() - 1)]
    orders = (p_bits, p_bits[::-1])
    dp_index, tensor_index = lax.axis_index("dp"), lax.axis_index("tensor")
    p, c = dp_index // 2, dp_index % 2
    h, t = tensor_index // tp, tensor_index % tp
    basis = p * 2 + h
    basis_ref = basis.astype(jnp.int32).reshape(1)
    home = c * tp + t

    def swap(array, mask):
        return lax.ppermute(array, AXES, [(i, i ^ mask) for i in range(total)])

    def turned(j, back):
        pairs = []
        for i in range(total):
            it = i % tp
            ih = i // tp % halves
            ic = i // tensor_size % 2
            ip = i // tensor_size // 2
            to = ((ip * 2 + ih) * halves + (j ^ ic)) * tp + it
            pairs.append((to, i) if back else (i, to))
        return pairs

    def turn(array, j):
        return lax.ppermute(array, AXES, turned(j, False))

    def turn_back(array, j):
        return lax.ppermute(array, AXES, turned(j, True))

    def fetch(shard, axis):
        found = {}
        for j in range(2):
            own = {0: turn(shard, j)}
            for bit in orders[j]:
                own.update({k | bit: swap(v, bit * 2 * tensor_size) for k, v in own.items()})
            found.update({k * 2 + j: v for k, v in own.items()})
        return jnp.concatenate([found[b] for b in range(blocks)], axis=axis)

    def reduce_grad(pieces):
        sums = []
        for j in range(2):
            own = {k: pieces[k * 2 + j] for k in range(chips)}
            for bit in orders[j][::-1]:
                kept = {}
                for k in own:
                    if not k & bit:
                        got = swap(own[k | bit], bit * 2 * tensor_size)
                        kept[k] = (own[k].astype(F32) + got.astype(F32)).astype(BF16)
                own = kept
            sums.append(turn_back(own[0], j))
        return sums[0].astype(F32) + sums[1].astype(F32)

    def row_pieces(array):
        size = array.shape[0] // blocks
        return [array[b * size : (b + 1) * size] for b in range(blocks)]

    def column_pieces(array):
        size = array.shape[1] // blocks
        return [array[:, b * size : (b + 1) * size] for b in range(blocks)]

    def gather_rows(array):
        parts = [array]
        for bit in t_bits:
            parts = parts + [swap(part, bit) for part in parts]
        parts = parts + [swap(part, core_bit) for part in parts]
        return jnp.concatenate(parts, axis=0)

    def reduce_rows(array):
        array = array.astype(BF16)
        middle = array.shape[0] // 2
        kept = array[:middle].astype(F32) + swap(array[middle:], core_bit).astype(F32)
        for bit in t_bits[::-1]:
            middle = kept.shape[0] // 2
            kept = kept[:middle] + swap(kept[middle:].astype(BF16), bit).astype(F32)
        return kept

    own_params = jnp.concatenate([norm_gains, norm_shifts], axis=0)
    other_params = swap(own_params, core_bit)
    pair = [jnp.where((h ^ j) == c, own_params, other_params) for j in range(2)]
    found = {0: jnp.stack(pair, axis=1)}
    for bit in p_bits:
        found.update({k | bit: swap(v, bit * 2 * tensor_size) for k, v in found.items()})
    params = jnp.stack([found[k] for k in range(chips)], axis=1).reshape(4, width).astype(F32)
    gains, shifts = params[:2], params[2:]

    own_segments = jnp.where(h == 0, segments[0, 0], segments[1, 0])
    other_segments = swap(own_segments, core_bit)

    def segments_of(j):
        row = jnp.where((h ^ j) == c, own_segments, other_segments)
        row = row.reshape(2 * tp, block_tokens)
        bits = [tp] + t_bits
        for bit in bits:
            moved = row.reshape(2 * tp // (2 * bit), 2, bit, block_tokens)
            moved = jnp.concatenate([moved[:, 1:], moved[:, :1]], axis=1)
            row = jnp.where((home & bit) != 0, moved.reshape(row.shape), row)
        row = row.reshape(-1)
        return row[:, None], row[None, :]

    def to_home(array, j):
        piece = jnp.where((j ^ c) == 0, array[0], array[1])
        return reorder(turn(piece, j), basis_ref, blocks)

    def from_home(pieces):
        back = [turn_back(reorder(piece, basis_ref, blocks), j) for j, piece in enumerate(pieces)]
        return jnp.stack(
            [jnp.where(c == 0, back[0], back[1]), jnp.where(c == 0, back[1], back[0])]
        )

    streams = range(2)
    homes = [to_home(tokens, j) for j in streams]
    rows = [gather_rows(x) for x in homes]

    shard = jnp.stack(
        [w.reshape(-1, heads, DH) for w in (query_weight, key_weight, value_weight)], axis=2
    ).reshape(-1, 3 * local_width)
    full_qkv = fetch(shard, 0)
    full_output = fetch(output_weight, 1)
    full_expand = fetch(expand_weight, 0)
    full_contract = fetch(contract_weight, 1)
    segs = [segments_of(j) for j in streams]
    grads_home = [to_home(cotangent, j) for j in streams]

    qkv = [dot_nn(x, full_qkv).astype(BF16) for x in rows]
    context = [attention_forward(qkv[j], *segs[j]) for j in streams]
    first = [
        norm_forward(
            homes[j].astype(F32) + reduce_rows(dot_nn(context[j], full_output)), gains[0], shifts[0]
        )
        for j in streams
    ]
    normed_rows = [gather_rows(first[j][0].astype(BF16)) for j in streams]
    active, slope = [], []
    for j in streams:
        value, derivative = gelu_pair(dot_nn(normed_rows[j], full_expand))
        active.append(value.astype(BF16))
        slope.append(derivative.astype(BF16))
    second = [
        norm_forward(
            first[j][0] + reduce_rows(dot_nn(active[j], full_contract)), gains[1], shifts[1]
        )
        for j in streams
    ]
    result = from_home([second[j][0].astype(BF16) for j in streams])

    branch_grad = [
        norm_backward(grads_home[j].astype(F32), second[j][1], second[j][2], gains[1])
        for j in streams
    ]
    branch_rows = [gather_rows(branch_grad[j][0].astype(BF16)) for j in streams]
    hidden_grad = [
        (dot_nt(branch_rows[j], full_contract) * slope[j].astype(F32)).astype(BF16)
        for j in streams
    ]
    normed_grad = [
        branch_grad[j][0] + reduce_rows(dot_nt(hidden_grad[j], full_expand)) for j in streams
    ]
    contract_grad = sum(dot_tn(active[j], branch_rows[j]) for j in streams).astype(BF16)
    contract_grad = reduce_grad(column_pieces(contract_grad))
    expand_grad = sum(dot_tn(normed_rows[j], hidden_grad[j]) for j in streams).astype(BF16)
    expand_grad = reduce_grad(row_pieces(expand_grad))

    first_grad = [
        norm_backward(normed_grad[j], first[j][1], first[j][2], gains[0]) for j in streams
    ]
    attended_rows = [gather_rows(first_grad[j][0].astype(BF16)) for j in streams]
    output_grad = sum(dot_tn(context[j], attended_rows[j]) for j in streams).astype(BF16)
    output_grad = reduce_grad(column_pieces(output_grad))
    context_grad = [dot_nt(attended_rows[j], full_output).astype(BF16) for j in streams]
    qkv_grad = [attention_backward(qkv[j], context_grad[j], *segs[j]) for j in streams]
    projection_grad = sum(dot_tn(rows[j], qkv_grad[j]) for j in streams).astype(BF16)
    projection_grad = reduce_grad(row_pieces(projection_grad))
    projection_grad = projection_grad.reshape(-1, heads, 3, DH)
    query_grad, key_grad, value_grad = [
        projection_grad[:, :, i].reshape(-1, local_width) for i in range(3)
    ]
    tokens_grad = from_home(
        [
            (first_grad[j][0] + reduce_rows(dot_nt(qkv_grad[j], full_qkv))).astype(BF16)
            for j in streams
        ]
    ).astype(F32)

    terms = jnp.stack(
        [
            sum(first_grad[j][1][0] for j in streams),
            sum(branch_grad[j][1][0] for j in streams),
            sum(first_grad[j][1][1] for j in streams),
            sum(branch_grad[j][1][1] for j in streams),
        ]
    )
    for bit in t_bits + [core_bit]:
        terms = terms + swap(terms, bit)
    terms = terms.reshape(4, chips, 2, -1)
    for bit in p_bits[::-1]:
        middle = terms.shape[1] // 2
        terms = terms[:, :middle] + swap(terms[:, middle:], bit * 2 * tensor_size)
    terms = turn_back(terms[:, 0, 0], 0) + turn_back(terms[:, 0, 1], 1)

    return (
        result,
        tokens_grad,
        query_grad,
        key_grad,
        value_grad,
        output_grad,
        expand_grad,
        contract_grad,
        terms[:2],
        terms[2:],
    )


def solution(mesh):
    in_specs = (
        P(None, ("dp", "tensor"), None),
        P(None, "dp", None),
        P("dp", "tensor"),
        P("dp", "tensor"),
        P("dp", "tensor"),
        P("tensor", "dp"),
        P("dp", "tensor"),
        P("tensor", "dp"),
        P(None, "dp"),
        P(None, "dp"),
        P(None, ("dp", "tensor"), None),
    )
    out_specs = (
        P(None, ("dp", "tensor"), None),
        P(None, ("dp", "tensor"), None),
        P("dp", "tensor"),
        P("dp", "tensor"),
        P("dp", "tensor"),
        P("tensor", "dp"),
        P("dp", "tensor"),
        P("tensor", "dp"),
        P(None, "dp"),
        P(None, "dp"),
    )
    return jax.shard_map(
        per_device, mesh=mesh, in_specs=in_specs, out_specs=out_specs, check_vma=False
    )
```

time: 2430 us -> 1360 us (0.56)
  waiting for transfers between devices: 1830 us -> 395 us
  starting transfers between devices: 3.44 us -> 384 us
  matrix products: 394 us -> 278 us
  Pallas kernels: 0 us -> 113 us
  local copies, waits for them, and re-layouts: 53.6 us -> 87.6 us
  blocking collectives: 29.7 us -> 0 us
    reduce_scatter x14 -> x0, waiting for transfers between devices: 1110 us -> none  [the longest x2 284 us: per_device(): lax.psum_scatter(plain_dot(active, full_contract), 'tensor', scatter_dime...]
    all_gather x14 -> x0, waiting for transfers between devices: 642 us -> none  [the longest x2 164 us: per_device(): lax.all_gather(normed.astype(jnp.bfloat16), 'tensor', axis=0, tiled=True)]
    ppermute x0 -> x123, waiting for transfers between devices: none -> 395 us  [the longest x97 311 us: swap(): return lax.ppermute(array, AXES, [(i, i ^ mask) for i in range(total)])]
    ppermute x0 -> x123, starting transfers between devices: none -> 384 us  [the longest x97 255 us: swap(): return lax.ppermute(array, AXES, [(i, i ^ mask) for i in range(total)])]
    dot_general x64 -> x24, matrix products: 394 us -> 278 us  [the longest x8 97.4 us: dot_tn(): lax.dot_general(left, right, (((0,), (0,)), ((), ())), preferred_element_...]
    pallas_call x0 -> x12, Pallas kernels: none -> 113 us  [the longest x2 46.3 us: attention_backward(): pl.pallas_call(functools.partial(attention_backward_kernel, block=min(256...]
    unnamed x32 -> x0, waiting for transfers between devices: 76.4 us -> none
    unnamed x139 -> x244, local copies, waits for them, and re-layouts: 25 us -> 57.6 us
  transfers between devices with their start and end apart: 30 -> 123, of which waited for: 29 -> 37; matrix products, arithmetic and copies ran while one was open for 19% -> 30% of each run, Pallas kernels for 0% -> 7%
where the time goes in v1:
time: 1360 us; the launch traced here: 1340 us
  waiting for transfers between devices  395 us (29%)
  starting transfers between devices  384 us (28%)
  matrix products  278 us (20%)
  Pallas kernels  113 us (8%)
  local copies, waits for them, and re-layouts  87.6 us (6%)
  other arithmetic  82 us (6%)
    ppermute x97, waiting for transfers between devices, swap(): return lax.ppermute(array, AXES, [(i, i ^ mask) for i in range(total)])  311 us
    ppermute x97, starting transfers between devices, swap(): return lax.ppermute(array, AXES, [(i, i ^ mask) for i in range(total)])  255 us
    dot_general x8, matrix products, dot_tn(): lax.dot_general(left, right, (((0,), (0,)), ((), ())), preferred_element_...  97.4 us
    dot_general x8, matrix products, dot_nt(): lax.dot_general(left, right, (((1,), (1,)), ((), ())), preferred_element_...  95.3 us
    dot_general x8, matrix products, dot_nn(): return jnp.dot(left, right, preferred_element_type=F32)  85.5 us
    ppermute x14, waiting for transfers between devices, turn_back(): return lax.ppermute(array, AXES, turned(j, True))  76.6 us
    ppermute x14, starting transfers between devices, turn_back(): return lax.ppermute(array, AXES, turned(j, True))  69.5 us
    ppermute x12, starting transfers between devices, turn(): return lax.ppermute(array, AXES, turned(j, False))  58.9 us
  transfers between devices with their start and end apart: 123, of which 37 were waited for; matrix products, arithmetic and copies ran while one was open for 30% of the time, Pallas kernels for 7%

profile of v1, /device:TPU:0, one launch (start us, length us, event | category | flops | bytes accessed | tf_op | source)
XLA Modules:
  0.0 1341.7 jit_solution(17698249132083645734)
XLA Ops:
  49.3 26.0 %collective-permute-start.1 = (bf16[256,2048]{1,0:T(8,128)(2,1)}, bf16[256,2048]{1,0:T(8,128)(2,1)S(1)}, u32[]{:S(2)}, u32[]{:S(2)}) collective-permute-start(bf16[256,2048]{1,0:T(8,128)(2,1)} %reorder.8), channel_id=1, source_target_pairs={{0,1},{1,0},{2,3},{3,2},{4,5},{5,4},{6,7},{7,6},{8,9},{9,8},{10,11... | collective-permute-start | bytes 3145736 | tf_op jit(solution)/shard_map/ppermute | solution.py:206
  110.5 16.6 %collective-permute-done.10 = bf16[256,1536]{0,1:T(8,128)(2,1)S(1)} collective-permute-done((bf16[256,1536]{0,1:T(8,128)(2,1)S(1)}, bf16[256,1536]{0,1:T(8,128)(2,1)S(1)}, u32[]{:S(2)}, u32[]{:S(2)}) %collective-permute-start.10) | collective-permute-done | bytes 786464 | tf_op jit(solution)/shard_map/ppermute | solution.py:206
  179.0 20.4 %collective-permute-start.21 = (bf16[512,2048]{1,0:T(8,128)(2,1)}, bf16[512,2048]{1,0:T(8,128)(2,1)}, u32[]{:S(2)}, u32[]{:S(2)}) collective-permute-start(bf16[512,2048]{1,0:T(8,128)(2,1)} %slice.407), channel_id=1, source_target_pairs={{0,4},{1,5},{2,6},{3,7},{4,0},{5,1},{6,2},{7,3},{8,12},{9,13},{10,... | collective-permute-start | bytes 6291464 | tf_op jit(solution)/shard_map/ppermute | solution.py:206
  233.4 13.8 %collective-permute-done.32 = bf16[256,2048]{1,0:T(8,128)(2,1)} collective-permute-done((bf16[256,2048]{1,0:T(8,128)(2,1)}, bf16[256,2048]{1,0:T(8,128)(2,1)}, u32[]{:S(2)}, u32[]{:S(2)}) %collective-permute-start.32) | collective-permute-done | bytes 1048608 | tf_op jit(solution)/shard_map/ppermute | solution.py:206
  269.7 14.6 %collective-permute-start.50 = (bf16[256,2048]{1,0:T(8,128)(2,1)S(1)}, bf16[256,2048]{1,0:T(8,128)(2,1)S(1)}, u32[]{:S(2)}, u32[]{:S(2)}) collective-permute-start(bf16[256,2048]{1,0:T(8,128)(2,1)S(1)} %copy-done.20), channel_id=1, source_target_pairs={{0,1},{1,0},{2,3},{3,2},{4,5},{5,4},{6,7},{7,6},{8,9},{9,8},{10,11... | collective-permute-start | bytes 3145736 | tf_op jit(solution)/shard_map/ppermute | solution.py:206
  373.4 14.6 %fusion.30 = f32[1024,2048]{1,0:T(8,128)} fusion(bf16[2048,2048]{1,0:T(8,128)(2,1)} %constant_dynamic-update-slice_fusion.16, bf16[256,2048]{1,0:T(8,128)(2,1)S(1)} %collective-permute-done.29, bf16[256,2048]{1,0:T(8,128)(2,1)S(1)} %collective-permute-done.28, bf16[256,2048]{1,0:T(8,128)(2,1)} %collective-permute-done.27, bf16[256,2048]{1,0:T(8,128)(2,1)} %fusion.24), kind=kOutput, calls=%fused_computation.146 | convolution fusion | flops 8606711808 | bytes 20971520 | tf_op jit(solution)/shard_map/dot_general | solution.py:19
  388.0 14.5 %convolution_convert_fusion.8 = bf16[1024,2048]{1,0:T(8,128)(2,1)S(1)} fusion(bf16[2048,2048]{1,0:T(8,128)(2,1)} %constant_dynamic-update-slice_fusion.24, f32[1024,2048]{1,0:T(8,128)} %fusion.30), kind=kOutput, calls=%fused_computation.38 | convolution fusion | flops 8610906112 | bytes 20971520 | tf_op jit(solution)/shard_map/dot_general | solution.py:19
  425.2 21.8 %collective-permute-done.47 = bf16[256,2048]{1,0:T(8,128)(2,1)} collective-permute-done((bf16[256,2048]{1,0:T(8,128)(2,1)}, bf16[256,2048]{1,0:T(8,128)(2,1)}, u32[]{:S(2)}, u32[]{:S(2)}) %collective-permute-start.47) | collective-permute-done | bytes 1048608 | tf_op jit(solution)/shard_map/ppermute | solution.py:206
  455.1 31.5 %collective-permute-start.63 = (bf16[256,2048]{1,0:T(8,128)(2,1)S(1)}, bf16[256,2048]{1,0:T(8,128)(2,1)S(1)}, u32[]{:S(2)}, u32[]{:S(2)}) collective-permute-start(bf16[256,2048]{1,0:T(8,128)(2,1)S(1)} %fusion.50), channel_id=1, source_target_pairs={{0,4},{1,5},{2,6},{3,7},{4,0},{5,1},{6,2},{7,3},{8,12},{9,13},{10,... | collective-permute-start | bytes 3145736 | tf_op jit(solution)/shard_map/ppermute | solution.py:206
  512.6 20.6 %multiply_convert_fusion.1 = bf16[1024,2048]{1,0:T(8,128)(2,1)} fusion(bf16[2048,2048]{1,0:T(8,128)(2,1)} %constant_dynamic-update-slice_fusion.24, f32[1024,2048]{1,0:T(8,128)} %fusion.30, bf16[256,2048]{1,0:T(8,128)(2,1)} %collective-permute-done.64, bf16[256,2048]{1,0:T(8,128)(2,1)} %copy-done.89, bf16[256,2048]{1,0:T(8,128)(2,1)} %copy-done.88, ...), kind=kOutput, calls=%fused_computation.5 | convolution fusion | flops 8648654848 | bytes 25165824 | tf_op jit(solution)/shard_map/dot_general | solution.py:27
  546.3 14.6 %fusion.28 = f32[1024,2048]{1,0:T(8,128)} fusion(bf16[2048,2048]{1,0:T(8,128)(2,1)} %constant_dynamic-update-slice_fusion.16, bf16[256,2048]{1,0:T(8,128)(2,1)} %collective-permute-done.57, bf16[256,2048]{1,0:T(8,128)(2,1)} %collective-permute-done.56, bf16[256,2048]{1,0:T(8,128)(2,1)} %collective-permute-done.55, bf16[256,2048]{1,0:T(8,128)(2,1)} %get-tuple-element.91), kind=kOutput, calls=%fused_computation.144 | convolution fusion | flops 8606711808 | bytes 20971520 | tf_op jit(solution)/shard_map/dot_general | solution.py:19
  575.1 23.7 %collective-permute-start.73 = (bf16[256,2048]{1,0:T(8,128)(2,1)S(1)}, bf16[256,2048]{1,0:T(8,128)(2,1)}, u32[]{:S(2)}, u32[]{:S(2)}) collective-permute-start(bf16[256,2048]{1,0:T(8,128)(2,1)S(1)} %copy-done.33), channel_id=1, source_target_pairs={{0,2},{1,3},{2,6},{3,7},{4,0},{5,1},{6,4},{7,5},{8,10},{9,11},{10,... | collective-permute-start | bytes 3145736 | tf_op jit(solution)/shard_map/ppermute | solution.py:220
  637.3 19.0 %collective-permute-done.59 = bf16[256,2048]{1,0:T(8,128)(2,1)S(1)} collective-permute-done((bf16[256,2048]{1,0:T(8,128)(2,1)S(1)}, bf16[256,2048]{1,0:T(8,128)(2,1)S(1)}, u32[]{:S(2)}, u32[]{:S(2)}) %collective-permute-start.59) | collective-permute-done | bytes 1048608 | tf_op jit(solution)/shard_map/ppermute | solution.py:206
  663.3 24.0 %collective-permute-done.74 = bf16[256,2048]{1,0:T(8,128)(2,1)S(1)} collective-permute-done((bf16[256,2048]{1,0:T(8,128)(2,1)S(1)}, bf16[256,2048]{1,0:T(8,128)(2,1)S(1)}, u32[]{:S(2)}, u32[]{:S(2)}) %collective-permute-start.74) | collective-permute-done | bytes 1048608 | tf_op jit(solution)/shard_map/ppermute | solution.py:206
  687.8 20.7 %collective-permute-done.67 = bf16[256,2048]{1,0:T(8,128)(2,1)} collective-permute-done((bf16[256,2048]{1,0:T(8,128)(2,1)S(1)}, bf16[256,2048]{1,0:T(8,128)(2,1)}, u32[]{:S(2)}, u32[]{:S(2)}) %collective-permute-start.67) | collective-permute-done | bytes 1048608 | tf_op jit(solution)/shard_map/ppermute | solution.py:206
  709.5 20.1 %multiply_convert_fusion = bf16[1024,2048]{1,0:T(8,128)(2,1)} fusion(bf16[2048,2048]{1,0:T(8,128)(2,1)} %constant_dynamic-update-slice_fusion.24, f32[1024,2048]{1,0:T(8,128)} %fusion.28, bf16[256,2048]{1,0:T(8,128)(2,1)} %collective-permute-done.76, bf16[256,2048]{1,0:T(8,128)(2,1)} %copy-done.94, bf16[256,2048]{1,0:T(8,128)(2,1)} %copy-done.92, ...), kind=kOutput, calls=%fused_computation.3 | convolution fusion | flops 8648654848 | bytes 25165824 | tf_op jit(solution)/shard_map/dot_general | solution.py:27
  729.6 14.2 %convolution_convert_fusion.4 = bf16[1024,2048]{1,0:T(8,128)(2,1)} fusion(bf16[1024,2048]{1,0:T(8,128)(2,1)} %multiply_convert_fusion, bf16[2048,2048]{1,0:T(8,128)(2,1)} %constant_dynamic-update-slice_fusion.16), kind=kOutput, calls=%fused_computation.34 | convolution fusion | flops 8592031744 | bytes 16777216 | tf_op jit(solution)/shard_map/dot_general | solution.py:27
  749.0 23.0 %attention_backward.2 = bf16[1024,1536]{1,0:T(8,128)(2,1)} custom-call(bf16[1024,1536]{1,0:T(8,128)(2,1)} %convolution_convert_fusion.3.qkv_ref, bf16[1024,512]{1,0:T(8,128)(2,1)} %convolution_convert_fusion.11.grad_ref, s32[1024,1]{1,0:T(8,128)} %copy.24.seg_col_ref, s32[1,1024]{1,0:T(1,128)} %bitcast.143), custom_call_target="tpu_custom_call" | custom-call | flops 5368709120 | bytes 7340032 | tf_op jit(solution)/shard_map/attention_backward/pallas_call | solution.py:103
  774.5 15.9 %fusion.26 = f32[2048,2048]{1,0:T(8,128)} fusion(bf16[256,2048]{1,0:T(8,128)(2,1)} %collective-permute-done.76, bf16[256,2048]{1,0:T(8,128)(2,1)S(1)} %copy-done.95, bf16[256,2048]{1,0:T(8,128)(2,1)S(1)} %copy-done.93, bf16[256,2048]{1,0:T(8,128)(2,1)S(1)} %copy-done.35, f32[1024,2048]{1,0:T(8,128)} %fusion.28), kind=kOutput, calls=%fused_computation.142 | convolution fusion | flops 8625586176 | bytes 29360128 | tf_op jit(solution)/shard_map/dot_general | solution.py:23
  790.4 20.6 %add_convert_fusion = bf16[2048,2048]{1,0:T(8,128)(2,1)} fusion(f32[2048,2048]{1,0:T(8,128)} %fusion.26, bf16[256,2048]{1,0:T(8,128)(2,1)} %collective-permute-done.64, bf16[256,2048]{1,0:T(8,128)(2,1)} %copy-done.89, bf16[256,2048]{1,0:T(8,128)(2,1)} %copy-done.88, bf16[256,2048]{1,0:T(8,128)(2,1)S(1)} %copy-done.32, f32[1024,2048]{1,0:T(8,128)} %fusion.30), kind=kOutput, calls=%fused_computation | convolution fusion | flops 8633974784 | bytes 37748736 | tf_op jit(solution)/shard_map/dot_general | solution.py:23
  817.1 14.6 %fusion.27 = f32[2048,2048]{1,0:T(8,128)} fusion(bf16[1024,2048]{1,0:T(8,128)(2,1)S(1)} %copy-done.100, bf16[256,2048]{1,0:T(8,128)(2,1)} %collective-permute-done.57, bf16[256,2048]{1,0:T(8,128)(2,1)} %collective-permute-done.56, bf16[256,2048]{1,0:T(8,128)(2,1)} %collective-permute-done.55, bf16[256,2048]{1,0:T(8,128)(2,1)} %get-tuple-element.91), kind=kOutput, calls=%fused_computation.143 | convolution fusion | flops 8606711808 | bytes 25165824 | tf_op jit(solution)/shard_map/dot_general | solution.py:23
  831.7 16.4 %add_convert_fusion.1 = bf16[2048,2048]{1,0:T(8,128)(2,1)} fusion(f32[2048,2048]{1,0:T(8,128)} %fusion.27, bf16[1024,2048]{1,0:T(8,128)(2,1)} %multiply_convert_fusion.1, bf16[256,2048]{1,0:T(8,128)(2,1)} %copy-done.87, bf16[256,2048]{1,0:T(8,128)(2,1)S(1)} %copy-done.86, bf16[256,2048]{1,0:T(8,128)(2,1)} %collective-permute-done.27, ...), kind=kOutput, calls=%fused_computation.1 | convolution fusion | flops 8615100416 | bytes 33554432 | tf_op jit(solution)/shard_map/dot_general | solution.py:23
  885.8 15.5 %collective-permute-done.109 = bf16[2048,256]{1,0:T(8,128)(2,1)S(1)} collective-permute-done((bf16[2048,256]{1,0:T(8,128)(2,1)}, bf16[2048,256]{1,0:T(8,128)(2,1)S(1)}, u32[]{:S(2)}, u32[]{:S(2)}) %collective-permute-start.109) | collective-permute-done | bytes 1048608 | tf_op jit(solution)/shard_map/ppermute | solution.py:206
  927.2 16.4 %collective-permute-done.106 = bf16[256,2048]{1,0:T(8,128)(2,1)S(1)} collective-permute-done((bf16[256,2048]{1,0:T(8,128)(2,1)S(1)}, bf16[256,2048]{1,0:T(8,128)(2,1)S(1)}, u32[]{:S(2)}, u32[]{:S(2)}) %collective-permute-start.106) | collective-permute-done | bytes 1048608 | tf_op jit(solution)/shard_map/ppermute | solution.py:206
  943.9 22.2 %collective-permute-done.103 = bf16[256,2048]{1,0:T(8,128)(2,1)S(1)} collective-permute-done((bf16[256,2048]{1,0:T(8,128)(2,1)S(1)}, bf16[256,2048]{1,0:T(8,128)(2,1)S(1)}, u32[]{:S(2)}, u32[]{:S(2)}) %collective-permute-start.103) | collective-permute-done | bytes 1048608 | tf_op jit(solution)/shard_map/ppermute | solution.py:206
  1037.0 23.4 %attention_backward.3 = bf16[1024,1536]{1,0:T(8,128)(2,1)} custom-call(bf16[1024,1536]{1,0:T(8,128)(2,1)} %convolution_convert_fusion.2.qkv_ref, bf16[1024,512]{1,0:T(8,128)(2,1)} %convolution_convert_fusion.10.grad_ref, s32[1024,1]{1,0:T(8,128)} %copy.25.seg_col_ref, s32[1,1024]{1,0:T(1,128)} %bitcast.140), custom_call_target="tpu_custom_call" | custom-call | flops 5368709120 | bytes 7340032 | tf_op jit(solution)/shard_map/attention_backward/pallas_call | solution.py:103
  1126.8 17.4 %collective-permute-done.95 = bf16[512,256]{1,0:T(8,128)(2,1)S(1)} collective-permute-done((bf16[512,256]{1,0:T(8,128)(2,1)S(1)}, bf16[512,256]{1,0:T(8,128)(2,1)S(1)}, u32[]{:S(2)}, u32[]{:S(2)}) %collective-permute-start.95) | collective-permute-done | bytes 262176 | tf_op jit(solution)/shard_map/ppermute | solution.py:206
  1167.4 25.6 %collective-permute-done.108 = bf16[256,2048]{1,0:T(8,128)(2,1)S(1)} collective-permute-done((bf16[256,2048]{1,0:T(8,128)(2,1)S(1)}, bf16[256,2048]{1,0:T(8,128)(2,1)S(1)}, u32[]{:S(2)}, u32[]{:S(2)}) %collective-permute-start.108) | collective-permute-done | bytes 1048608 | tf_op jit(solution)/shard_map/ppermute | solution.py:223
  1209.6 24.3 %collective-permute-done.83 = bf16[256,2048]{1,0:T(8,128)(2,1)S(1)} collective-permute-done((bf16[256,2048]{1,0:T(8,128)(2,1)S(1)}, bf16[256,2048]{1,0:T(8,128)(2,1)S(1)}, u32[]{:S(2)}, u32[]{:S(2)}) %collective-permute-start.83) | collective-permute-done | bytes 1048608 | tf_op jit(solution)/shard_map/ppermute | solution.py:206
  1250.0 31.6 %collective-permute-start.84 = (bf16[256,2048]{1,0:T(8,128)(2,1)}, bf16[256,2048]{1,0:T(8,128)(2,1)}, u32[]{:S(2)}, u32[]{:S(2)}) collective-permute-start(bf16[256,2048]{1,0:T(8,128)(2,1)} %reorder.15), channel_id=1, source_target_pairs={{2,0},{3,1},{6,2},{7,3},{0,4},{1,5},{4,6},{5,7},{10,8},{11,9},{14,... | collective-permute-start | bytes 3145736 | tf_op jit(solution)/shard_map/ppermute | solution.py:223
  1283.4 18.1 %collective-permute-done.92 = bf16[256,1536]{1,0:T(8,128)(2,1)} collective-permute-done((bf16[256,1536]{1,0:T(8,128)(2,1)}, bf16[256,1536]{1,0:T(8,128)(2,1)}, u32[]{:S(2)}, u32[]{:S(2)}) %collective-permute-start.92) | collective-permute-done | bytes 786464 | tf_op jit(solution)/shard_map/ppermute | solution.py:223
  1312.8 22.5 %collective-permute-done.84 = bf16[256,2048]{1,0:T(8,128)(2,1)} collective-permute-done((bf16[256,2048]{1,0:T(8,128)(2,1)}, bf16[256,2048]{1,0:T(8,128)(2,1)}, u32[]{:S(2)}, u32[]{:S(2)}) %collective-permute-start.84) | collective-permute-done | bytes 1048608 | tf_op jit(solution)/shard_map/ppermute | solution.py:223
  (621 shorter events, 700.7 us)
Async XLA Ops:
  10.6 67.0 %collective-permute-start.5 = (bf16[256,1536]{0,1:T(8,128)(2,1)}, bf16[256,1536]{0,1:T(8,128)(2,1)}, u32[]{:S(2)}, u32[]{:S(2)}) collective-permute-start(bf16[256,1536]{0,1:T(8,128)(2,1)} %bitcast.5), channel_id=1, source_target_pairs={{0,2},{1,3},{2,6},{3,7},{4,0},{5,1},{6,4},{7,5},{8,10},{9,11},{10,... | collective-permute-start | bytes 2359304 | tf_op jit(solution)/shard_map/ppermute | solution.py:220
  49.3 55.6 %collective-permute-start.1 = (bf16[256,2048]{1,0:T(8,128)(2,1)}, bf16[256,2048]{1,0:T(8,128)(2,1)S(1)}, u32[]{:S(2)}, u32[]{:S(2)}) collective-permute-start(bf16[256,2048]{1,0:T(8,128)(2,1)} %reorder.8), channel_id=1, source_target_pairs={{0,1},{1,0},{2,3},{3,2},{4,5},{5,4},{6,7},{7,6},{8,9},{9,8},{10,11... | collective-permute-start | bytes 3145736 | tf_op jit(solution)/shard_map/ppermute | solution.py:206
  93.4 52.8 %collective-permute-start.2 = (bf16[256,2048]{1,0:T(8,128)(2,1)S(1)}, bf16[256,2048]{1,0:T(8,128)(2,1)S(1)}, u32[]{:S(2)}, u32[]{:S(2)}) collective-permute-start(bf16[256,2048]{1,0:T(8,128)(2,1)S(1)} %copy-done.18), channel_id=1, source_target_pairs={{0,4},{1,5},{2,6},{3,7},{4,0},{5,1},{6,2},{7,3},{8,12},{9,13},{10,... | collective-permute-start | bytes 3145736 | tf_op jit(solution)/shard_map/ppermute | solution.py:206
  110.3 68.7 %collective-permute-start.31 = (bf16[256,2048]{1,0:T(8,128)(2,1)}, bf16[256,2048]{1,0:T(8,128)(2,1)}, u32[]{:S(2)}, u32[]{:S(2)}) collective-permute-start(bf16[256,2048]{1,0:T(8,128)(2,1)} %param.17), channel_id=1, source_target_pairs={{0,2},{1,3},{2,6},{3,7},{4,0},{5,1},{6,4},{7,5},{8,10},{9,11},{10,... | collective-permute-start | bytes 3145736 | tf_op jit(solution)/shard_map/ppermute | solution.py:220
  127.1 78.6 %collective-permute-start.30 = (bf16[256,2048]{1,0:T(8,128)(2,1)}, bf16[256,2048]{1,0:T(8,128)(2,1)}, u32[]{:S(2)}, u32[]{:S(2)}) collective-permute-start(bf16[256,2048]{1,0:T(8,128)(2,1)} %param.17), channel_id=1, source_target_pairs={{0,0},{1,1},{2,4},{3,5},{4,2},{5,3},{6,6},{7,7},{8,8},{9,9},{10,12... | collective-permute-start | bytes 3145736 | tf_op jit(solution)/shard_map/ppermute | solution.py:220
  136.7 63.8 %collective-permute-start.38 = (bf16[2048,256]{1,0:T(8,128)(2,1)}, bf16[2048,256]{1,0:T(8,128)(2,1)}, u32[]{:S(2)}, u32[]{:S(2)}) collective-permute-start(bf16[2048,256]{1,0:T(8,128)(2,1)} %param.18), channel_id=1, source_target_pairs={{0,0},{1,1},{2,4},{3,5},{4,2},{5,3},{6,6},{7,7},{8,8},{9,9},{10,12... | collective-permute-start | bytes 3145736 | tf_op jit(solution)/shard_map/ppermute | solution.py:220
  179.0 76.8 %collective-permute-start.21 = (bf16[512,2048]{1,0:T(8,128)(2,1)}, bf16[512,2048]{1,0:T(8,128)(2,1)}, u32[]{:S(2)}, u32[]{:S(2)}) collective-permute-start(bf16[512,2048]{1,0:T(8,128)(2,1)} %slice.407), channel_id=1, source_target_pairs={{0,4},{1,5},{2,6},{3,7},{4,0},{5,1},{6,2},{7,3},{8,12},{9,13},{10,... | collective-permute-start | bytes 6291464 | tf_op jit(solution)/shard_map/ppermute | solution.py:206
  210.1 76.4 %collective-permute-start.35 = (bf16[256,2048]{1,0:T(8,128)(2,1)}, bf16[256,2048]{1,0:T(8,128)(2,1)}, u32[]{:S(2)}, u32[]{:S(2)}) collective-permute-start(bf16[256,2048]{1,0:T(8,128)(2,1)} %collective-permute-done.31), channel_id=1, source_target_pairs={{0,16},{1,17},{2,18},{3,19},{4,20},{5,21},{6,22},{7,23},{8,24},{9,... | collective-permute-start | bytes 3145736 | tf_op jit(solution)/shard_map/ppermute | solution.py:206
  227.1 57.2 %collective-permute-start.34 = (bf16[256,2048]{1,0:T(8,128)(2,1)}, bf16[256,2048]{1,0:T(8,128)(2,1)S(1)}, u32[]{:S(2)}, u32[]{:S(2)}) collective-permute-start(bf16[256,2048]{1,0:T(8,128)(2,1)} %collective-permute-done.30), channel_id=1, source_target_pairs={{0,16},{1,17},{2,18},{3,19},{4,20},{5,21},{6,22},{7,23},{8,24},{9,... | collective-permute-start | bytes 3145736 | tf_op jit(solution)/shard_map/ppermute | solution.py:206
  247.2 56.4 %collective-permute-start.43 = (bf16[2048,256]{1,0:T(8,128)(2,1)}, bf16[2048,256]{1,0:T(8,128)(2,1)S(1)}, u32[]{:S(2)}, u32[]{:S(2)}) collective-permute-start(bf16[2048,256]{1,0:T(8,128)(2,1)} %collective-permute-done.39), channel_id=1, source_target_pairs={{0,16},{1,17},{2,18},{3,19},{4,20},{5,21},{6,22},{7,23},{8,24},{9,... | collective-permute-start | bytes 3145736 | tf_op jit(solution)/shard_map/ppermute | solution.py:206
  286.5 47.9 %collective-permute-start.51 = (bf16[256,2048]{1,0:T(8,128)(2,1)S(1)}, bf16[256,2048]{1,0:T(8,128)(2,1)S(1)}, u32[]{:S(2)}, u32[]{:S(2)}) collective-permute-start(bf16[256,2048]{1,0:T(8,128)(2,1)S(1)} %copy-done.20), channel_id=1, source_target_pairs={{0,4},{1,5},{2,6},{3,7},{4,0},{5,1},{6,2},{7,3},{8,12},{9,13},{10,... | collective-permute-start | bytes 3145736 | tf_op jit(solution)/shard_map/ppermute | solution.py:206
  300.5 70.6 %collective-permute-start.37 = (bf16[256,2048]{1,0:T(8,128)(2,1)}, bf16[256,2048]{1,0:T(8,128)(2,1)}, u32[]{:S(2)}, u32[]{:S(2)}) collective-permute-start(bf16[256,2048]{1,0:T(8,128)(2,1)} %collective-permute-done.35), channel_id=1, source_target_pairs={{0,8},{1,9},{2,10},{3,11},{4,12},{5,13},{6,14},{7,15},{8,0},{9,1},... | collective-permute-start | bytes 3145736 | tf_op jit(solution)/shard_map/ppermute | solution.py:206
  303.6 65.1 %collective-permute-start.36 = (bf16[256,2048]{1,0:T(8,128)(2,1)}, bf16[256,2048]{1,0:T(8,128)(2,1)}, u32[]{:S(2)}, u32[]{:S(2)}) collective-permute-start(bf16[256,2048]{1,0:T(8,128)(2,1)} %collective-permute-done.32), channel_id=1, source_target_pairs={{0,16},{1,17},{2,18},{3,19},{4,20},{5,21},{6,22},{7,23},{8,24},{9,... | collective-permute-start | bytes 3145736 | tf_op jit(solution)/shard_map/ppermute | solution.py:206
  307.9 57.9 %collective-permute-start.45 = (bf16[2048,256]{1,0:T(8,128)(2,1)S(1)}, bf16[2048,256]{1,0:T(8,128)(2,1)}, u32[]{:S(2)}, u32[]{:S(2)}) collective-permute-start(bf16[2048,256]{1,0:T(8,128)(2,1)S(1)} %collective-permute-done.43), channel_id=1, source_target_pairs={{0,8},{1,9},{2,10},{3,11},{4,12},{5,13},{6,14},{7,15},{8,0},{9,1},... | collective-permute-start | bytes 3145736 | tf_op jit(solution)/shard_map/ppermute | solution.py:206
  455.1 56.5 %collective-permute-start.63 = (bf16[256,2048]{1,0:T(8,128)(2,1)S(1)}, bf16[256,2048]{1,0:T(8,128)(2,1)S(1)}, u32[]{:S(2)}, u32[]{:S(2)}) collective-permute-start(bf16[256,2048]{1,0:T(8,128)(2,1)S(1)} %fusion.50), channel_id=1, source_target_pairs={{0,4},{1,5},{2,6},{3,7},{4,0},{5,1},{6,2},{7,3},{8,12},{9,13},{10,... | collective-permute-start | bytes 3145736 | tf_op jit(solution)/shard_map/ppermute | solution.py:206
  546.2 52.5 %collective-permute-start.65 = (bf16[512,2048]{1,0:T(8,128)(2,1)S(1)}, bf16[512,2048]{1,0:T(8,128)(2,1)S(1)}, u32[]{:S(2)}, u32[]{:S(2)}) collective-permute-start(bf16[512,2048]{1,0:T(8,128)(2,1)S(1)} %slice.431), channel_id=1, source_target_pairs={{0,4},{1,5},{2,6},{3,7},{4,0},{5,1},{6,2},{7,3},{8,12},{9,13},{10,... | collective-permute-start | bytes 6291464 | tf_op jit(solution)/shard_map/ppermute | solution.py:206
  687.3 56.5 %collective-permute-start.68 = (bf16[256,2048]{1,0:T(8,128)(2,1)S(1)}, bf16[256,2048]{1,0:T(8,128)(2,1)}, u32[]{:S(2)}, u32[]{:S(2)}) collective-permute-start(bf16[256,2048]{1,0:T(8,128)(2,1)S(1)} %get-tuple-element.36), channel_id=1, source_target_pairs={{0,4},{1,5},{2,6},{3,7},{4,0},{5,1},{6,2},{7,3},{8,12},{9,13},{10,... | collective-permute-start | bytes 3145736 | tf_op jit(solution)/shard_map/ppermute | solution.py:206
  773.9 107.4 %collective-permute-start.77 = (bf16[512,2048]{1,0:T(8,128)(2,1)S(1)}, bf16[512,2048]{1,0:T(8,128)(2,1)}, u32[]{:S(2)}, u32[]{:S(2)}) collective-permute-start(bf16[512,2048]{1,0:T(8,128)(2,1)S(1)} %slice.439), channel_id=1, source_target_pairs={{0,4},{1,5},{2,6},{3,7},{4,0},{5,1},{6,2},{7,3},{8,12},{9,13},{10,... | collective-permute-start | bytes 6291464 | tf_op jit(solution)/shard_map/ppermute | solution.py:206
  815.4 57.0 %collective-permute-start.110 = (bf16[2048,256]{1,0:T(8,128)(2,1)}, bf16[2048,256]{1,0:T(8,128)(2,1)S(1)}, u32[]{:S(2)}, u32[]{:S(2)}) collective-permute-start(bf16[2048,256]{1,0:T(8,128)(2,1)} %get-tuple-element.55), channel_id=1, source_target_pairs={{0,16},{1,17},{2,18},{3,19},{4,20},{5,21},{6,22},{7,23},{8,24},{9,... | collective-permute-start | bytes 3145736 | tf_op jit(solution)/shard_map/ppermute | solution.py:206
  903.3 62.8 %collective-permute-start.103 = (bf16[256,2048]{1,0:T(8,128)(2,1)S(1)}, bf16[256,2048]{1,0:T(8,128)(2,1)S(1)}, u32[]{:S(2)}, u32[]{:S(2)}) collective-permute-start(bf16[256,2048]{1,0:T(8,128)(2,1)S(1)} %add_convert_fusion.16), channel_id=1, source_target_pairs={{0,8},{1,9},{2,10},{3,11},{4,12},{5,13},{6,14},{7,15},{8,0},{9,1},... | collective-permute-start | bytes 3145736 | tf_op jit(solution)/shard_map/ppermute | solution.py:206
  905.9 87.4 %collective-permute-start.113 = (bf16[2048,256]{1,0:T(8,128)(2,1)}, bf16[2048,256]{1,0:T(8,128)(2,1)}, u32[]{:S(2)}, u32[]{:S(2)}) collective-permute-start(bf16[2048,256]{1,0:T(8,128)(2,1)} %get-tuple-element.54), channel_id=1, source_target_pairs={{0,8},{1,9},{2,10},{3,11},{4,12},{5,13},{6,14},{7,15},{8,0},{9,1},... | collective-permute-start | bytes 3145736 | tf_op jit(solution)/shard_map/ppermute | solution.py:206
  921.2 48.8 %collective-permute-start.78 = (bf16[256,2048]{1,0:T(8,128)(2,1)S(1)}, bf16[256,2048]{1,0:T(8,128)(2,1)S(1)}, u32[]{:S(2)}, u32[]{:S(2)}) collective-permute-start(bf16[256,2048]{1,0:T(8,128)(2,1)S(1)} %slice.564), channel_id=1, source_target_pairs={{0,1},{1,0},{2,3},{3,2},{4,5},{5,4},{6,7},{7,6},{8,9},{9,8},{10,11... | collective-permute-start | bytes 3145736 | tf_op jit(solution)/shard_map/ppermute | solution.py:206
  925.2 86.1 %collective-permute-start.105 = (bf16[256,2048]{1,0:T(8,128)(2,1)}, bf16[256,2048]{1,0:T(8,128)(2,1)}, u32[]{:S(2)}, u32[]{:S(2)}) collective-permute-start(bf16[256,2048]{1,0:T(8,128)(2,1)} %get-tuple-element.60), channel_id=1, source_target_pairs={{0,8},{1,9},{2,10},{3,11},{4,12},{5,13},{6,14},{7,15},{8,0},{9,1},... | collective-permute-start | bytes 3145736 | tf_op jit(solution)/shard_map/ppermute | solution.py:206
  993.3 121.4 %collective-permute-start.112 = (bf16[2048,256]{1,0:T(8,128)(2,1)}, bf16[2048,256]{1,0:T(8,128)(2,1)}, u32[]{:S(2)}, u32[]{:S(2)}) collective-permute-start(bf16[2048,256]{1,0:T(8,128)(2,1)} %get-tuple-element.50), channel_id=1, source_target_pairs={{0,0},{1,1},{4,2},{5,3},{2,4},{3,5},{6,6},{7,7},{8,8},{9,9},{12,10... | collective-permute-start | bytes 3145736 | tf_op jit(solution)/shard_map/ppermute | solution.py:223
  1026.1 90.4 %collective-permute-start.116 = (bf16[2048,256]{1,0:T(8,128)(2,1)}, bf16[2048,256]{1,0:T(8,128)(2,1)}, u32[]{:S(2)}, u32[]{:S(2)}) collective-permute-start(bf16[2048,256]{1,0:T(8,128)(2,1)} %add_convert_fusion.6), channel_id=1, source_target_pairs={{2,0},{3,1},{6,2},{7,3},{0,4},{1,5},{4,6},{5,7},{10,8},{11,9},{14,... | collective-permute-start | bytes 3145736 | tf_op jit(solution)/shard_map/ppermute | solution.py:223
  1104.6 59.8 %collective-permute-start.82 = (bf16[512,2048]{1,0:T(8,128)(2,1)S(1)}, bf16[512,2048]{1,0:T(8,128)(2,1)S(1)}, u32[]{:S(2)}, u32[]{:S(2)}) collective-permute-start(bf16[512,2048]{1,0:T(8,128)(2,1)S(1)} %slice.443), channel_id=1, source_target_pairs={{0,4},{1,5},{2,6},{3,7},{4,0},{5,1},{6,2},{7,3},{8,12},{9,13},{10,... | collective-permute-start | bytes 6291464 | tf_op jit(solution)/shard_map/ppermute | solution.py:206
  1145.2 47.9 %collective-permute-start.108 = (bf16[256,2048]{1,0:T(8,128)(2,1)S(1)}, bf16[256,2048]{1,0:T(8,128)(2,1)S(1)}, u32[]{:S(2)}, u32[]{:S(2)}) collective-permute-start(bf16[256,2048]{1,0:T(8,128)(2,1)S(1)} %copy-done.39), channel_id=1, source_target_pairs={{2,0},{3,1},{6,2},{7,3},{0,4},{1,5},{4,6},{5,7},{10,8},{11,9},{14,... | collective-permute-start | bytes 3145736 | tf_op jit(solution)/shard_map/ppermute | solution.py:223
  1194.8 112.0 %collective-permute-start.48 = (bf16[256,2048]{1,0:T(8,128)(2,1)}, bf16[256,2048]{1,0:T(8,128)(2,1)}, u32[]{:S(2)}, u32[]{:S(2)}) collective-permute-start(bf16[256,2048]{1,0:T(8,128)(2,1)} %reorder.9), channel_id=1, source_target_pairs={{0,0},{1,1},{4,2},{5,3},{2,4},{3,5},{6,6},{7,7},{8,8},{9,9},{12,10... | collective-permute-start | bytes 3145736 | tf_op jit(solution)/shard_map/ppermute | solution.py:223
  1233.9 67.7 %collective-permute-start.92 = (bf16[256,1536]{1,0:T(8,128)(2,1)}, bf16[256,1536]{1,0:T(8,128)(2,1)}, u32[]{:S(2)}, u32[]{:S(2)}) collective-permute-start(bf16[256,1536]{1,0:T(8,128)(2,1)} %add_convert_fusion.20), channel_id=1, source_target_pairs={{2,0},{3,1},{6,2},{7,3},{0,4},{1,5},{4,6},{5,7},{10,8},{11,9},{14,... | collective-permute-start | bytes 2359304 | tf_op jit(solution)/shard_map/ppermute | solution.py:223
  1240.6 72.2 %collective-permute-start.60 = (bf16[256,2048]{1,0:T(8,128)(2,1)}, bf16[256,2048]{1,0:T(8,128)(2,1)}, u32[]{:S(2)}, u32[]{:S(2)}) collective-permute-start(bf16[256,2048]{1,0:T(8,128)(2,1)} %reorder.11), channel_id=1, source_target_pairs={{2,0},{3,1},{6,2},{7,3},{0,4},{1,5},{4,6},{5,7},{10,8},{11,9},{14,... | collective-permute-start | bytes 3145736 | tf_op jit(solution)/shard_map/ppermute | solution.py:223
  1240.6 72.2 %collective-permute-start.72 = (bf16[256,2048]{1,0:T(8,128)(2,1)}, bf16[256,2048]{1,0:T(8,128)(2,1)}, u32[]{:S(2)}, u32[]{:S(2)}) collective-permute-start(bf16[256,2048]{1,0:T(8,128)(2,1)} %reorder.13), channel_id=1, source_target_pairs={{0,0},{1,1},{4,2},{5,3},{2,4},{3,5},{6,6},{7,7},{8,8},{9,9},{12,10... | collective-permute-start | bytes 3145736 | tf_op jit(solution)/shard_map/ppermute | solution.py:223
  1250.0 85.2 %collective-permute-start.84 = (bf16[256,2048]{1,0:T(8,128)(2,1)}, bf16[256,2048]{1,0:T(8,128)(2,1)}, u32[]{:S(2)}, u32[]{:S(2)}) collective-permute-start(bf16[256,2048]{1,0:T(8,128)(2,1)} %reorder.15), channel_id=1, source_target_pairs={{2,0},{3,1},{6,2},{7,3},{0,4},{1,5},{4,6},{5,7},{10,8},{11,9},{14,... | collective-permute-start | bytes 3145736 | tf_op jit(solution)/shard_map/ppermute | solution.py:223
  (196 other events, 6240.8 us)

commit v2 on v1

--- a/solution.py
+++ b/solution.py
@@ -125,22 +125,23 @@
     out_ref[...] = in_ref[...]
 
 
-def reorder(array, mask, count):
+def reorder(array, table):
     rows, width = array.shape
+    count = table.shape[0]
     return pl.pallas_call(
         reorder_kernel,
         out_shape=jax.ShapeDtypeStruct(array.shape, array.dtype),
         grid_spec=pltpu.PrefetchScalarGridSpec(
             num_scalar_prefetch=1,
             grid=(count,),
-            in_specs=[pl.BlockSpec((rows, width // count), lambda i, m: (0, i ^ m[0]))],
+            in_specs=[pl.BlockSpec((rows, width // count), lambda i, m: (0, m[i]))],
             out_specs=pl.BlockSpec((rows, width // count), lambda i, m: (0, i)),
         ),
         cost_estimate=pl.CostEstimate(
             flops=0, transcendentals=0, bytes_accessed=4 * rows * width
         ),
         name="reorder",
-    )(mask, array)
+    )(table, array)
 
 
 def norm_forward(values, gain, shift):
@@ -198,85 +199,105 @@
     dp_index, tensor_index = lax.axis_index("dp"), lax.axis_index("tensor")
     p, c = dp_index // 2, dp_index % 2
     h, t = tensor_index // tp, tensor_index % tp
-    basis = p * 2 + h
-    basis_ref = basis.astype(jnp.int32).reshape(1)
+    basis = (p * 2 + h).astype(jnp.int32)
+
+    def reversed_bits(k):
+        return sum(((k // bit) % 2) * (chips // 2 // bit) for bit in p_bits)
+
+    def place(block):
+        k, j = block // 2, block % 2
+        return j * chips + jnp.where(j == 0, k, reversed_bits(k))
+
+    numbers = jnp.arange(blocks, dtype=jnp.int32)
+    rank = numbers % chips
+    to_table = (
+        jnp.where(numbers < chips, rank * 2, reversed_bits(rank) * 2 + 1).astype(jnp.int32) ^ basis
+    )
+    from_table = place(numbers ^ basis).astype(jnp.int32)
     home = c * tp + t
 
     def swap(array, mask):
         return lax.ppermute(array, AXES, [(i, i ^ mask) for i in range(total)])
 
-    def turned(j, back):
-        pairs = []
-        for i in range(total):
-            it = i % tp
-            ih = i // tp % halves
-            ic = i // tensor_size % 2
-            ip = i // tensor_size // 2
-            to = ((ip * 2 + ih) * halves + (j ^ ic)) * tp + it
-            pairs.append((to, i) if back else (i, to))
-        return pairs
-
-    def turn(array, j):
-        return lax.ppermute(array, AXES, turned(j, False))
-
-    def turn_back(array, j):
-        return lax.ppermute(array, AXES, turned(j, True))
-
-    def fetch(shard, axis):
-        found = {}
-        for j in range(2):
-            own = {0: turn(shard, j)}
-            for bit in orders[j]:
-                own.update({k | bit: swap(v, bit * 2 * tensor_size) for k, v in own.items()})
-            found.update({k * 2 + j: v for k, v in own.items()})
-        return jnp.concatenate([found[b] for b in range(blocks)], axis=axis)
-
-    def reduce_grad(pieces):
-        sums = []
-        for j in range(2):
-            own = {k: pieces[k * 2 + j] for k in range(chips)}
-            for bit in orders[j][::-1]:
-                kept = {}
-                for k in own:
-                    if not k & bit:
-                        got = swap(own[k | bit], bit * 2 * tensor_size)
-                        kept[k] = (own[k].astype(F32) + got.astype(F32)).astype(BF16)
-                own = kept
-            sums.append(turn_back(own[0], j))
-        return sums[0].astype(F32) + sums[1].astype(F32)
-
-    def row_pieces(array):
-        size = array.shape[0] // blocks
-        return [array[b * size : (b + 1) * size] for b in range(blocks)]
-
-    def column_pieces(array):
-        size = array.shape[1] // blocks
-        return [array[:, b * size : (b + 1) * size] for b in range(blocks)]
-
-    def gather_rows(array):
+    same = c == h
+
+    def after(array, *others):
+        return lax.optimization_barrier((array, *others))[0]
+
+
+    def near(shard, other):
+        got = swap(jnp.where(same, other, shard), core_bit)
+        return [jnp.where(same, shard, got), jnp.where(same, got, other)]
+
+    def moved(parts, step):
+        got = [swap(v, order[step] * 2 * tensor_size) for v, order in zip(parts, orders)]
+        return list(lax.optimization_barrier(tuple(got)))
+
+    def joined(parts, got, axis):
+        return [jnp.concatenate([v, w], axis=axis) for v, w in zip(parts, got)]
+
+    def doubled(parts, axis, begin, end):
+        for step in range(begin, end):
+            parts = joined(parts, moved(parts, step), axis)
+        return parts
+
+    def tied(parts, *others):
+        return list(lax.optimization_barrier((*parts, *others)))[: len(parts)]
+
+    last = len(p_bits) - 1
+
+
+    def split_send(parts, step, axis):
+        halves_of = [jnp.split(v, 2, axis=axis) for v in parts]
+        got = [
+            swap(v[1], order[step] * 2 * tensor_size) for v, order in zip(halves_of, orders)
+        ]
+        return [v[0] for v in halves_of], list(lax.optimization_barrier(tuple(got)))
+
+    def added(kept, got):
+        return [(v.astype(F32) + w.astype(F32)).astype(BF16) for v, w in zip(kept, got)]
+
+    def collect(first, second):
+        got = swap(jnp.where(same, second, first), core_bit)
+        kept = jnp.where(same, first, got)
+        return kept, swap(jnp.where(same, got, second), half_bit)
+
+    def reduce_rest(parts, axis, step):
+        for s in range(step, -1, -1):
+            parts = added(*split_send(parts, s, axis))
+        kept, got = collect(*parts)
+        return kept, got
+
+    def total_of(kept, got):
+        return kept.astype(F32) + got.astype(F32)
+
+
+    def gather_far(array):
         parts = [array]
         for bit in t_bits:
             parts = parts + [swap(part, bit) for part in parts]
-        parts = parts + [swap(part, core_bit) for part in parts]
-        return jnp.concatenate(parts, axis=0)
-
-    def reduce_rows(array):
+        return parts
+
+    def gather_near(parts):
+        return jnp.concatenate(parts + [swap(part, core_bit) for part in parts], axis=0)
+
+    def gather_rows(array):
+        return gather_near(gather_far(array))
+
+    def reduce_near(array):
         array = array.astype(BF16)
         middle = array.shape[0] // 2
-        kept = array[:middle].astype(F32) + swap(array[middle:], core_bit).astype(F32)
-        for bit in t_bits[::-1]:
+        return array[:middle].astype(F32) + swap(array[middle:], core_bit).astype(F32)
+
+    def reduce_far(kept):
+        for bit in t_bits[:0:-1]:
             middle = kept.shape[0] // 2
             kept = kept[:middle] + swap(kept[middle:].astype(BF16), bit).astype(F32)
-        return kept
-
-    own_params = jnp.concatenate([norm_gains, norm_shifts], axis=0)
-    other_params = swap(own_params, core_bit)
-    pair = [jnp.where((h ^ j) == c, own_params, other_params) for j in range(2)]
-    found = {0: jnp.stack(pair, axis=1)}
-    for bit in p_bits:
-        found.update({k | bit: swap(v, bit * 2 * tensor_size) for k, v in found.items()})
-    params = jnp.stack([found[k] for k in range(chips)], axis=1).reshape(4, width).astype(F32)
-    gains, shifts = params[:2], params[2:]
+        middle = kept.shape[0] // 2
+        return kept[:middle], swap(kept[middle:].astype(BF16), t_bits[0])
+
+    def ready(pair, *others):
+        return pair[0] + after(pair[1], *others).astype(F32)
 
     own_segments = jnp.where(h == 0, segments[0, 0], segments[1, 0])
     other_segments = swap(own_segments, core_bit)
@@ -292,89 +313,154 @@
         row = row.reshape(-1)
         return row[:, None], row[None, :]
 
-    def to_home(array, j):
-        piece = jnp.where((j ^ c) == 0, array[0], array[1])
-        return reorder(turn(piece, j), basis_ref, blocks)
-
-    def from_home(pieces):
-        back = [turn_back(reorder(piece, basis_ref, blocks), j) for j, piece in enumerate(pieces)]
-        return jnp.stack(
-            [jnp.where(c == 0, back[0], back[1]), jnp.where(c == 0, back[1], back[0])]
-        )
+    def parted(array):
+        return jnp.where(h == 0, array[0], array[1]), jnp.where(h == 0, array[1], array[0])
+
+    def to_home(own, other):
+        got = swap(jnp.where(same, other, own), core_bit)
+        pair = [jnp.where(same, own, got), jnp.where(same, got, other)]
+        both = reorder(jnp.concatenate(pair, axis=0), to_table)
+        return [both[:block_tokens], both[block_tokens:]]
+
+    def sent_home(pieces):
+        both = reorder(jnp.concatenate(pieces, axis=0), from_table)
+        return collect(both[:block_tokens], both[block_tokens:])
+
+    def home_pair(kept, got):
+        return jnp.stack([jnp.where(h == 0, kept, got), jnp.where(h == 0, got, kept)])
 
     streams = range(2)
-    homes = [to_home(tokens, j) for j in streams]
-    rows = [gather_rows(x) for x in homes]
-
-    shard = jnp.stack(
+    extra = 16
+    qkv_shard = jnp.stack(
         [w.reshape(-1, heads, DH) for w in (query_weight, key_weight, value_weight)], axis=2
     ).reshape(-1, 3 * local_width)
-    full_qkv = fetch(shard, 0)
-    full_output = fetch(output_weight, 1)
-    full_expand = fetch(expand_weight, 0)
-    full_contract = fetch(contract_weight, 1)
+    params = jnp.concatenate([norm_gains, norm_shifts], axis=0)
+    params = jnp.pad(params, ((0, extra - params.shape[0]), (0, 0)))
+    output_shard = jnp.concatenate([output_weight, params], axis=0)
+
+    qkv_other = swap(qkv_shard, half_bit)
+    token_own, token_send = parted(tokens)
+    token_other = swap(after(token_send, qkv_other), half_bit)
+    qkv_parts = doubled(near(qkv_shard, qkv_other), 0, 0, 1)
+    token_other = after(token_other, *qkv_parts)
+    qkv_parts = tied(qkv_parts, token_other)
+    output_other = swap(after(output_shard, token_other), half_bit)
+    expand_other = swap(after(expand_weight, token_other), half_bit)
+    homes = to_home(token_own, token_other)
+    sent = [gather_far(homes[0])]
+    sent.append(gather_far(after(homes[1], *sent[0])))
+    qkv_parts = doubled(qkv_parts, 0, 1, last)
+    qkv_got = moved(qkv_parts, last)
+    full_qkv = jnp.concatenate([qkv_parts[0], qkv_got[0], qkv_parts[1], qkv_got[1]], axis=0)
+    output_other = after(output_other, full_qkv, sent[0][-1])
+    output_parts = doubled(near(output_shard, output_other), 1, 0, last + 1)
     segs = [segments_of(j) for j in streams]
-    grads_home = [to_home(cotangent, j) for j in streams]
-
-    qkv = [dot_nn(x, full_qkv).astype(BF16) for x in rows]
-    context = [attention_forward(qkv[j], *segs[j]) for j in streams]
+
+    rows = [gather_near(sent[0])]
+    qkv = [dot_nn(rows[0], full_qkv).astype(BF16)]
+    context = [attention_forward(qkv[0], *segs[0])]
+    full_output = jnp.concatenate([x[:local_width] for x in output_parts], axis=1)
+    params = jnp.concatenate([x[local_width : local_width + 4] for x in output_parts], axis=1)
+    params = params.astype(F32)
+    gains, shifts = params[:2], params[2:]
+    partial = [reduce_near(dot_nn(context[0], full_output))]
+    attended = [reduce_far(partial[0])]
+    expand_other = after(expand_other, partial[0])
+    contract_other = swap(after(contract_weight, expand_other), half_bit)
+    expand_parts = doubled(near(expand_weight, expand_other), 0, 0, last)
+    rows.append(gather_near(tied(sent[1], partial[0])))
+    qkv.append(dot_nn(rows[1], full_qkv).astype(BF16))
+    context.append(attention_forward(qkv[1], *segs[1]))
+    expand_got = moved(tied(expand_parts, context[1]), last)
+
+    partial.append(reduce_near(dot_nn(context[1], full_output)))
+    attended.append(reduce_far(partial[1]))
     first = [
+        norm_forward(homes[0].astype(F32) + ready(attended[0], partial[1]), gains[0], shifts[0])
+    ]
+    normed = [first[0][0].astype(BF16)]
+    sent = [gather_far(normed[0])]
+    contract_other = after(contract_other, normed[0])
+    first.append(
         norm_forward(
-            homes[j].astype(F32) + reduce_rows(dot_nn(context[j], full_output)), gains[0], shifts[0]
+            homes[1].astype(F32) + ready(attended[1], contract_other), gains[0], shifts[0]
         )
-        for j in streams
-    ]
-    normed_rows = [gather_rows(first[j][0].astype(BF16)) for j in streams]
-    active, slope = [], []
+    )
+    normed.append(first[1][0].astype(BF16))
+    sent.append(gather_far(normed[1]))
+    cotangent_own, cotangent_send = parted(cotangent)
+    cotangent_other = swap(after(cotangent_send, contract_other), half_bit)
+    contract_parts = near(contract_weight, contract_other)
+    expand_got = tied(expand_got, normed[1])
+    full_expand = jnp.concatenate(
+        [expand_parts[0], expand_got[0], expand_parts[1], expand_got[1]], axis=0
+    )
+    contract_parts = doubled(tied(contract_parts, *expand_got), 1, 0, last)
+    normed_rows, active, slope, branch = [], [], [], []
+    gate = tuple(contract_parts)
     for j in streams:
+        normed_rows.append(after(gather_near(sent[j]), *gate))
         value, derivative = gelu_pair(dot_nn(normed_rows[j], full_expand))
         active.append(value.astype(BF16))
         slope.append(derivative.astype(BF16))
-    second = [
-        norm_forward(
-            first[j][0] + reduce_rows(dot_nn(active[j], full_contract)), gains[1], shifts[1]
+        gate = (active[j],)
+    contract_got = tied(moved(contract_parts, last), active[1])
+    full_contract = jnp.concatenate(
+        [contract_parts[0], contract_got[0], contract_parts[1], contract_got[1]], axis=1
+    )
+    grads_home = to_home(cotangent_own, after(cotangent_other, active[1]))
+    partial, pairs = [], []
+    gate = (active[1],)
+    for j in streams:
+        branch.append(dot_nn(after(active[j], *gate), full_contract).astype(BF16))
+        partial.append(reduce_near(branch[j]))
+        pairs.append(reduce_far(partial[j]))
+        gate = (branch[j],)
+
+    second, branch_grad, sent = [], [], []
+    gate = (partial[1], *grads_home)
+    for j in streams:
+        second.append(norm_forward(first[j][0] + ready(pairs[j], *gate), gains[1], shifts[1]))
+        branch_grad.append(
+            norm_backward(grads_home[j].astype(F32), second[j][1], second[j][2], gains[1])
         )
-        for j in streams
-    ]
-    result = from_home([second[j][0].astype(BF16) for j in streams])
-
-    branch_grad = [
-        norm_backward(grads_home[j].astype(F32), second[j][1], second[j][2], gains[1])
-        for j in streams
-    ]
-    branch_rows = [gather_rows(branch_grad[j][0].astype(BF16)) for j in streams]
-    hidden_grad = [
-        (dot_nt(branch_rows[j], full_contract) * slope[j].astype(F32)).astype(BF16)
-        for j in streams
-    ]
-    normed_grad = [
-        branch_grad[j][0] + reduce_rows(dot_nt(hidden_grad[j], full_expand)) for j in streams
-    ]
-    contract_grad = sum(dot_tn(active[j], branch_rows[j]) for j in streams).astype(BF16)
-    contract_grad = reduce_grad(column_pieces(contract_grad))
-    expand_grad = sum(dot_tn(normed_rows[j], hidden_grad[j]) for j in streams).astype(BF16)
-    expand_grad = reduce_grad(row_pieces(expand_grad))
-
-    first_grad = [
-        norm_backward(normed_grad[j], first[j][1], first[j][2], gains[0]) for j in streams
-    ]
-    attended_rows = [gather_rows(first_grad[j][0].astype(BF16)) for j in streams]
-    output_grad = sum(dot_tn(context[j], attended_rows[j]) for j in streams).astype(BF16)
-    output_grad = reduce_grad(column_pieces(output_grad))
-    context_grad = [dot_nt(attended_rows[j], full_output).astype(BF16) for j in streams]
-    qkv_grad = [attention_backward(qkv[j], context_grad[j], *segs[j]) for j in streams]
-    projection_grad = sum(dot_tn(rows[j], qkv_grad[j]) for j in streams).astype(BF16)
-    projection_grad = reduce_grad(row_pieces(projection_grad))
-    projection_grad = projection_grad.reshape(-1, heads, 3, DH)
-    query_grad, key_grad, value_grad = [
-        projection_grad[:, :, i].reshape(-1, local_width) for i in range(3)
-    ]
-    tokens_grad = from_home(
-        [
-            (first_grad[j][0] + reduce_rows(dot_nt(qkv_grad[j], full_qkv))).astype(BF16)
-            for j in streams
-        ]
-    ).astype(F32)
+        gate = (branch_grad[j][0].astype(BF16),)
+        sent.append(gather_far(gate[0]))
+    branch_rows, hidden_grad, normed_part = [], [], []
+    partial, pairs = [], []
+    for j in streams:
+        branch_rows.append(after(gather_near(sent[j]), *gate))
+        hidden_grad.append(
+            (dot_nt(branch_rows[j], full_contract) * slope[j].astype(F32)).astype(BF16)
+        )
+        normed_part.append(dot_nt(hidden_grad[j], full_expand).astype(BF16))
+        partial.append(reduce_near(normed_part[j]))
+        pairs.append(reduce_far(partial[j]))
+        gate = (partial[j],)
+    result_kept, result_got = sent_home(
+        [after(second[j][0].astype(BF16), branch_rows[1]) for j in streams]
+    )
+    tied_active = after(active[0], *gate)
+    contract_grad = dot_tn(tied_active, branch_rows[0]) + dot_tn(active[1], branch_rows[1])
+    contract_grad = contract_grad.astype(BF16)
+    contract_kept, contract_got = split_send(jnp.split(contract_grad, 2, axis=1), last, 1)
+    normed_grad = [branch_grad[0][0] + ready(pairs[0], contract_grad)]
+    first_grad = [norm_backward(normed_grad[0], first[0][1], first[0][2], gains[0])]
+    gate = first_grad[0][0].astype(BF16)
+    sent = [gather_far(gate)]
+    tied_normed = after(normed_rows[0], gate)
+    expand_grad = dot_tn(tied_normed, hidden_grad[0]) + dot_tn(normed_rows[1], hidden_grad[1])
+    expand_grad = expand_grad.astype(BF16)
+    result_got = after(result_got, expand_grad)
+    result = home_pair(result_kept, result_got)
+    normed_grad.append(branch_grad[1][0] + ready(pairs[1], expand_grad))
+    first_grad.append(norm_backward(normed_grad[1], first[1][1], first[1][2], gains[0]))
+    sent.append(gather_far(first_grad[1][0].astype(BF16)))
+    contract_got = tied(contract_got, expand_grad, sent[1][0])
+    contract_kept, contract_got = split_send(added(contract_kept, contract_got), last - 1, 1)
+    expand_kept, expand_got = split_send(
+        tied(jnp.split(expand_grad, 2, axis=0), *contract_kept), last, 0
+    )
 
     terms = jnp.stack(
         [
@@ -384,13 +470,49 @@
             sum(branch_grad[j][1][1] for j in streams),
         ]
     )
+
+    attended_rows = [after(gather_near(sent[0]), expand_grad, sent[1][0])]
+    context_grad = dot_nt(attended_rows[0], full_output).astype(BF16)
+    qkv_grad = [attention_backward(qkv[0], context_grad, *segs[0])]
+    partial = [reduce_near(dot_nt(qkv_grad[0], full_qkv).astype(BF16))]
+    pairs = [reduce_far(partial[0])]
+    attended_rows.append(after(gather_near(tied(sent[1], qkv_grad[0])), partial[0]))
+    contract_kept, contract_got = reduce_rest(
+        added(contract_kept, tied(contract_got, qkv_grad[0])), 1, last - 2
+    )
+    terms = after(terms, qkv_grad[0])
     for bit in t_bits + [core_bit]:
         terms = terms + swap(terms, bit)
-    terms = terms.reshape(4, chips, 2, -1)
-    for bit in p_bits[::-1]:
-        middle = terms.shape[1] // 2
-        terms = terms[:, :middle] + swap(terms[:, middle:], bit * 2 * tensor_size)
-    terms = turn_back(terms[:, 0, 0], 0) + turn_back(terms[:, 0, 1], 1)
+    terms = jnp.pad(terms, ((0, extra - 4), (0, 0)))
+    output_grad = dot_tn(context[0], attended_rows[0]) + dot_tn(context[1], attended_rows[1])
+    output_grad = jnp.concatenate([output_grad, terms], axis=0).astype(BF16)
+    expand_kept, expand_got = split_send(
+        added(expand_kept, tied(expand_got, output_grad)), last - 1, 0
+    )
+    context_grad = dot_nt(
+        after(attended_rows[1], output_grad, contract_kept, *expand_kept), full_output
+    ).astype(BF16)
+    qkv_grad.append(attention_backward(qkv[1], context_grad, *segs[1]))
+    expand_kept, expand_got = reduce_rest(
+        added(expand_kept, tied(expand_got, qkv_grad[1])), 0, last - 2
+    )
+    contract_grad = total_of(contract_kept, after(contract_got, expand_kept))
+    output_parts = jnp.split(output_grad, 2, axis=1)
+    partial.append(reduce_near(dot_nt(qkv_grad[1], full_qkv).astype(BF16)))
+    pairs.append(reduce_far(partial[1]))
+    projection_grad = dot_tn(after(rows[0], partial[1], expand_kept), qkv_grad[0])
+    projection_grad = (projection_grad + dot_tn(rows[1], qkv_grad[1])).astype(BF16)
+    token_sums = [
+        (first_grad[j][0] + ready(pairs[j], projection_grad)).astype(BF16) for j in streams
+    ]
+    output_grad = total_of(*reduce_rest(output_parts, 1, last))
+    tokens_grad = home_pair(*sent_home(token_sums)).astype(F32)
+    projection_grad = total_of(*reduce_rest(jnp.split(projection_grad, 2, axis=0), 0, last))
+    expand_grad = total_of(expand_kept, expand_got)
+    projection_grad = projection_grad.reshape(-1, heads, 3, DH)
+    query_grad, key_grad, value_grad = [
+        projection_grad[:, :, i].reshape(-1, local_width) for i in range(3)
+    ]
 
     return (
         result,
@@ -398,11 +520,11 @@
         query_grad,
         key_grad,
         value_grad,
-        output_grad,
+        output_grad[:local_width],
         expand_grad,
         contract_grad,
-        terms[:2],
-        terms[2:],
+        output_grad[local_width : local_width + 2],
+        output_grad[local_width + 2 : local_width + 4],
     )
 
 

time: 1360 us -> 1170 us (0.86); the launches traced: 1340 us -> 1170 us
  starting transfers between devices: 384 us -> 63.6 us
  waiting for transfers between devices: 395 us -> 571 us
  other arithmetic: 82 us -> 111 us
  matrix products: 278 us -> 250 us
  Pallas kernels: 113 us -> 95.7 us
  local copies, waits for them, and re-layouts: 87.6 us -> 73.4 us
    ppermute x97 -> x99, waiting for transfers between devices: 311 us -> 571 us  [swap(): return lax.ppermute(array, AXES, [(i, i ^ mask) for i in range(total)])]
    ppermute x97 -> x99, starting transfers between devices: 255 us -> 63.6 us  [swap(): return lax.ppermute(array, AXES, [(i, i ^ mask) for i in range(total)])]
    ppermute x26 -> x0, starting transfers between devices: 128 us -> none  [the longest x14 69.5 us: turn_back(): return lax.ppermute(array, AXES, turned(j, True))]
    ppermute x26 -> x0, waiting for transfers between devices: 83.3 us -> none  [the longest x14 76.6 us: turn_back(): return lax.ppermute(array, AXES, turned(j, True))]
    unnamed x244 -> x202, local copies, waits for them, and re-layouts: 57.6 us -> 32.4 us
    concatenate x1 -> x21, other arithmetic: 0.7 us -> 21.6 us  [the longest x7 9 us: gather_near(): jnp.concatenate(parts + [swap(part, core_bit) for part in parts], axis=0)]
    select_n x2 -> x25, other arithmetic: 2.28 us -> 21.4 us  [the longest x6 7.02 us: collect(): got = swap(jnp.where(same, second, first), core_bit)]
    pallas_call x8 -> x4, Pallas kernels: 42.4 us -> 25.6 us  [reorder(): pl.pallas_call(reorder_kernel, out_shape=jax.ShapeDtypeStruct(array.shape...]
  transfers between devices with their start and end apart: 123 -> 99, of which waited for: 37 -> 43; matrix products, arithmetic and copies ran while one was open for 30% -> 30% of each run, Pallas kernels for 7% -> 8%
where the time goes in v2:
time: 1170 us
  waiting for transfers between devices  571 us (49%)
  matrix products  250 us (21%)
  other arithmetic  111 us (9%)
  Pallas kernels  95.7 us (8%)
  local copies, waits for them, and re-layouts  73.4 us (6%)
  starting transfers between devices  63.6 us (5%)
    ppermute x99, waiting for transfers between devices, swap(): return lax.ppermute(array, AXES, [(i, i ^ mask) for i in range(total)])  571 us
    dot_general x8, matrix products, dot_nt(): lax.dot_general(left, right, (((1,), (1,)), ((), ())), preferred_element_...  86 us
    dot_general x8, matrix products, dot_nn(): return jnp.dot(left, right, preferred_element_type=F32)  83.1 us
    dot_general x8, matrix products, dot_tn(): lax.dot_general(left, right, (((0,), (0,)), ((), ())), preferred_element_...  80.8 us
    ppermute x99, starting transfers between devices, swap(): return lax.ppermute(array, AXES, [(i, i ^ mask) for i in range(total)])  63.6 us
    pallas_call x2, Pallas kernels, attention_backward(): pl.pallas_call(functools.partial(attention_backward_kernel, block=min(256...  46.5 us
    unnamed x202, local copies, waits for them, and re-layouts  32.4 us
    pallas_call x4, Pallas kernels, reorder(): pl.pallas_call(reorder_kernel, out_shape=jax.ShapeDtypeStruct(array.shape...  25.6 us
  transfers between devices with their start and end apart: 99, of which 43 were waited for; matrix products, arithmetic and copies ran while one was open for 30% of the time, Pallas kernels for 8%

profile of v2, /device:TPU:0, one launch (start us, length us, event | category | flops | bytes accessed | tf_op | source)
XLA Modules:
  0.0 1166.8 jit_solution(12959008706870578273)
XLA Ops:
  8.1 34.5 %collective-permute-done = bf16[256,1536]{0,1:T(8,128)(2,1)} collective-permute-done((bf16[256,1536]{0,1:T(8,128)(2,1)S(1)}, bf16[256,1536]{0,1:T(8,128)(2,1)}, u32[]{:S(2)}, u32[]{:S(2)}) %collective-permute-start) | collective-permute-done | bytes 786464 | tf_op jit(solution)/shard_map/ppermute | solution.py:220
  52.1 16.4 %collective-permute-done.3 = bf16[256,1536]{0,1:T(8,128)(2,1)S(1)} collective-permute-done((bf16[256,1536]{0,1:T(8,128)(2,1)S(1)}, bf16[256,1536]{0,1:T(8,128)(2,1)S(1)}, u32[]{:S(2)}, u32[]{:S(2)}) %collective-permute-start.3) | collective-permute-done | bytes 786464 | tf_op jit(solution)/shard_map/ppermute | solution.py:220
  71.7 28.5 %collective-permute-done.1 = bf16[256,2048]{1,0:T(8,128)(2,1)S(1)} collective-permute-done((bf16[256,2048]{1,0:T(8,128)(2,1)S(1)}, bf16[256,2048]{1,0:T(8,128)(2,1)S(1)}, u32[]{:S(2)}, u32[]{:S(2)}) %collective-permute-start.1) | collective-permute-done | bytes 1048608 | tf_op jit(solution)/shard_map/ppermute | solution.py:220
  118.2 21.7 %collective-permute-done.10 = bf16[512,1536]{0,1:T(8,128)(2,1)} collective-permute-done((bf16[512,1536]{0,1:T(8,128)(2,1)}, bf16[512,1536]{0,1:T(8,128)(2,1)}, u32[]{:S(2)}, u32[]{:S(2)}) %collective-permute-start.10) | collective-permute-done | bytes 1572896 | tf_op jit(solution)/shard_map/ppermute | solution.py:220
  160.0 12.3 %convolution_convert_fusion.3.qkv_ref = bf16[1024,1536]{1,0:T(8,128)(2,1)} fusion(bf16[2048,1536]{0,1:T(8,128)(2,1)} %copy-done.64, bf16[256,2048]{1,0:T(8,128)(2,1)} %collective-permute-done.8, bf16[256,2048]{1,0:T(8,128)(2,1)} %collective-permute-done.7, bf16[256,2048]{1,0:T(8,128)(2,1)} %collective-permute-done.6, ...), kind=kOutput, calls=%fused_computation.38 | convolution fusion | flops 6460801024 | bytes 13631488 | tf_op jit(solution)/shard_map/dot_general | solution.py:19
  196.8 39.4 %collective-permute-done.20 = bf16[256,2048]{1,0:T(8,128)(2,1)} collective-permute-done((bf16[256,2048]{1,0:T(8,128)(2,1)}, bf16[256,2048]{1,0:T(8,128)(2,1)}, u32[]{:S(2)}, u32[]{:S(2)}) %collective-permute-start.20) | collective-permute-done | bytes 1048608 | tf_op jit(solution)/shard_map/ppermute | solution.py:220
  282.2 18.8 %collective-permute-done.31 = bf16[256,2048]{1,0:T(8,128)(2,1)S(1)} collective-permute-done((bf16[256,2048]{1,0:T(8,128)(2,1)S(1)}, bf16[256,2048]{1,0:T(8,128)(2,1)S(1)}, u32[]{:S(2)}, u32[]{:S(2)}) %collective-permute-start.31) | collective-permute-done | bytes 1048608 | tf_op jit(solution)/shard_map/ppermute | solution.py:220
  306.6 19.9 %collective-permute-done.19 = bf16[256,2048]{1,0:T(8,128)(2,1)S(1)} collective-permute-done((bf16[256,2048]{1,0:T(8,128)(2,1)S(1)}, bf16[256,2048]{1,0:T(8,128)(2,1)S(1)}, u32[]{:S(2)}, u32[]{:S(2)}) %collective-permute-start.19) | collective-permute-done | bytes 1048608 | tf_op jit(solution)/shard_map/ppermute | solution.py:220
  330.4 23.0 %collective-permute-done.35 = bf16[256,2048]{1,0:T(8,128)(2,1)S(1)} collective-permute-done((bf16[256,2048]{1,0:T(8,128)(2,1)S(1)}, bf16[256,2048]{1,0:T(8,128)(2,1)S(1)}, u32[]{:S(2)}, u32[]{:S(2)}) %collective-permute-start.35) | collective-permute-done | bytes 1048608 | tf_op jit(solution)/shard_map/ppermute | solution.py:220
  360.1 15.8 %collective-permute-done.24 = bf16[256,2048]{1,0:T(8,128)(2,1)S(1)} collective-permute-done((bf16[256,2048]{1,0:T(8,128)(2,1)S(1)}, bf16[256,2048]{1,0:T(8,128)(2,1)S(1)}, u32[]{:S(2)}, u32[]{:S(2)}) %collective-permute-start.24) | collective-permute-done | bytes 1048608 | tf_op jit(solution)/shard_map/ppermute | solution.py:220
  386.4 22.4 %collective-permute-done.38 = bf16[256,2048]{1,0:T(8,128)(2,1)S(1)} collective-permute-done((bf16[256,2048]{1,0:T(8,128)(2,1)S(1)}, bf16[256,2048]{1,0:T(8,128)(2,1)S(1)}, u32[]{:S(2)}, u32[]{:S(2)}) %collective-permute-start.38) | collective-permute-done | bytes 1048608 | tf_op jit(solution)/shard_map/ppermute | solution.py:220
  408.8 15.4 %multiply_convert_fusion.3 = (bf16[1024,2048]{1,0:T(8,128)(2,1)}, f32[1024,2048]{1,0:T(8,128)}) fusion(bf16[1024,2048]{1,0:T(8,128)(2,1)S(1)} %pad_maximum_fusion.1, bf16[2048,2048]{1,0:T(8,128)(2,1)} %constant_dynamic-update-slice_fusion.12), kind=kOutput, calls=%fused_computation.10 | convolution fusion | flops 8608808960 | bytes 25165824 | tf_op jit(solution)/shard_map/dot_general | solution.py:19
  424.9 16.8 %multiply_convert_fusion.2 = (bf16[1024,2048]{1,0:T(8,128)(2,1)}, f32[1024,2048]{1,0:T(8,128)}) fusion(bf16[1024,2048]{1,0:T(8,128)(2,1)S(1)} %pad_maximum_fusion.2, bf16[2048,2048]{1,0:T(8,128)(2,1)} %constant_dynamic-update-slice_fusion.12), kind=kOutput, calls=%fused_computation.7 | convolution fusion | flops 8608808960 | bytes 25165824 | tf_op jit(solution)/shard_map/dot_general | solution.py:19
  505.2 18.0 %collective-permute-done.48 = bf16[256,2048]{1,0:T(8,128)(2,1)S(1)} collective-permute-done((bf16[256,2048]{1,0:T(8,128)(2,1)S(1)}, bf16[256,2048]{1,0:T(8,128)(2,1)S(1)}, u32[]{:S(2)}, u32[]{:S(2)}) %collective-permute-start.48) | collective-permute-done | bytes 1048608 | tf_op jit(solution)/shard_map/ppermute | solution.py:220
  524.3 20.4 %collective-permute-done.52 = bf16[256,2048]{1,0:T(8,128)(2,1)S(1)} collective-permute-done((bf16[256,2048]{1,0:T(8,128)(2,1)S(1)}, bf16[256,2048]{1,0:T(8,128)(2,1)S(1)}, u32[]{:S(2)}, u32[]{:S(2)}) %collective-permute-start.52) | collective-permute-done | bytes 1048608 | tf_op jit(solution)/shard_map/ppermute | solution.py:220
  547.9 17.8 %multiply_convert_fusion.1 = bf16[1024,2048]{1,0:T(8,128)(2,1)S(1)} fusion(bf16[1024,2048]{1,0:T(8,128)(2,1)S(1)} %pad_maximum_fusion.4, bf16[2048,2048]{1,0:T(8,128)(2,1)} %constant_dynamic-update-slice_fusion.18, f32[1024,2048]{1,0:T(8,128)} %get-tuple-element.287), kind=kOutput, calls=%fused_computation.5 | convolution fusion | flops 8631877632 | bytes 25165824 | tf_op jit(solution)/shard_map/dot_general | solution.py:27
  565.6 12.8 %convolution_convert_fusion.5 = bf16[1024,2048]{1,0:T(8,128)(2,1)S(1)} fusion(bf16[1024,2048]{1,0:T(8,128)(2,1)S(1)} %multiply_convert_fusion.1, bf16[2048,2048]{1,0:T(8,128)(2,1)} %constant_dynamic-update-slice_fusion.12), kind=kOutput, calls=%fused_computation.40 | convolution fusion | flops 8592031744 | bytes 16777216 | tf_op jit(solution)/shard_map/dot_general | solution.py:27
  588.5 18.7 %multiply_convert_fusion = bf16[1024,2048]{1,0:T(8,128)(2,1)} fusion(bf16[1024,2048]{1,0:T(8,128)(2,1)S(1)} %pad_maximum_fusion.3, bf16[2048,2048]{1,0:T(8,128)(2,1)} %constant_dynamic-update-slice_fusion.18, f32[1024,2048]{1,0:T(8,128)} %get-tuple-element.289), kind=kOutput, calls=%fused_computation.3 | convolution fusion | flops 8631877632 | bytes 25165824 | tf_op jit(solution)/shard_map/dot_general | solution.py:27
  607.2 12.6 %convolution_convert_fusion.4 = bf16[1024,2048]{1,0:T(8,128)(2,1)S(1)} fusion(bf16[1024,2048]{1,0:T(8,128)(2,1)} %multiply_convert_fusion, bf16[2048,2048]{1,0:T(8,128)(2,1)} %constant_dynamic-update-slice_fusion.12), kind=kOutput, calls=%fused_computation.39 | convolution fusion | flops 8592031744 | bytes 16777216 | tf_op jit(solution)/shard_map/dot_general | solution.py:27
  639.8 16.7 %add_convert_fusion.1 = bf16[2048,2048]{1,0:T(8,128)(2,1)} fusion(f32[2048,2048]{1,0:T(8,128)} %fusion.67, bf16[1024,2048]{1,0:T(8,128)(2,1)} %get-tuple-element.144, bf16[1024,2048]{1,0:T(8,128)(2,1)} %copy-done.41), kind=kOutput, calls=%fused_computation.1 | convolution fusion | flops 8598323200 | bytes 33554432 | tf_op jit(solution)/shard_map/dot_general | solution.py:23
  677.7 14.9 %add_convert_fusion = bf16[2048,2048]{1,0:T(8,128)(2,1)S(1)} fusion(f32[2048,2048]{1,0:T(8,128)} %fusion.68, bf16[1024,2048]{1,0:T(8,128)(2,1)} %copy-done.38, bf16[1024,2048]{1,0:T(8,128)(2,1)} %multiply_convert_fusion), kind=kOutput, calls=%fused_computation | convolution fusion | flops 8598323200 | bytes 33554432 | tf_op jit(solution)/shard_map/dot_general | solution.py:23
  705.2 13.3 %collective-permute-done.63 = bf16[256,2048]{1,0:T(8,128)(2,1)S(1)} collective-permute-done((bf16[256,2048]{1,0:T(8,128)(2,1)}, bf16[256,2048]{1,0:T(8,128)(2,1)S(1)}, u32[]{:S(2)}, u32[]{:S(2)}) %collective-permute-start.63) | collective-permute-done | bytes 1048608 | tf_op jit(solution)/shard_map/ppermute | solution.py:220
  744.1 23.2 %attention_backward.2 = bf16[1024,1536]{1,0:T(8,128)(2,1)} custom-call(bf16[1024,1536]{1,0:T(8,128)(2,1)} %convolution_convert_fusion.3.qkv_ref, bf16[1024,512]{1,0:T(8,128)(2,1)} %convolution_convert_fusion.11.grad_ref, s32[1024,1]{1,0:T(8,128)} %copy.30.seg_col_ref, s32[1,1024]{1,0:T(1,128)} %bitcast.137), custom_call_target="tpu_custom_call" | custom-call | flops 5368709120 | bytes 7340032 | tf_op jit(solution)/shard_map/attention_backward/pallas_call | solution.py:103
  767.2 22.0 %collective-permute-done.71 = bf16[2048,512]{1,0:T(8,128)(2,1)} collective-permute-done((bf16[2048,512]{1,0:T(8,128)(2,1)}, bf16[2048,512]{1,0:T(8,128)(2,1)}, u32[]{:S(2)}, u32[]{:S(2)}) %collective-permute-start.71) | collective-permute-done | bytes 2097184 | tf_op jit(solution)/shard_map/ppermute | solution.py:220
  796.9 17.1 %collective-permute-done.69 = f32[4,2048]{1,0:T(4,128)S(1)} collective-permute-done((f32[4,2048]{1,0:T(4,128)S(1)}, f32[4,2048]{1,0:T(4,128)S(1)}, u32[]{:S(2)}, u32[]{:S(2)}) %collective-permute-start.69) | collective-permute-done | bytes 32800 | tf_op jit(solution)/shard_map/ppermute | solution.py:220
  837.8 23.1 %collective-permute-done.57 = bf16[256,2048]{1,0:T(8,128)(2,1)S(1)} collective-permute-done((bf16[256,2048]{1,0:T(8,128)(2,1)S(1)}, bf16[256,2048]{1,0:T(8,128)(2,1)S(1)}, u32[]{:S(2)}, u32[]{:S(2)}) %collective-permute-start.57) | collective-permute-done | bytes 1048608 | tf_op jit(solution)/shard_map/ppermute | solution.py:220
  892.0 23.4 %attention_backward.3 = bf16[1024,1536]{1,0:T(8,128)(2,1)} custom-call(bf16[1024,1536]{1,0:T(8,128)(2,1)} %convolution_convert_fusion.2.qkv_ref, bf16[1024,512]{1,0:T(8,128)(2,1)} %convolution_convert_fusion.10.grad_ref, s32[1024,1]{1,0:T(8,128)} %copy.31.seg_col_ref, s32[1,1024]{1,0:T(1,128)} %bitcast.134), custom_call_target="tpu_custom_call" | custom-call | flops 5368709120 | bytes 7340032 | tf_op jit(solution)/shard_map/attention_backward/pallas_call | solution.py:103
  952.4 51.6 %collective-permute-done.97 = bf16[256,2048]{1,0:T(8,128)(2,1)S(1)} collective-permute-done((bf16[256,2048]{1,0:T(8,128)(2,1)S(1)}, bf16[256,2048]{1,0:T(8,128)(2,1)S(1)}, u32[]{:S(2)}, u32[]{:S(2)}) %collective-permute-start.97) | collective-permute-done | bytes 1048608 | tf_op jit(solution)/shard_map/ppermute | solution.py:220
  1024.1 21.3 %collective-permute-done.82 = bf16[256,2048]{1,0:T(8,128)(2,1)} collective-permute-done((bf16[256,2048]{1,0:T(8,128)(2,1)}, bf16[256,2048]{1,0:T(8,128)(2,1)}, u32[]{:S(2)}, u32[]{:S(2)}) %collective-permute-start.82) | collective-permute-done | bytes 1048608 | tf_op jit(solution)/shard_map/ppermute | solution.py:220
  1066.7 13.1 %collective-permute-done.87 = bf16[256,1536]{0,1:T(8,128)(2,1)S(1)} collective-permute-done((bf16[256,1536]{0,1:T(8,128)(2,1)S(1)}, bf16[256,1536]{0,1:T(8,128)(2,1)S(1)}, u32[]{:S(2)}, u32[]{:S(2)}) %collective-permute-start.87) | collective-permute-done | bytes 786464 | tf_op jit(solution)/shard_map/ppermute | solution.py:220
  1087.2 59.1 %collective-permute-done.84 = bf16[256,2048]{1,0:T(8,128)(2,1)S(1)} collective-permute-done((bf16[256,2048]{1,0:T(8,128)(2,1)S(1)}, bf16[256,2048]{1,0:T(8,128)(2,1)S(1)}, u32[]{:S(2)}, u32[]{:S(2)}) %collective-permute-start.84) | collective-permute-done | bytes 1048608 | tf_op jit(solution)/shard_map/ppermute | solution.py:220
  1148.8 14.3 %collective-permute-done.90 = bf16[256,1536]{0,1:T(8,128)(2,1)S(1)} collective-permute-done((bf16[256,1536]{0,1:T(8,128)(2,1)S(1)}, bf16[256,1536]{0,1:T(8,128)(2,1)S(1)}, u32[]{:S(2)}, u32[]{:S(2)}) %collective-permute-start.90) | collective-permute-done | bytes 786464 | tf_op jit(solution)/shard_map/ppermute | solution.py:220
  (578 shorter events, 465.8 us)
Async XLA Ops:
  51.9 48.3 %collective-permute-start.1 = (bf16[256,2048]{1,0:T(8,128)(2,1)S(1)}, bf16[256,2048]{1,0:T(8,128)(2,1)S(1)}, u32[]{:S(2)}, u32[]{:S(2)}) collective-permute-start(bf16[256,2048]{1,0:T(8,128)(2,1)S(1)} %select_bitcast_fusion.5), channel_id=1, source_target_pairs={{0,2},{1,3},{2,0},{3,1},{4,6},{5,7},{6,4},{7,5},{8,10},{9,11},{10,... | collective-permute-start | bytes 3145736 | tf_op jit(solution)/shard_map/ppermute | solution.py:220
  52.0 50.6 %collective-permute-start.11 = (s32[1024]{0:T(1024)S(1)}, s32[1024]{0:T(1024)S(1)}, u32[]{:S(2)}, u32[]{:S(2)}) collective-permute-start(s32[1024]{0:T(1024)S(1)} %bitcast.138), channel_id=1, source_target_pairs={{0,4},{1,5},{2,6},{3,7},{4,0},{5,1},{6,2},{7,3},{8,12},{9,13},{10,... | collective-permute-start | bytes 12296 | tf_op jit(solution)/shard_map/ppermute | solution.py:220
  189.9 46.4 %collective-permute-start.20 = (bf16[256,2048]{1,0:T(8,128)(2,1)}, bf16[256,2048]{1,0:T(8,128)(2,1)}, u32[]{:S(2)}, u32[]{:S(2)}) collective-permute-start(bf16[256,2048]{1,0:T(8,128)(2,1)} %get-tuple-element.117), channel_id=1, source_target_pairs={{0,1},{1,0},{2,3},{3,2},{4,5},{5,4},{6,7},{7,6},{8,9},{9,8},{10,11... | collective-permute-start | bytes 3145736 | tf_op jit(solution)/shard_map/ppermute | solution.py:220
  190.8 48.2 %collective-permute-start.27 = (bf16[256,2048]{1,0:T(8,128)(2,1)S(1)}, bf16[256,2048]{1,0:T(8,128)(2,1)S(1)}, u32[]{:S(2)}, u32[]{:S(2)}) collective-permute-start(bf16[256,2048]{1,0:T(8,128)(2,1)S(1)} %copy-done.35), channel_id=1, source_target_pairs={{0,2},{1,3},{2,0},{3,1},{4,6},{5,7},{6,4},{7,5},{8,10},{9,11},{10,... | collective-permute-start | bytes 3145736 | tf_op jit(solution)/shard_map/ppermute | solution.py:220
  280.2 46.4 %collective-permute-start.19 = (bf16[256,2048]{1,0:T(8,128)(2,1)S(1)}, bf16[256,2048]{1,0:T(8,128)(2,1)S(1)}, u32[]{:S(2)}, u32[]{:S(2)}) collective-permute-start(bf16[256,2048]{1,0:T(8,128)(2,1)S(1)} %slice.483), channel_id=1, source_target_pairs={{0,1},{1,0},{2,3},{3,2},{4,5},{5,4},{6,7},{7,6},{8,9},{9,8},{10,11... | collective-permute-start | bytes 3145736 | tf_op jit(solution)/shard_map/ppermute | solution.py:220
  280.2 50.0 %collective-permute-start.28 = (bf16[2048,256]{1,0:T(8,128)(2,1)S(1)}, bf16[2048,256]{1,0:T(8,128)(2,1)S(1)}, u32[]{:S(2)}, u32[]{:S(2)}) collective-permute-start(bf16[2048,256]{1,0:T(8,128)(2,1)S(1)} %copy-done.43), channel_id=1, source_target_pairs={{0,2},{1,3},{2,0},{3,1},{4,6},{5,7},{6,4},{7,5},{8,10},{9,11},{10,... | collective-permute-start | bytes 3145736 | tf_op jit(solution)/shard_map/ppermute | solution.py:220
  302.6 51.4 %collective-permute-start.33 = (bf16[512,2048]{1,0:T(8,128)(2,1)S(1)}, bf16[512,2048]{1,0:T(8,128)(2,1)S(1)}, u32[]{:S(2)}, u32[]{:S(2)}) collective-permute-start(bf16[512,2048]{1,0:T(8,128)(2,1)S(1)} %pad_maximum_fusion.9), channel_id=1, source_target_pairs={{0,16},{1,17},{2,18},{3,19},{4,20},{5,21},{6,22},{7,23},{8,24},{9,... | collective-permute-start | bytes 6291464 | tf_op jit(solution)/shard_map/ppermute | solution.py:220
  304.2 49.8 %collective-permute-start.34 = (bf16[512,2048]{1,0:T(8,128)(2,1)S(1)}, bf16[512,2048]{1,0:T(8,128)(2,1)S(1)}, u32[]{:S(2)}, u32[]{:S(2)}) collective-permute-start(bf16[512,2048]{1,0:T(8,128)(2,1)S(1)} %pad_maximum_fusion.10), channel_id=1, source_target_pairs={{0,8},{1,9},{2,10},{3,11},{4,12},{5,13},{6,14},{7,15},{8,0},{9,1},... | collective-permute-start | bytes 6291464 | tf_op jit(solution)/shard_map/ppermute | solution.py:220
  328.5 47.3 %collective-permute-start.24 = (bf16[256,2048]{1,0:T(8,128)(2,1)S(1)}, bf16[256,2048]{1,0:T(8,128)(2,1)S(1)}, u32[]{:S(2)}, u32[]{:S(2)}) collective-permute-start(bf16[256,2048]{1,0:T(8,128)(2,1)S(1)} %fusion.26), channel_id=1, source_target_pairs={{0,1},{1,0},{2,3},{3,2},{4,5},{5,4},{6,7},{7,6},{8,9},{9,8},{10,11... | collective-permute-start | bytes 3145736 | tf_op jit(solution)/shard_map/ppermute | solution.py:220
  330.3 54.1 %collective-permute-start.25 = (bf16[256,2048]{1,0:T(8,128)(2,1)S(1)}, bf16[256,2048]{1,0:T(8,128)(2,1)S(1)}, u32[]{:S(2)}, u32[]{:S(2)}) collective-permute-start(bf16[256,2048]{1,0:T(8,128)(2,1)S(1)} %fusion.26), channel_id=1, source_target_pairs={{0,4},{1,5},{2,6},{3,7},{4,0},{5,1},{6,2},{7,3},{8,12},{9,13},{10,... | collective-permute-start | bytes 3145736 | tf_op jit(solution)/shard_map/ppermute | solution.py:220
  354.8 53.9 %collective-permute-start.38 = (bf16[256,2048]{1,0:T(8,128)(2,1)S(1)}, bf16[256,2048]{1,0:T(8,128)(2,1)S(1)}, u32[]{:S(2)}, u32[]{:S(2)}) collective-permute-start(bf16[256,2048]{1,0:T(8,128)(2,1)S(1)} %fusion.27), channel_id=1, source_target_pairs={{0,1},{1,0},{2,3},{3,2},{4,5},{5,4},{6,7},{7,6},{8,9},{9,8},{10,11... | collective-permute-start | bytes 3145736 | tf_op jit(solution)/shard_map/ppermute | solution.py:220
  381.5 60.1 %collective-permute-start.46 = (bf16[256,2048]{1,0:T(8,128)(2,1)S(1)}, bf16[256,2048]{1,0:T(8,128)(2,1)S(1)}, u32[]{:S(2)}, u32[]{:S(2)}) collective-permute-start(bf16[256,2048]{1,0:T(8,128)(2,1)S(1)} %select_bitcast_fusion.4), channel_id=1, source_target_pairs={{0,2},{1,3},{2,0},{3,1},{4,6},{5,7},{6,4},{7,5},{8,10},{9,11},{10,... | collective-permute-start | bytes 3145736 | tf_op jit(solution)/shard_map/ppermute | solution.py:220
  383.0 41.1 %collective-permute-start.39 = (bf16[256,2048]{1,0:T(8,128)(2,1)S(1)}, bf16[256,2048]{1,0:T(8,128)(2,1)S(1)}, u32[]{:S(2)}, u32[]{:S(2)}) collective-permute-start(bf16[256,2048]{1,0:T(8,128)(2,1)S(1)} %fusion.27), channel_id=1, source_target_pairs={{0,4},{1,5},{2,6},{3,7},{4,0},{5,1},{6,2},{7,3},{8,12},{9,13},{10,... | collective-permute-start | bytes 3145736 | tf_op jit(solution)/shard_map/ppermute | solution.py:220
  384.4 57.3 %collective-permute-start.42 = (bf16[2048,512]{1,0:T(8,128)(2,1)S(1)}, bf16[2048,512]{1,0:T(8,128)(2,1)S(1)}, u32[]{:S(2)}, u32[]{:S(2)}) collective-permute-start(bf16[2048,512]{1,0:T(8,128)(2,1)S(1)} %constant_dynamic-update-slice_fusion.10), channel_id=1, source_target_pairs={{0,8},{1,9},{2,10},{3,11},{4,12},{5,13},{6,14},{7,15},{8,0},{9,1},... | collective-permute-start | bytes 6291464 | tf_op jit(solution)/shard_map/ppermute | solution.py:220
  384.9 56.8 %collective-permute-start.41 = (bf16[2048,512]{1,0:T(8,128)(2,1)S(1)}, bf16[2048,512]{1,0:T(8,128)(2,1)S(1)}, u32[]{:S(2)}, u32[]{:S(2)}) collective-permute-start(bf16[2048,512]{1,0:T(8,128)(2,1)S(1)} %get-tuple-element.258), channel_id=1, source_target_pairs={{0,16},{1,17},{2,18},{3,19},{4,20},{5,21},{6,22},{7,23},{8,24},{9,... | collective-permute-start | bytes 6291464 | tf_op jit(solution)/shard_map/ppermute | solution.py:220
  505.1 41.8 %collective-permute-start.53 = (bf16[256,2048]{1,0:T(8,128)(2,1)S(1)}, bf16[256,2048]{1,0:T(8,128)(2,1)S(1)}, u32[]{:S(2)}, u32[]{:S(2)}) collective-permute-start(bf16[256,2048]{1,0:T(8,128)(2,1)S(1)} %fusion.42), channel_id=1, source_target_pairs={{0,4},{1,5},{2,6},{3,7},{4,0},{5,1},{6,2},{7,3},{8,12},{9,13},{10,... | collective-permute-start | bytes 3145736 | tf_op jit(solution)/shard_map/ppermute | solution.py:220
  663.6 66.3 %collective-permute-start.60 = (bf16[256,2048]{1,0:T(8,128)(2,1)}, bf16[256,2048]{1,0:T(8,128)(2,1)}, u32[]{:S(2)}, u32[]{:S(2)}) collective-permute-start(bf16[256,2048]{1,0:T(8,128)(2,1)} %get-tuple-element.215), channel_id=1, source_target_pairs={{0,1},{1,0},{2,3},{3,2},{4,5},{5,4},{6,7},{7,6},{8,9},{9,8},{10,11... | collective-permute-start | bytes 3145736 | tf_op jit(solution)/shard_map/ppermute | solution.py:220
  664.9 70.1 %collective-permute-start.61 = (bf16[256,2048]{1,0:T(8,128)(2,1)}, bf16[256,2048]{1,0:T(8,128)(2,1)}, u32[]{:S(2)}, u32[]{:S(2)}) collective-permute-start(bf16[256,2048]{1,0:T(8,128)(2,1)} %get-tuple-element.215), channel_id=1, source_target_pairs={{0,4},{1,5},{2,6},{3,7},{4,0},{5,1},{6,2},{7,3},{8,12},{9,13},{10,... | collective-permute-start | bytes 3145736 | tf_op jit(solution)/shard_map/ppermute | solution.py:220
  696.7 117.9 %collective-permute-start.76 = (bf16[512,2048]{1,0:T(8,128)(2,1)}, bf16[512,2048]{1,0:T(8,128)(2,1)}, u32[]{:S(2)}, u32[]{:S(2)}) collective-permute-start(bf16[512,2048]{1,0:T(8,128)(2,1)} %split.119), channel_id=1, source_target_pairs={{0,16},{1,17},{2,18},{3,19},{4,20},{5,21},{6,22},{7,23},{8,24},{9,... | collective-permute-start | bytes 6291464 | tf_op jit(solution)/shard_map/ppermute | solution.py:220
  704.3 85.0 %collective-permute-start.71 = (bf16[2048,512]{1,0:T(8,128)(2,1)}, bf16[2048,512]{1,0:T(8,128)(2,1)}, u32[]{:S(2)}, u32[]{:S(2)}) collective-permute-start(bf16[2048,512]{1,0:T(8,128)(2,1)} %get-tuple-element.233), channel_id=1, source_target_pairs={{0,16},{1,17},{2,18},{3,19},{4,20},{5,21},{6,22},{7,23},{8,24},{9,... | collective-permute-start | bytes 6291464 | tf_op jit(solution)/shard_map/ppermute | solution.py:220
  718.4 72.1 %collective-permute-start.72 = (bf16[2048,512]{1,0:T(8,128)(2,1)}, bf16[2048,512]{1,0:T(8,128)(2,1)}, u32[]{:S(2)}, u32[]{:S(2)}) collective-permute-start(bf16[2048,512]{1,0:T(8,128)(2,1)} %get-tuple-element.232), channel_id=1, source_target_pairs={{0,8},{1,9},{2,10},{3,11},{4,12},{5,13},{6,14},{7,15},{8,0},{9,1},... | collective-permute-start | bytes 6291464 | tf_op jit(solution)/shard_map/ppermute | solution.py:220
  735.0 81.7 %collective-permute-start.77 = (bf16[512,2048]{1,0:T(8,128)(2,1)}, bf16[512,2048]{1,0:T(8,128)(2,1)}, u32[]{:S(2)}, u32[]{:S(2)}) collective-permute-start(bf16[512,2048]{1,0:T(8,128)(2,1)} %split.120), channel_id=1, source_target_pairs={{0,8},{1,9},{2,10},{3,11},{4,12},{5,13},{6,14},{7,15},{8,0},{9,1},... | collective-permute-start | bytes 6291464 | tf_op jit(solution)/shard_map/ppermute | solution.py:220
  736.5 59.6 %collective-permute-start.56 = (bf16[256,2048]{1,0:T(8,128)(2,1)}, bf16[256,2048]{1,0:T(8,128)(2,1)S(1)}, u32[]{:S(2)}, u32[]{:S(2)}) collective-permute-start(bf16[256,2048]{1,0:T(8,128)(2,1)} %broadcast_select_fusion.16), channel_id=1, source_target_pairs={{0,4},{1,5},{2,6},{3,7},{4,0},{5,1},{6,2},{7,3},{8,12},{9,13},{10,... | collective-permute-start | bytes 3145736 | tf_op jit(solution)/shard_map/ppermute | solution.py:220
  814.5 46.4 %collective-permute-start.57 = (bf16[256,2048]{1,0:T(8,128)(2,1)S(1)}, bf16[256,2048]{1,0:T(8,128)(2,1)S(1)}, u32[]{:S(2)}, u32[]{:S(2)}) collective-permute-start(bf16[256,2048]{1,0:T(8,128)(2,1)S(1)} %broadcast_select_fusion.14), channel_id=1, source_target_pairs={{0,2},{1,3},{2,0},{3,1},{4,6},{5,7},{6,4},{7,5},{8,10},{9,11},{10,... | collective-permute-start | bytes 3145736 | tf_op jit(solution)/shard_map/ppermute | solution.py:220
  837.8 46.8 %collective-permute-start.75 = (bf16[2048,256]{1,0:T(8,128)(2,1)S(1)}, bf16[2048,256]{1,0:T(8,128)(2,1)S(1)}, u32[]{:S(2)}, u32[]{:S(2)}) collective-permute-start(bf16[2048,256]{1,0:T(8,128)(2,1)S(1)} %broadcast_select_fusion.2), channel_id=1, source_target_pairs={{0,4},{1,5},{2,6},{3,7},{4,0},{5,1},{6,2},{7,3},{8,12},{9,13},{10,... | collective-permute-start | bytes 3145736 | tf_op jit(solution)/shard_map/ppermute | solution.py:220
  933.8 70.1 %collective-permute-start.97 = (bf16[256,2048]{1,0:T(8,128)(2,1)S(1)}, bf16[256,2048]{1,0:T(8,128)(2,1)S(1)}, u32[]{:S(2)}, u32[]{:S(2)}) collective-permute-start(bf16[256,2048]{1,0:T(8,128)(2,1)S(1)} %broadcast_select_fusion.8), channel_id=1, source_target_pairs={{0,2},{1,3},{2,0},{3,1},{4,6},{5,7},{6,4},{7,5},{8,10},{9,11},{10,... | collective-permute-start | bytes 3145736 | tf_op jit(solution)/shard_map/ppermute | solution.py:220
  944.7 121.9 %collective-permute-start.98 = (bf16[2048,256]{1,0:T(8,128)(2,1)}, bf16[2048,256]{1,0:T(8,128)(2,1)}, u32[]{:S(2)}, u32[]{:S(2)}) collective-permute-start(bf16[2048,256]{1,0:T(8,128)(2,1)} %get-tuple-element.253), channel_id=1, source_target_pairs={{0,2},{1,3},{2,0},{3,1},{4,6},{5,7},{6,4},{7,5},{8,10},{9,11},{10,... | collective-permute-start | bytes 3145736 | tf_op jit(solution)/shard_map/ppermute | solution.py:220
  947.6 76.5 %collective-permute-start.65 = (bf16[256,2048]{1,0:T(8,128)(2,1)}, bf16[256,2048]{1,0:T(8,128)(2,1)}, u32[]{:S(2)}, u32[]{:S(2)}) collective-permute-start(bf16[256,2048]{1,0:T(8,128)(2,1)} %slice.477), channel_id=1, source_target_pairs={{0,1},{1,0},{2,3},{3,2},{4,5},{5,4},{6,7},{7,6},{8,9},{9,8},{10,11... | collective-permute-start | bytes 3145736 | tf_op jit(solution)/shard_map/ppermute | solution.py:220
  948.5 73.9 %collective-permute-start.95 = (bf16[528,256]{1,0:T(8,128)(2,1)}, bf16[528,256]{1,0:T(8,128)(2,1)S(1)}, u32[]{:S(2)}, u32[]{:S(2)}) collective-permute-start(bf16[528,256]{1,0:T(8,128)(2,1)} %broadcast_select_fusion.28), channel_id=1, source_target_pairs={{0,4},{1,5},{2,6},{3,7},{4,0},{5,1},{6,2},{7,3},{8,12},{9,13},{10,... | collective-permute-start | bytes 811016 | tf_op jit(solution)/shard_map/ppermute | solution.py:220
  950.4 95.1 %collective-permute-start.82 = (bf16[256,2048]{1,0:T(8,128)(2,1)}, bf16[256,2048]{1,0:T(8,128)(2,1)}, u32[]{:S(2)}, u32[]{:S(2)}) collective-permute-start(bf16[256,2048]{1,0:T(8,128)(2,1)} %slice.476), channel_id=1, source_target_pairs={{0,1},{1,0},{2,3},{3,2},{4,5},{5,4},{6,7},{7,6},{8,9},{9,8},{10,11... | collective-permute-start | bytes 3145736 | tf_op jit(solution)/shard_map/ppermute | solution.py:220
  1081.0 65.3 %collective-permute-start.84 = (bf16[256,2048]{1,0:T(8,128)(2,1)S(1)}, bf16[256,2048]{1,0:T(8,128)(2,1)S(1)}, u32[]{:S(2)}, u32[]{:S(2)}) collective-permute-start(bf16[256,2048]{1,0:T(8,128)(2,1)S(1)} %broadcast_select_fusion.9), channel_id=1, source_target_pairs={{0,2},{1,3},{2,0},{3,1},{4,6},{5,7},{6,4},{7,5},{8,10},{9,11},{10,... | collective-permute-start | bytes 3145736 | tf_op jit(solution)/shard_map/ppermute | solution.py:220
  1084.3 78.9 %collective-permute-start.90 = (bf16[256,1536]{0,1:T(8,128)(2,1)S(1)}, bf16[256,1536]{0,1:T(8,128)(2,1)S(1)}, u32[]{:S(2)}, u32[]{:S(2)}) collective-permute-start(bf16[256,1536]{0,1:T(8,128)(2,1)S(1)} %broadcast_select_fusion.22), channel_id=1, source_target_pairs={{0,2},{1,3},{2,0},{3,1},{4,6},{5,7},{6,4},{7,5},{8,10},{9,11},{10,... | collective-permute-start | bytes 2359304 | tf_op jit(solution)/shard_map/ppermute | solution.py:220
  (160 other events, 2964.5 us)

commit v3 on v2

--- a/solution.py
+++ b/solution.py
@@ -11,6 +11,7 @@
 EPSILON = 1e-06
 NEGATIVE = -1e30
 AXES = ("dp", "tensor")
+HINT = 1 << 16
 F32 = jnp.float32
 BF16 = jnp.bfloat16
 
@@ -89,9 +90,7 @@
         ],
         out_specs=pl.BlockSpec((length, DH), lambda i: (0, i)),
         cost_estimate=pl.CostEstimate(
-            flops=4 * heads * length * length * DH,
-            transcendentals=heads * length * length,
-            bytes_accessed=2 * length * heads * DH * 4,
+            flops=HINT, transcendentals=0, bytes_accessed=HINT
         ),
         name="attention_forward",
     )(qkv, seg_col, seg_row)
@@ -113,29 +112,70 @@
         out_specs=pl.BlockSpec((length, 3 * DH), lambda i: (0, i)),
         scratch_shapes=[pltpu.VMEM((length, DH), F32), pltpu.VMEM((length, DH), F32)],
         cost_estimate=pl.CostEstimate(
-            flops=10 * heads * length * length * DH,
-            transcendentals=heads * length * length,
-            bytes_accessed=2 * length * heads * DH * 7,
+            flops=HINT, transcendentals=0, bytes_accessed=HINT
         ),
         name="attention_backward",
     )(qkv, grad, seg_col, seg_row)
 
 
-def reorder_kernel(mask_ref, in_ref, out_ref):
-    out_ref[...] = in_ref[...]
+def matmul_kernel(*refs, contract, finish, extras):
+    left_ref, right_ref = refs[:2]
+    product = lax.dot_general(
+        left_ref[...], right_ref[...], (((1,), (contract,)), ((), ())), preferred_element_type=F32
+    )
+    results = finish(product, *[ref[...] for ref in refs[2 : 2 + extras]])
+    for ref, value in zip(refs[2 + extras :], results):
+        ref[...] = value.astype(ref.dtype)
+
+
+def rounded(product):
+    return (product,)
+
+
+def matmul(left, right, transposed=False, finish=rounded, extras=(), outs=1, name="matmul"):
+    rows, depth = left.shape
+    columns = right.shape[0 if transposed else 1]
+    block = min(512, columns)
+    if transposed:
+        right_spec = pl.BlockSpec((block, depth), lambda i: (i, 0))
+    else:
+        right_spec = pl.BlockSpec((depth, block), lambda i: (0, i))
+    wide = pl.BlockSpec((rows, block), lambda i: (0, i))
+    found = pl.pallas_call(
+        functools.partial(
+            matmul_kernel, contract=int(transposed), finish=finish, extras=len(extras)
+        ),
+        out_shape=[jax.ShapeDtypeStruct((rows, columns), BF16)] * outs,
+        grid=(columns // block,),
+        in_specs=[pl.BlockSpec((rows, depth), lambda i: (0, 0)), right_spec] + [wide] * len(extras),
+        out_specs=[wide] * outs,
+        cost_estimate=pl.CostEstimate(
+            flops=HINT, transcendentals=0, bytes_accessed=HINT
+        ),
+        name=name,
+    )(left, right, *extras)
+    return found if outs > 1 else found[0]
+
+
+def reorder_kernel(table_ref, in_ref, out_ref):
+    count = table_ref.shape[0]
+    size = in_ref.shape[1] // count
+    for i in range(count):
+        start = pl.multiple_of(table_ref[i] * size, size)
+        out_ref[:, i * size : (i + 1) * size] = in_ref[:, pl.ds(start, size)]
 
 
 def reorder(array, table):
     rows, width = array.shape
-    count = table.shape[0]
+    block = min(128, rows)
     return pl.pallas_call(
         reorder_kernel,
         out_shape=jax.ShapeDtypeStruct(array.shape, array.dtype),
         grid_spec=pltpu.PrefetchScalarGridSpec(
             num_scalar_prefetch=1,
-            grid=(count,),
-            in_specs=[pl.BlockSpec((rows, width // count), lambda i, m: (0, m[i]))],
-            out_specs=pl.BlockSpec((rows, width // count), lambda i, m: (0, i)),
+            grid=(rows // block,),
+            in_specs=[pl.BlockSpec((block, width), lambda i, table: (i, 0))],
+            out_specs=pl.BlockSpec((block, width), lambda i, table: (i, 0)),
         ),
         cost_estimate=pl.CostEstimate(
             flops=0, transcendentals=0, bytes_accessed=4 * rows * width
@@ -320,7 +360,7 @@
         got = swap(jnp.where(same, other, own), core_bit)
         pair = [jnp.where(same, own, got), jnp.where(same, got, other)]
         both = reorder(jnp.concatenate(pair, axis=0), to_table)
-        return [both[:block_tokens], both[block_tokens:]]
+        return [both[:block_tokens], both[block_tokens:]], both
 
     def sent_home(pieces):
         both = reorder(jnp.concatenate(pieces, axis=0), from_table)
@@ -346,7 +386,7 @@
     qkv_parts = tied(qkv_parts, token_other)
     output_other = swap(after(output_shard, token_other), half_bit)
     expand_other = swap(after(expand_weight, token_other), half_bit)
-    homes = to_home(token_own, token_other)
+    homes, _ = to_home(token_own, token_other)
     sent = [gather_far(homes[0])]
     sent.append(gather_far(after(homes[1], *sent[0])))
     qkv_parts = doubled(qkv_parts, 0, 1, last)
@@ -365,26 +405,27 @@
     gains, shifts = params[:2], params[2:]
     partial = [reduce_near(dot_nn(context[0], full_output))]
     attended = [reduce_far(partial[0])]
-    expand_other = after(expand_other, partial[0])
     contract_other = swap(after(contract_weight, expand_other), half_bit)
     expand_parts = doubled(near(expand_weight, expand_other), 0, 0, last)
-    rows.append(gather_near(tied(sent[1], partial[0])))
+    sent1 = tied(sent[1], partial[0])
+    pre = ()
+    rows.append(after(gather_near(sent1), partial[0], *pre))
     qkv.append(dot_nn(rows[1], full_qkv).astype(BF16))
-    context.append(attention_forward(qkv[1], *segs[1]))
+    pre = ()
+    context.append(attention_forward(after(qkv[1], *pre), *segs[1]))
     expand_got = moved(tied(expand_parts, context[1]), last)
 
-    partial.append(reduce_near(dot_nn(context[1], full_output)))
+    pre = ()
+    partial.append(reduce_near(dot_nn(after(context[1], *pre), full_output)))
     attended.append(reduce_far(partial[1]))
-    first = [
-        norm_forward(homes[0].astype(F32) + ready(attended[0], partial[1]), gains[0], shifts[0])
-    ]
+    attended[0] = ready(attended[0], partial[1])
+    first = [norm_forward(homes[0].astype(F32) + attended[0], gains[0], shifts[0])]
     normed = [first[0][0].astype(BF16)]
     sent = [gather_far(normed[0])]
-    contract_other = after(contract_other, normed[0])
+    contract_other = after(contract_other, context[1])
+    pre = (contract_other, normed[0])
     first.append(
-        norm_forward(
-            homes[1].astype(F32) + ready(attended[1], contract_other), gains[0], shifts[0]
-        )
+        norm_forward(homes[1].astype(F32) + ready(attended[1], *pre), gains[0], shifts[0])
     )
     normed.append(first[1][0].astype(BF16))
     sent.append(gather_far(normed[1]))
@@ -398,27 +439,32 @@
     contract_parts = doubled(tied(contract_parts, *expand_got), 1, 0, last)
     normed_rows, active, slope, branch = [], [], [], []
     gate = tuple(contract_parts)
-    for j in streams:
+    contract_got = moved(contract_parts, last)
+
+    def feed(j, *gate):
         normed_rows.append(after(gather_near(sent[j]), *gate))
         value, derivative = gelu_pair(dot_nn(normed_rows[j], full_expand))
         active.append(value.astype(BF16))
         slope.append(derivative.astype(BF16))
-        gate = (active[j],)
-    contract_got = tied(moved(contract_parts, last), active[1])
+
+    feed(0, normed[1], *gate)
+    feed(1, active[0])
+    contract_got = tied(contract_got, active[1])
     full_contract = jnp.concatenate(
         [contract_parts[0], contract_got[0], contract_parts[1], contract_got[1]], axis=1
     )
-    grads_home = to_home(cotangent_own, after(cotangent_other, active[1]))
-    partial, pairs = [], []
-    gate = (active[1],)
-    for j in streams:
-        branch.append(dot_nn(after(active[j], *gate), full_contract).astype(BF16))
-        partial.append(reduce_near(branch[j]))
-        pairs.append(reduce_far(partial[j]))
-        gate = (branch[j],)
+    gate = active[1]
+    branch.append(dot_nn(after(active[0], gate), full_contract).astype(BF16))
+    partial = [reduce_near(branch[0])]
+    pairs = [reduce_far(partial[0])]
+    grads_home, grads_all = to_home(cotangent_own, after(cotangent_other, active[1]))
+    gate = (branch[0],)
+    branch.append(dot_nn(after(active[1], *gate), full_contract).astype(BF16))
+    partial.append(reduce_near(branch[1]))
+    pairs.append(reduce_far(partial[1]))
 
     second, branch_grad, sent = [], [], []
-    gate = (partial[1], *grads_home)
+    gate = (partial[1], grads_all)
     for j in streams:
         second.append(norm_forward(first[j][0] + ready(pairs[j], *gate), gains[1], shifts[1]))
         branch_grad.append(
@@ -426,8 +472,10 @@
         )
         gate = (branch_grad[j][0].astype(BF16),)
         sent.append(gather_far(gate[0]))
+    result_kept, result_got = sent_home([second[j][0].astype(BF16) for j in streams])
     branch_rows, hidden_grad, normed_part = [], [], []
     partial, pairs = [], []
+    gate = (*gate, result_kept)
     for j in streams:
         branch_rows.append(after(gather_near(sent[j]), *gate))
         hidden_grad.append(
@@ -436,31 +484,33 @@
         normed_part.append(dot_nt(hidden_grad[j], full_expand).astype(BF16))
         partial.append(reduce_near(normed_part[j]))
         pairs.append(reduce_far(partial[j]))
-        gate = (partial[j],)
-    result_kept, result_got = sent_home(
-        [after(second[j][0].astype(BF16), branch_rows[1]) for j in streams]
-    )
-    tied_active = after(active[0], *gate)
-    contract_grad = dot_tn(tied_active, branch_rows[0]) + dot_tn(active[1], branch_rows[1])
-    contract_grad = contract_grad.astype(BF16)
+        if j == 0:
+            branch_all = gather_near(sent[1])
+            gate = partial[0]
+            contract_grad = dot_tn(after(active[0], gate), branch_rows[0])
+            contract_grad = contract_grad + dot_tn(active[1], branch_all)
+            contract_grad = contract_grad.astype(BF16)
+            result_got = after(result_got, partial[0])
+            gate = (contract_grad,)
+            gate = (*gate, result_got)
     contract_kept, contract_got = split_send(jnp.split(contract_grad, 2, axis=1), last, 1)
+    result = home_pair(result_kept, result_got)
     normed_grad = [branch_grad[0][0] + ready(pairs[0], contract_grad)]
     first_grad = [norm_backward(normed_grad[0], first[0][1], first[0][2], gains[0])]
     gate = first_grad[0][0].astype(BF16)
     sent = [gather_far(gate)]
-    tied_normed = after(normed_rows[0], gate)
-    expand_grad = dot_tn(tied_normed, hidden_grad[0]) + dot_tn(normed_rows[1], hidden_grad[1])
+    expand_grad = dot_tn(after(normed_rows[0], gate, partial[1]), hidden_grad[0])
+    contract_sum = added(contract_kept, tied(contract_got, partial[1]))
+    pre = tuple(contract_sum)
+    expand_grad = expand_grad + dot_tn(after(normed_rows[1], *pre), hidden_grad[1])
     expand_grad = expand_grad.astype(BF16)
-    result_got = after(result_got, expand_grad)
-    result = home_pair(result_kept, result_got)
+    contract_kept, contract_got = split_send(contract_sum, last - 1, 1)
+    expand_kept = jnp.split(expand_grad, 2, axis=0)
+    expand_kept, expand_got = split_send(expand_kept, last, 0)
     normed_grad.append(branch_grad[1][0] + ready(pairs[1], expand_grad))
     first_grad.append(norm_backward(normed_grad[1], first[1][1], first[1][2], gains[0]))
-    sent.append(gather_far(first_grad[1][0].astype(BF16)))
-    contract_got = tied(contract_got, expand_grad, sent[1][0])
-    contract_kept, contract_got = split_send(added(contract_kept, contract_got), last - 1, 1)
-    expand_kept, expand_got = split_send(
-        tied(jnp.split(expand_grad, 2, axis=0), *contract_kept), last, 0
-    )
+    gate = first_grad[1][0].astype(BF16)
+    sent.append(gather_far(gate))
 
     terms = jnp.stack(
         [
@@ -471,43 +521,68 @@
         ]
     )
 
-    attended_rows = [after(gather_near(sent[0]), expand_grad, sent[1][0])]
+    contract_sum = added(contract_kept, tied(contract_got, expand_grad))
+    contract_kept, contract_got = reduce_rest(contract_sum, 1, last - 2)
+    pre = (gate, contract_kept)
+    attended_rows = [after(gather_near(sent[0]), expand_grad, *pre)]
     context_grad = dot_nt(attended_rows[0], full_output).astype(BF16)
     qkv_grad = [attention_backward(qkv[0], context_grad, *segs[0])]
-    partial = [reduce_near(dot_nt(qkv_grad[0], full_qkv).astype(BF16))]
+    attended_rows.append(gather_near(tied(sent[1], qkv_grad[0])))
+    expand_sum = added(expand_kept, tied(expand_got, qkv_grad[0]))
+    expand_kept, expand_got = split_send(expand_sum, last - 1, 0)
+    pre = tuple(expand_sum)
+    tied_grad = after(qkv_grad[0], attended_rows[1], *pre)
+    token_part = dot_nt(tied_grad, full_qkv).astype(BF16)
+    partial = [reduce_near(token_part)]
     pairs = [reduce_far(partial[0])]
-    attended_rows.append(after(gather_near(tied(sent[1], qkv_grad[0])), partial[0]))
-    contract_kept, contract_got = reduce_rest(
-        added(contract_kept, tied(contract_got, qkv_grad[0])), 1, last - 2
-    )
-    terms = after(terms, qkv_grad[0])
+    terms = after(terms, attended_rows[1])
     for bit in t_bits + [core_bit]:
         terms = terms + swap(terms, bit)
     terms = jnp.pad(terms, ((0, extra - 4), (0, 0)))
-    output_grad = dot_tn(context[0], attended_rows[0]) + dot_tn(context[1], attended_rows[1])
+    pre = ()
+    output_grad = dot_tn(after(context[0], partial[0], *pre), attended_rows[0])
+    output_grad = output_grad + dot_tn(context[1], attended_rows[1])
     output_grad = jnp.concatenate([output_grad, terms], axis=0).astype(BF16)
-    expand_kept, expand_got = split_send(
-        added(expand_kept, tied(expand_got, output_grad)), last - 1, 0
-    )
-    context_grad = dot_nt(
-        after(attended_rows[1], output_grad, contract_kept, *expand_kept), full_output
-    ).astype(BF16)
-    qkv_grad.append(attention_backward(qkv[1], context_grad, *segs[1]))
+    output_kept, output_got = split_send(jnp.split(output_grad, 2, axis=1), last, 1)
+    pre = ()
+    context_grad = dot_nt(after(attended_rows[1], output_grad, *pre), full_output)
+    qkv_grad.append(attention_backward(qkv[1], context_grad.astype(BF16), *segs[1]))
     expand_kept, expand_got = reduce_rest(
         added(expand_kept, tied(expand_got, qkv_grad[1])), 0, last - 2
     )
-    contract_grad = total_of(contract_kept, after(contract_got, expand_kept))
-    output_parts = jnp.split(output_grad, 2, axis=1)
-    partial.append(reduce_near(dot_nt(qkv_grad[1], full_qkv).astype(BF16)))
+    output_sum = added(output_kept, tied(output_got, qkv_grad[1]))
+    output_kept, output_got = split_send(output_sum, last - 1, 1)
+    token_sums = [(first_grad[0][0] + ready(pairs[0], qkv_grad[1])).astype(BF16)]
+    contract_got = after(contract_got, qkv_grad[1])
+    pre = (contract_got,)
+    pre = (*pre, token_sums[0])
+    pre = (*pre, *output_sum)
+    tied_grad = after(qkv_grad[1], expand_kept, *pre)
+    token_part = dot_nt(tied_grad, full_qkv).astype(BF16)
+    partial.append(reduce_near(token_part))
     pairs.append(reduce_far(partial[1]))
-    projection_grad = dot_tn(after(rows[0], partial[1], expand_kept), qkv_grad[0])
-    projection_grad = (projection_grad + dot_tn(rows[1], qkv_grad[1])).astype(BF16)
-    token_sums = [
-        (first_grad[j][0] + ready(pairs[j], projection_grad)).astype(BF16) for j in streams
-    ]
-    output_grad = total_of(*reduce_rest(output_parts, 1, last))
-    tokens_grad = home_pair(*sent_home(token_sums)).astype(F32)
-    projection_grad = total_of(*reduce_rest(jnp.split(projection_grad, 2, axis=0), 0, last))
+    middle = width // 2
+    parts = []
+    gate = (partial[1],)
+    for i in range(2):
+        columns = slice(i * middle, (i + 1) * middle)
+        part = dot_tn(after(rows[0][:, columns], *gate), qkv_grad[0])
+        parts.append((part + dot_tn(rows[1][:, columns], qkv_grad[1])).astype(BF16))
+        if i == 0:
+            gate = (parts[0],)
+            expand_got = after(expand_got, parts[0])
+            gate = (*gate, expand_got)
+            output_got = tied(output_got, parts[0])
+            output_kept, output_got = reduce_rest(added(output_kept, output_got), 1, last - 2)
+            gate = (*gate, output_kept)
+    pre = (parts[1],)
+    token_sums.append((first_grad[1][0] + ready(pairs[1], *pre)).astype(BF16))
+    tokens_kept, tokens_got = sent_home(token_sums)
+    output_got = after(output_got, token_sums[1])
+    output_grad = total_of(output_kept, output_got)
+    tokens_grad = home_pair(tokens_kept, tokens_got).astype(F32)
+    projection_grad = total_of(*reduce_rest(parts, 0, last))
+    contract_grad = total_of(contract_kept, contract_got)
     expand_grad = total_of(expand_kept, expand_got)
     projection_grad = projection_grad.reshape(-1, heads, 3, DH)
     query_grad, key_grad, value_grad = [

time: 1170 us -> 1070 us (0.915)
  waiting for transfers between devices: 571 us -> 467 us
    ppermute x99, waiting for transfers between devices: 571 us -> 467 us  [swap(): return lax.ppermute(array, AXES, [(i, i ^ mask) for i in range(total)])]
    unnamed x202 -> x242, local copies, waits for them, and re-layouts: 32.4 us -> 37.8 us
    dot_general x8 -> x10, matrix products: 80.8 us -> 84.5 us  [dot_tn(): lax.dot_general(left, right, (((0,), (0,)), ((), ())), preferred_element_...]
  transfers between devices with their start and end apart: 99 -> 99, of which waited for: 43 -> 49; matrix products, arithmetic and copies ran while one was open for 30% -> 35% of each run, Pallas kernels for 8% -> 8%
where the time goes in v3:
time: 1070 us; the launch traced here: 1060 us
  waiting for transfers between devices  467 us (44%)
  matrix products  249 us (23%)
  other arithmetic  121 us (11%)
  Pallas kernels  89.1 us (8%)
  local copies, waits for them, and re-layouts  71.3 us (7%)
  starting transfers between devices  62.3 us (6%)
    ppermute x99, waiting for transfers between devices, swap(): return lax.ppermute(array, AXES, [(i, i ^ mask) for i in range(total)])  467 us
    dot_general x8, matrix products, dot_nt(): lax.dot_general(left, right, (((1,), (1,)), ((), ())), preferred_element_...  85.2 us
    dot_general x10, matrix products, dot_tn(): lax.dot_general(left, right, (((0,), (0,)), ((), ())), preferred_element_...  84.5 us
    dot_general x8, matrix products, dot_nn(): return jnp.dot(left, right, preferred_element_type=F32)  79.7 us
    ppermute x99, starting transfers between devices, swap(): return lax.ppermute(array, AXES, [(i, i ^ mask) for i in range(total)])  62.3 us
    pallas_call x2, Pallas kernels, attention_backward(): pl.pallas_call(functools.partial(attention_backward_kernel, block=min(256...  46.6 us
    unnamed x242, local copies, waits for them, and re-layouts  37.8 us
    pallas_call x2, Pallas kernels, attention_forward(): pl.pallas_call(functools.partial(attention_forward_kernel, block=min(256,...  23.6 us
  transfers between devices with their start and end apart: 99, of which 49 were waited for; matrix products, arithmetic and copies ran while one was open for 35% of the time, Pallas kernels for 8%

profile of v3, /device:TPU:0, one launch (start us, length us, event | category | flops | bytes accessed | tf_op | source)
XLA Modules:
  0.0 1063.4 jit_solution(4828633082435152280)
XLA Ops:
  8.4 34.5 %collective-permute-done = bf16[256,1536]{1,0:T(8,128)(2,1)} collective-permute-done((bf16[256,1536]{1,0:T(8,128)(2,1)S(1)}, bf16[256,1536]{1,0:T(8,128)(2,1)}, u32[]{:S(2)}, u32[]{:S(2)}) %collective-permute-start) | collective-permute-done | bytes 786464 | tf_op jit(solution)/shard_map/ppermute | solution.py:260
  52.4 16.4 %collective-permute-done.3 = bf16[256,1536]{1,0:T(8,128)(2,1)S(1)} collective-permute-done((bf16[256,1536]{1,0:T(8,128)(2,1)S(1)}, bf16[256,1536]{1,0:T(8,128)(2,1)S(1)}, u32[]{:S(2)}, u32[]{:S(2)}) %collective-permute-start.3) | collective-permute-done | bytes 786464 | tf_op jit(solution)/shard_map/ppermute | solution.py:260
  71.9 28.5 %collective-permute-done.1 = bf16[256,2048]{1,0:T(8,128)(2,1)S(1)} collective-permute-done((bf16[256,2048]{1,0:T(8,128)(2,1)S(1)}, bf16[256,2048]{1,0:T(8,128)(2,1)S(1)}, u32[]{:S(2)}, u32[]{:S(2)}) %collective-permute-start.1) | collective-permute-done | bytes 1048608 | tf_op jit(solution)/shard_map/ppermute | solution.py:260
  116.8 23.3 %collective-permute-done.10 = bf16[512,1536]{1,0:T(8,128)(2,1)} collective-permute-done((bf16[512,1536]{1,0:T(8,128)(2,1)}, bf16[512,1536]{1,0:T(8,128)(2,1)}, u32[]{:S(2)}, u32[]{:S(2)}) %collective-permute-start.10) | collective-permute-done | bytes 1572896 | tf_op jit(solution)/shard_map/ppermute | solution.py:260
  160.0 12.5 %convolution_convert_fusion.3.qkv_ref = bf16[1024,1536]{1,0:T(8,128)(2,1)} fusion(bf16[2048,1536]{1,0:T(8,128)(2,1)} %copy-done.77, bf16[256,2048]{1,0:T(8,128)(2,1)} %collective-permute-done.8, bf16[256,2048]{1,0:T(8,128)(2,1)} %collective-permute-done.7, bf16[256,2048]{1,0:T(8,128)(2,1)} %collective-permute-done.6, bf16[256,2048]{1,0:T(8,128)(2,1)} %get-tuple-element.272), kind=kOutput, calls=%fused_computation.39 | convolution fusion | flops 6460801024 | bytes 13631488 | tf_op jit(solution)/shard_map/dot_general | solution.py:20
  172.5 11.8 %attention_forward.2 = bf16[1024,512]{1,0:T(8,128)(2,1)} custom-call(bf16[1024,1536]{1,0:T(8,128)(2,1)} %convolution_convert_fusion.3.qkv_ref, s32[1024,1]{1,0:T(8,128)} %copy.30.seg_col_ref, s32[1,1024]{1,0:T(1,128)} %bitcast.131), custom_call_target="tpu_custom_call" | custom-call | flops 65536 | bytes 65536 | tf_op jit(solution)/shard_map/attention_forward/pallas_call | solution.py:82
  206.3 17.0 %collective-permute-done.20 = bf16[256,2048]{1,0:T(8,128)(2,1)} collective-permute-done((bf16[256,2048]{1,0:T(8,128)(2,1)}, bf16[256,2048]{1,0:T(8,128)(2,1)}, u32[]{:S(2)}, u32[]{:S(2)}) %collective-permute-start.20) | collective-permute-done | bytes 1048608 | tf_op jit(solution)/shard_map/ppermute | solution.py:260
  259.9 14.3 %collective-permute-done.29 = bf16[2048,256]{1,0:T(8,128)(2,1)} collective-permute-done((bf16[2048,256]{1,0:T(8,128)(2,1)S(1)}, bf16[2048,256]{1,0:T(8,128)(2,1)}, u32[]{:S(2)}, u32[]{:S(2)}) %collective-permute-start.29) | collective-permute-done | bytes 1048608 | tf_op jit(solution)/shard_map/ppermute | solution.py:260
  283.9 22.4 %collective-permute-done.19 = bf16[256,2048]{1,0:T(8,128)(2,1)S(1)} collective-permute-done((bf16[256,2048]{1,0:T(8,128)(2,1)S(1)}, bf16[256,2048]{1,0:T(8,128)(2,1)S(1)}, u32[]{:S(2)}, u32[]{:S(2)}) %collective-permute-start.19) | collective-permute-done | bytes 1048608 | tf_op jit(solution)/shard_map/ppermute | solution.py:260
  309.8 19.7 %collective-permute-done.34 = bf16[512,2048]{1,0:T(8,128)(2,1)S(1)} collective-permute-done((bf16[512,2048]{1,0:T(8,128)(2,1)S(1)}, bf16[512,2048]{1,0:T(8,128)(2,1)S(1)}, u32[]{:S(2)}, u32[]{:S(2)}) %collective-permute-start.34) | collective-permute-done | bytes 2097184 | tf_op jit(solution)/shard_map/ppermute | solution.py:260
  337.8 16.9 %collective-permute-done.24 = bf16[256,2048]{1,0:T(8,128)(2,1)S(1)} collective-permute-done((bf16[256,2048]{1,0:T(8,128)(2,1)S(1)}, bf16[256,2048]{1,0:T(8,128)(2,1)S(1)}, u32[]{:S(2)}, u32[]{:S(2)}) %collective-permute-start.24) | collective-permute-done | bytes 1048608 | tf_op jit(solution)/shard_map/ppermute | solution.py:260
  363.6 22.6 %collective-permute-done.38 = bf16[256,2048]{1,0:T(8,128)(2,1)S(1)} collective-permute-done((bf16[256,2048]{1,0:T(8,128)(2,1)S(1)}, bf16[256,2048]{1,0:T(8,128)(2,1)S(1)}, u32[]{:S(2)}, u32[]{:S(2)}) %collective-permute-start.38) | collective-permute-done | bytes 1048608 | tf_op jit(solution)/shard_map/ppermute | solution.py:260
  386.2 15.3 %multiply_convert_fusion.3 = (bf16[1024,2048]{1,0:T(8,128)(2,1)}, f32[1024,2048]{1,0:T(8,128)}) fusion(bf16[1024,2048]{1,0:T(8,128)(2,1)S(1)} %pad_maximum_fusion.2, bf16[2048,2048]{1,0:T(8,128)(2,1)} %constant_dynamic-update-slice_fusion.8), kind=kOutput, calls=%fused_computation.9 | convolution fusion | flops 8608808960 | bytes 25165824 | tf_op jit(solution)/shard_map/dot_general | solution.py:20
  402.3 16.1 %multiply_convert_fusion.2 = (bf16[1024,2048]{1,0:T(8,128)(2,1)S(1)}, f32[1024,2048]{1,0:T(8,128)}) fusion(bf16[1024,2048]{1,0:T(8,128)(2,1)S(1)} %pad_maximum_fusion.3, bf16[2048,2048]{1,0:T(8,128)(2,1)} %constant_dynamic-update-slice_fusion.8), kind=kOutput, calls=%fused_computation.6 | convolution fusion | flops 8608808960 | bytes 25165824 | tf_op jit(solution)/shard_map/dot_general | solution.py:20
  463.3 14.0 %collective-permute-done.44 = bf16[256,2048]{1,0:T(8,128)(2,1)} collective-permute-done((bf16[256,2048]{1,0:T(8,128)(2,1)S(1)}, bf16[256,2048]{1,0:T(8,128)(2,1)}, u32[]{:S(2)}, u32[]{:S(2)}) %collective-permute-start.44) | collective-permute-done | bytes 1048608 | tf_op jit(solution)/shard_map/ppermute | solution.py:260
  482.3 17.4 %collective-permute-done.48 = bf16[256,2048]{1,0:T(8,128)(2,1)S(1)} collective-permute-done((bf16[256,2048]{1,0:T(8,128)(2,1)S(1)}, bf16[256,2048]{1,0:T(8,128)(2,1)S(1)}, u32[]{:S(2)}, u32[]{:S(2)}) %collective-permute-start.48) | collective-permute-done | bytes 1048608 | tf_op jit(solution)/shard_map/ppermute | solution.py:260
  526.5 16.3 %multiply_convert_fusion.1 = bf16[1024,2048]{1,0:T(8,128)(2,1)S(1)} fusion(bf16[1024,2048]{1,0:T(8,128)(2,1)S(1)} %pad_maximum_fusion.4, bf16[2048,2048]{1,0:T(8,128)(2,1)} %constant_dynamic-update-slice_fusion.14, f32[1024,2048]{1,0:T(8,128)} %get-tuple-element.315), kind=kOutput, calls=%fused_computation.4 | convolution fusion | flops 8631877632 | bytes 25165824 | tf_op jit(solution)/shard_map/dot_general | solution.py:28
  542.8 13.0 %convolution_convert_fusion.5 = bf16[1024,2048]{1,0:T(8,128)(2,1)S(1)} fusion(bf16[1024,2048]{1,0:T(8,128)(2,1)S(1)} %multiply_convert_fusion.1, bf16[2048,2048]{1,0:T(8,128)(2,1)} %constant_dynamic-update-slice_fusion.8), kind=kOutput, calls=%fused_computation.41 | convolution fusion | flops 8592031744 | bytes 16777216 | tf_op jit(solution)/shard_map/dot_general | solution.py:28
  567.8 11.9 %fusion.70 = f32[2048,2048]{1,0:T(8,128)} fusion(bf16[1024,2048]{1,0:T(8,128)(2,1)S(1)} %copy-done.103, bf16[1024,2048]{1,0:T(8,128)(2,1)S(1)} %pad_maximum_fusion.4), kind=kOutput, calls=%fused_computation.312 | convolution fusion | flops 8589934592 | bytes 25165824 | tf_op jit(solution)/shard_map/dot_general | solution.py:24
  579.8 16.5 %add_convert_fusion.1 = bf16[2048,2048]{1,0:T(8,128)(2,1)} fusion(f32[2048,2048]{1,0:T(8,128)} %fusion.70, bf16[1024,2048]{1,0:T(8,128)(2,1)} %copy-done.101, bf16[256,2048]{1,0:T(8,128)(2,1)} %copy-done.76, bf16[256,2048]{1,0:T(8,128)(2,1)} %copy-done.75, bf16[256,2048]{1,0:T(8,128)(2,1)} %copy-done.74, bf16[256,2048]{1,0:T(8,128)(2,1)} %copy-done.53), kind=kOutput, calls=%fused_computation.1 | convolution fusion | flops 8615100416 | bytes 33554432 | tf_op jit(solution)/shard_map/dot_general | solution.py:24
  606.7 18.5 %multiply_convert_fusion = bf16[1024,2048]{1,0:T(8,128)(2,1)} fusion(bf16[1024,2048]{1,0:T(8,128)(2,1)S(1)} %copy-done.40, bf16[2048,2048]{1,0:T(8,128)(2,1)} %constant_dynamic-update-slice_fusion.14, f32[1024,2048]{1,0:T(8,128)} %get-tuple-element.317), kind=kOutput, calls=%fused_computation.2 | convolution fusion | flops 8631877632 | bytes 25165824 | tf_op jit(solution)/shard_map/dot_general | solution.py:28
  625.2 12.8 %convolution_convert_fusion.4 = bf16[1024,2048]{1,0:T(8,128)(2,1)S(1)} fusion(bf16[1024,2048]{1,0:T(8,128)(2,1)} %multiply_convert_fusion, bf16[2048,2048]{1,0:T(8,128)(2,1)} %constant_dynamic-update-slice_fusion.8), kind=kOutput, calls=%fused_computation.40 | convolution fusion | flops 8592031744 | bytes 16777216 | tf_op jit(solution)/shard_map/dot_general | solution.py:28
  658.8 11.9 %fusion.71 = f32[2048,2048]{1,0:T(8,128)} fusion(bf16[1024,2048]{1,0:T(8,128)(2,1)S(1)} %copy-done.38, bf16[1024,2048]{1,0:T(8,128)(2,1)S(1)} %copy-done.105), kind=kOutput, calls=%fused_computation.313 | convolution fusion | flops 8589934592 | bytes 25165824 | tf_op jit(solution)/shard_map/dot_general | solution.py:24
  672.3 16.9 %add_convert_fusion = bf16[2048,2048]{1,0:T(8,128)(2,1)} fusion(f32[2048,2048]{1,0:T(8,128)} %fusion.71, bf16[1024,2048]{1,0:T(8,128)(2,1)} %copy-done.39, bf16[1024,2048]{1,0:T(8,128)(2,1)} %multiply_convert_fusion), kind=kOutput, calls=%fused_computation | convolution fusion | flops 8598323200 | bytes 33554432 | tf_op jit(solution)/shard_map/dot_general | solution.py:24
  715.8 23.2 %attention_backward.2 = bf16[1024,1536]{1,0:T(8,128)(2,1)} custom-call(bf16[1024,1536]{1,0:T(8,128)(2,1)} %convolution_convert_fusion.3.qkv_ref, bf16[1024,512]{1,0:T(8,128)(2,1)} %convolution_convert_fusion.11.grad_ref, s32[1024,1]{1,0:T(8,128)} %copy.30.seg_col_ref, s32[1,1024]{1,0:T(1,128)} %bitcast.132), custom_call_target="tpu_custom_call" | custom-call | flops 65536 | bytes 65536 | tf_op jit(solution)/shard_map/attention_backward/pallas_call | solution.py:102
  768.2 16.9 %collective-permute-done.78 = bf16[256,2048]{1,0:T(8,128)(2,1)S(1)} collective-permute-done((bf16[256,2048]{1,0:T(8,128)(2,1)S(1)}, bf16[256,2048]{1,0:T(8,128)(2,1)S(1)}, u32[]{:S(2)}, u32[]{:S(2)}) %collective-permute-start.78) | collective-permute-done | bytes 1048608 | tf_op jit(solution)/shard_map/ppermute | solution.py:260
  800.5 23.4 %attention_backward.3 = bf16[1024,1536]{1,0:T(8,128)(2,1)} custom-call(bf16[1024,1536]{1,0:T(8,128)(2,1)} %convolution_convert_fusion.2.qkv_ref, bf16[1024,512]{1,0:T(8,128)(2,1)} %convolution_convert_fusion.10.grad_ref, s32[1024,1]{1,0:T(8,128)} %copy.31.seg_col_ref, s32[1,1024]{1,0:T(1,128)} %bitcast.129), custom_call_target="tpu_custom_call" | custom-call | flops 65536 | bytes 65536 | tf_op jit(solution)/shard_map/attention_backward/pallas_call | solution.py:102
  884.9 27.3 %collective-permute-done.86 = bf16[256,2048]{1,0:T(8,128)(2,1)S(1)} collective-permute-done((bf16[256,2048]{1,0:T(8,128)(2,1)}, bf16[256,2048]{1,0:T(8,128)(2,1)S(1)}, u32[]{:S(2)}, u32[]{:S(2)}) %collective-permute-start.86) | collective-permute-done | bytes 1048608 | tf_op jit(solution)/shard_map/ppermute | solution.py:260
  924.7 11.9 %collective-permute-done.85 = bf16[256,2048]{1,0:T(8,128)(2,1)S(1)} collective-permute-done((bf16[256,2048]{1,0:T(8,128)(2,1)S(1)}, bf16[256,2048]{1,0:T(8,128)(2,1)S(1)}, u32[]{:S(2)}, u32[]{:S(2)}) %collective-permute-start.85) | collective-permute-done | bytes 1048608 | tf_op jit(solution)/shard_map/ppermute | solution.py:260
  982.5 20.7 %collective-permute-done.98 = bf16[528,256]{1,0:T(8,128)(2,1)S(1)} collective-permute-done((bf16[528,256]{1,0:T(8,128)(2,1)S(1)}, bf16[528,256]{1,0:T(8,128)(2,1)S(1)}, u32[]{:S(2)}, u32[]{:S(2)}) %collective-permute-start.98) | collective-permute-done | bytes 270368 | tf_op jit(solution)/shard_map/ppermute | solution.py:260
  1005.0 37.5 %collective-permute-done.91 = bf16[256,2048]{1,0:T(8,128)(2,1)S(1)} collective-permute-done((bf16[256,2048]{1,0:T(8,128)(2,1)S(1)}, bf16[256,2048]{1,0:T(8,128)(2,1)S(1)}, u32[]{:S(2)}, u32[]{:S(2)}) %collective-permute-start.91) | collective-permute-done | bytes 1048608 | tf_op jit(solution)/shard_map/ppermute | solution.py:260
  1045.0 14.3 %collective-permute-done.97 = bf16[256,1536]{1,0:T(8,128)(2,1)S(1)} collective-permute-done((bf16[256,1536]{1,0:T(8,128)(2,1)S(1)}, bf16[256,1536]{1,0:T(8,128)(2,1)S(1)}, u32[]{:S(2)}, u32[]{:S(2)}) %collective-permute-start.97) | collective-permute-done | bytes 786464 | tf_op jit(solution)/shard_map/ppermute | solution.py:260
  (618 shorter events, 464.4 us)
Async XLA Ops:
  4.3 38.6 %collective-permute-start = (bf16[256,1536]{1,0:T(8,128)(2,1)S(1)}, bf16[256,1536]{1,0:T(8,128)(2,1)}, u32[]{:S(2)}, u32[]{:S(2)}) collective-permute-start(bf16[256,1536]{1,0:T(8,128)(2,1)S(1)} %copy.27), channel_id=1, source_target_pairs={{0,2},{1,3},{2,0},{3,1},{4,6},{5,7},{6,4},{7,5},{8,10},{9,11},{10,... | collective-permute-start | bytes 2359304 | tf_op jit(solution)/shard_map/ppermute | solution.py:260
  52.2 48.3 %collective-permute-start.1 = (bf16[256,2048]{1,0:T(8,128)(2,1)S(1)}, bf16[256,2048]{1,0:T(8,128)(2,1)S(1)}, u32[]{:S(2)}, u32[]{:S(2)}) collective-permute-start(bf16[256,2048]{1,0:T(8,128)(2,1)S(1)} %select_bitcast_fusion.5), channel_id=1, source_target_pairs={{0,2},{1,3},{2,0},{3,1},{4,6},{5,7},{6,4},{7,5},{8,10},{9,11},{10,... | collective-permute-start | bytes 3145736 | tf_op jit(solution)/shard_map/ppermute | solution.py:260
  52.3 50.6 %collective-permute-start.11 = (s32[1024]{0:T(1024)S(1)}, s32[1024]{0:T(1024)S(1)}, u32[]{:S(2)}, u32[]{:S(2)}) collective-permute-start(s32[1024]{0:T(1024)S(1)} %bitcast.141), channel_id=1, source_target_pairs={{0,4},{1,5},{2,6},{3,7},{4,0},{5,1},{6,2},{7,3},{8,12},{9,13},{10,... | collective-permute-start | bytes 12296 | tf_op jit(solution)/shard_map/ppermute | solution.py:260
  102.9 37.2 %collective-permute-start.10 = (bf16[512,1536]{1,0:T(8,128)(2,1)}, bf16[512,1536]{1,0:T(8,128)(2,1)}, u32[]{:S(2)}, u32[]{:S(2)}) collective-permute-start(bf16[512,1536]{1,0:T(8,128)(2,1)} %get-tuple-element.113), channel_id=1, source_target_pairs={{0,8},{1,9},{2,10},{3,11},{4,12},{5,13},{6,14},{7,15},{8,0},{9,1},... | collective-permute-start | bytes 4718600 | tf_op jit(solution)/shard_map/ppermute | solution.py:260
  103.5 36.8 %collective-permute-start.9 = (bf16[512,1536]{1,0:T(8,128)(2,1)}, bf16[512,1536]{1,0:T(8,128)(2,1)}, u32[]{:S(2)}, u32[]{:S(2)}) collective-permute-start(bf16[512,1536]{1,0:T(8,128)(2,1)} %get-tuple-element.112), channel_id=1, source_target_pairs={{0,16},{1,17},{2,18},{3,19},{4,20},{5,21},{6,22},{7,23},{8,24},{9,... | collective-permute-start | bytes 4718600 | tf_op jit(solution)/shard_map/ppermute | solution.py:260
  103.9 39.6 %collective-permute-start.12 = (bf16[528,256]{1,0:T(8,128)(2,1)}, bf16[528,256]{1,0:T(8,128)(2,1)}, u32[]{:S(2)}, u32[]{:S(2)}) collective-permute-start(bf16[528,256]{1,0:T(8,128)(2,1)} %pad_maximum_fusion.22), channel_id=1, source_target_pairs={{0,2},{1,3},{2,0},{3,1},{4,6},{5,7},{6,4},{7,5},{8,10},{9,11},{10,... | collective-permute-start | bytes 811016 | tf_op jit(solution)/shard_map/ppermute | solution.py:260
  149.7 47.6 %collective-permute-start.28 = (bf16[256,2048]{1,0:T(8,128)(2,1)S(1)}, bf16[256,2048]{1,0:T(8,128)(2,1)S(1)}, u32[]{:S(2)}, u32[]{:S(2)}) collective-permute-start(bf16[256,2048]{1,0:T(8,128)(2,1)S(1)} %copy-done.33), channel_id=1, source_target_pairs={{0,2},{1,3},{2,0},{3,1},{4,6},{5,7},{6,4},{7,5},{8,10},{9,11},{10,... | collective-permute-start | bytes 3145736 | tf_op jit(solution)/shard_map/ppermute | solution.py:260
  226.0 48.3 %collective-permute-start.29 = (bf16[2048,256]{1,0:T(8,128)(2,1)S(1)}, bf16[2048,256]{1,0:T(8,128)(2,1)}, u32[]{:S(2)}, u32[]{:S(2)}) collective-permute-start(bf16[2048,256]{1,0:T(8,128)(2,1)S(1)} %copy-done.43), channel_id=1, source_target_pairs={{0,2},{1,3},{2,0},{3,1},{4,6},{5,7},{6,4},{7,5},{8,10},{9,11},{10,... | collective-permute-start | bytes 3145736 | tf_op jit(solution)/shard_map/ppermute | solution.py:260
  281.5 48.0 %collective-permute-start.34 = (bf16[512,2048]{1,0:T(8,128)(2,1)S(1)}, bf16[512,2048]{1,0:T(8,128)(2,1)S(1)}, u32[]{:S(2)}, u32[]{:S(2)}) collective-permute-start(bf16[512,2048]{1,0:T(8,128)(2,1)S(1)} %copy-done.64), channel_id=1, source_target_pairs={{0,16},{1,17},{2,18},{3,19},{4,20},{5,21},{6,22},{7,23},{8,24},{9,... | collective-permute-start | bytes 6291464 | tf_op jit(solution)/shard_map/ppermute | solution.py:260
  282.2 47.7 %collective-permute-start.35 = (bf16[512,2048]{1,0:T(8,128)(2,1)S(1)}, bf16[512,2048]{1,0:T(8,128)(2,1)S(1)}, u32[]{:S(2)}, u32[]{:S(2)}) collective-permute-start(bf16[512,2048]{1,0:T(8,128)(2,1)S(1)} %pad_maximum_fusion.10), channel_id=1, source_target_pairs={{0,8},{1,9},{2,10},{3,11},{4,12},{5,13},{6,14},{7,15},{8,0},{9,1},... | collective-permute-start | bytes 6291464 | tf_op jit(solution)/shard_map/ppermute | solution.py:260
  308.0 46.8 %collective-permute-start.24 = (bf16[256,2048]{1,0:T(8,128)(2,1)S(1)}, bf16[256,2048]{1,0:T(8,128)(2,1)S(1)}, u32[]{:S(2)}, u32[]{:S(2)}) collective-permute-start(bf16[256,2048]{1,0:T(8,128)(2,1)S(1)} %fusion.29), channel_id=1, source_target_pairs={{0,1},{1,0},{2,3},{3,2},{4,5},{5,4},{6,7},{7,6},{8,9},{9,8},{10,11... | collective-permute-start | bytes 3145736 | tf_op jit(solution)/shard_map/ppermute | solution.py:260
  309.8 52.0 %collective-permute-start.25 = (bf16[256,2048]{1,0:T(8,128)(2,1)S(1)}, bf16[256,2048]{1,0:T(8,128)(2,1)S(1)}, u32[]{:S(2)}, u32[]{:S(2)}) collective-permute-start(bf16[256,2048]{1,0:T(8,128)(2,1)S(1)} %fusion.29), channel_id=1, source_target_pairs={{0,4},{1,5},{2,6},{3,7},{4,0},{5,1},{6,2},{7,3},{8,12},{9,13},{10,... | collective-permute-start | bytes 3145736 | tf_op jit(solution)/shard_map/ppermute | solution.py:260
  333.7 52.5 %collective-permute-start.38 = (bf16[256,2048]{1,0:T(8,128)(2,1)S(1)}, bf16[256,2048]{1,0:T(8,128)(2,1)S(1)}, u32[]{:S(2)}, u32[]{:S(2)}) collective-permute-start(bf16[256,2048]{1,0:T(8,128)(2,1)S(1)} %fusion.30), channel_id=1, source_target_pairs={{0,1},{1,0},{2,3},{3,2},{4,5},{5,4},{6,7},{7,6},{8,9},{9,8},{10,11... | collective-permute-start | bytes 3145736 | tf_op jit(solution)/shard_map/ppermute | solution.py:260
  359.9 58.5 %collective-permute-start.46 = (bf16[256,2048]{1,0:T(8,128)(2,1)S(1)}, bf16[256,2048]{1,0:T(8,128)(2,1)S(1)}, u32[]{:S(2)}, u32[]{:S(2)}) collective-permute-start(bf16[256,2048]{1,0:T(8,128)(2,1)S(1)} %copy-done.71), channel_id=1, source_target_pairs={{0,2},{1,3},{2,0},{3,1},{4,6},{5,7},{6,4},{7,5},{8,10},{9,11},{10,... | collective-permute-start | bytes 3145736 | tf_op jit(solution)/shard_map/ppermute | solution.py:260
  359.9 41.6 %collective-permute-start.39 = (bf16[256,2048]{1,0:T(8,128)(2,1)S(1)}, bf16[256,2048]{1,0:T(8,128)(2,1)S(1)}, u32[]{:S(2)}, u32[]{:S(2)}) collective-permute-start(bf16[256,2048]{1,0:T(8,128)(2,1)S(1)} %fusion.30), channel_id=1, source_target_pairs={{0,4},{1,5},{2,6},{3,7},{4,0},{5,1},{6,2},{7,3},{8,12},{9,13},{10,... | collective-permute-start | bytes 3145736 | tf_op jit(solution)/shard_map/ppermute | solution.py:260
  361.8 56.6 %collective-permute-start.42 = (bf16[2048,512]{1,0:T(8,128)(2,1)S(1)}, bf16[2048,512]{1,0:T(8,128)(2,1)S(1)}, u32[]{:S(2)}, u32[]{:S(2)}) collective-permute-start(bf16[2048,512]{1,0:T(8,128)(2,1)S(1)} %constant_dynamic-update-slice_fusion.6), channel_id=1, source_target_pairs={{0,8},{1,9},{2,10},{3,11},{4,12},{5,13},{6,14},{7,15},{8,0},{9,1},... | collective-permute-start | bytes 6291464 | tf_op jit(solution)/shard_map/ppermute | solution.py:260
  362.3 56.1 %collective-permute-start.41 = (bf16[2048,512]{1,0:T(8,128)(2,1)S(1)}, bf16[2048,512]{1,0:T(8,128)(2,1)S(1)}, u32[]{:S(2)}, u32[]{:S(2)}) collective-permute-start(bf16[2048,512]{1,0:T(8,128)(2,1)S(1)} %get-tuple-element.284), channel_id=1, source_target_pairs={{0,16},{1,17},{2,18},{3,19},{4,20},{5,21},{6,22},{7,23},{8,24},{9,... | collective-permute-start | bytes 6291464 | tf_op jit(solution)/shard_map/ppermute | solution.py:260
  463.2 36.5 %collective-permute-start.48 = (bf16[256,2048]{1,0:T(8,128)(2,1)S(1)}, bf16[256,2048]{1,0:T(8,128)(2,1)S(1)}, u32[]{:S(2)}, u32[]{:S(2)}) collective-permute-start(bf16[256,2048]{1,0:T(8,128)(2,1)S(1)} %slice.498), channel_id=1, source_target_pairs={{0,1},{1,0},{2,3},{3,2},{4,5},{5,4},{6,7},{7,6},{8,9},{9,8},{10,11... | collective-permute-start | bytes 3145736 | tf_op jit(solution)/shard_map/ppermute | solution.py:260
  482.2 39.6 %collective-permute-start.51 = (bf16[256,2048]{1,0:T(8,128)(2,1)S(1)}, bf16[256,2048]{1,0:T(8,128)(2,1)}, u32[]{:S(2)}, u32[]{:S(2)}) collective-permute-start(bf16[256,2048]{1,0:T(8,128)(2,1)S(1)} %get-tuple-element.269), channel_id=1, source_target_pairs={{0,1},{1,0},{2,3},{3,2},{4,5},{5,4},{6,7},{7,6},{8,9},{9,8},{10,11... | collective-permute-start | bytes 3145736 | tf_op jit(solution)/shard_map/ppermute | solution.py:260
  556.8 49.3 %collective-permute-start.50 = (bf16[256,2048]{1,0:T(8,128)(2,1)}, bf16[256,2048]{1,0:T(8,128)(2,1)}, u32[]{:S(2)}, u32[]{:S(2)}) collective-permute-start(bf16[256,2048]{1,0:T(8,128)(2,1)} %get-tuple-element.261), channel_id=1, source_target_pairs={{0,2},{1,3},{2,0},{3,1},{4,6},{5,7},{6,4},{7,5},{8,10},{9,11},{10,... | collective-permute-start | bytes 3145736 | tf_op jit(solution)/shard_map/ppermute | solution.py:260
  601.2 48.0 %collective-permute-start.63 = (bf16[2048,512]{1,0:T(8,128)(2,1)}, bf16[2048,512]{1,0:T(8,128)(2,1)}, u32[]{:S(2)}, u32[]{:S(2)}) collective-permute-start(bf16[2048,512]{1,0:T(8,128)(2,1)} %get-tuple-element.255), channel_id=1, source_target_pairs={{0,16},{1,17},{2,18},{3,19},{4,20},{5,21},{6,22},{7,23},{8,24},{9,... | collective-permute-start | bytes 6291464 | tf_op jit(solution)/shard_map/ppermute | solution.py:260
  602.9 47.7 %collective-permute-start.64 = (bf16[2048,512]{1,0:T(8,128)(2,1)}, bf16[2048,512]{1,0:T(8,128)(2,1)}, u32[]{:S(2)}, u32[]{:S(2)}) collective-permute-start(bf16[2048,512]{1,0:T(8,128)(2,1)} %get-tuple-element.254), channel_id=1, source_target_pairs={{0,8},{1,9},{2,10},{3,11},{4,12},{5,13},{6,14},{7,15},{8,0},{9,1},... | collective-permute-start | bytes 6291464 | tf_op jit(solution)/shard_map/ppermute | solution.py:260
  644.5 49.7 %collective-permute-start.59 = (bf16[256,2048]{1,0:T(8,128)(2,1)S(1)}, bf16[256,2048]{1,0:T(8,128)(2,1)}, u32[]{:S(2)}, u32[]{:S(2)}) collective-permute-start(bf16[256,2048]{1,0:T(8,128)(2,1)S(1)} %get-tuple-element.235), channel_id=1, source_target_pairs={{0,1},{1,0},{2,3},{3,2},{4,5},{5,4},{6,7},{7,6},{8,9},{9,8},{10,11... | collective-permute-start | bytes 3145736 | tf_op jit(solution)/shard_map/ppermute | solution.py:260
  645.9 59.1 %collective-permute-start.60 = (bf16[256,2048]{1,0:T(8,128)(2,1)S(1)}, bf16[256,2048]{1,0:T(8,128)(2,1)}, u32[]{:S(2)}, u32[]{:S(2)}) collective-permute-start(bf16[256,2048]{1,0:T(8,128)(2,1)S(1)} %get-tuple-element.235), channel_id=1, source_target_pairs={{0,4},{1,5},{2,6},{3,7},{4,0},{5,1},{6,2},{7,3},{8,12},{9,13},{10,... | collective-permute-start | bytes 3145736 | tf_op jit(solution)/shard_map/ppermute | solution.py:260
  694.2 46.9 %collective-permute-start.72 = (bf16[512,2048]{1,0:T(8,128)(2,1)}, bf16[512,2048]{1,0:T(8,128)(2,1)}, u32[]{:S(2)}, u32[]{:S(2)}) collective-permute-start(bf16[512,2048]{1,0:T(8,128)(2,1)} %get-tuple-element.251), channel_id=1, source_target_pairs={{0,16},{1,17},{2,18},{3,19},{4,20},{5,21},{6,22},{7,23},{8,24},{9,... | collective-permute-start | bytes 6291464 | tf_op jit(solution)/shard_map/ppermute | solution.py:260
  695.9 45.8 %collective-permute-start.73 = (bf16[512,2048]{1,0:T(8,128)(2,1)}, bf16[512,2048]{1,0:T(8,128)(2,1)}, u32[]{:S(2)}, u32[]{:S(2)}) collective-permute-start(bf16[512,2048]{1,0:T(8,128)(2,1)} %get-tuple-element.250), channel_id=1, source_target_pairs={{0,8},{1,9},{2,10},{3,11},{4,12},{5,13},{6,14},{7,15},{8,0},{9,1},... | collective-permute-start | bytes 6291464 | tf_op jit(solution)/shard_map/ppermute | solution.py:260
  762.9 64.9 %collective-permute-start.81 = (bf16[2048,256]{1,0:T(8,128)(2,1)}, bf16[2048,256]{1,0:T(8,128)(2,1)}, u32[]{:S(2)}, u32[]{:S(2)}) collective-permute-start(bf16[2048,256]{1,0:T(8,128)(2,1)} %get-tuple-element.279), channel_id=1, source_target_pairs={{0,2},{1,3},{2,0},{3,1},{4,6},{5,7},{6,4},{7,5},{8,10},{9,11},{10,... | collective-permute-start | bytes 3145736 | tf_op jit(solution)/shard_map/ppermute | solution.py:260
  798.1 40.1 %collective-permute-start.75 = (bf16[256,2048]{1,0:T(8,128)(2,1)}, bf16[256,2048]{1,0:T(8,128)(2,1)}, u32[]{:S(2)}, u32[]{:S(2)}) collective-permute-start(bf16[256,2048]{1,0:T(8,128)(2,1)} %slice.495), channel_id=1, source_target_pairs={{0,1},{1,0},{2,3},{3,2},{4,5},{5,4},{6,7},{7,6},{8,9},{9,8},{10,11... | collective-permute-start | bytes 3145736 | tf_op jit(solution)/shard_map/ppermute | solution.py:260
  864.2 48.0 %collective-permute-start.86 = (bf16[256,2048]{1,0:T(8,128)(2,1)}, bf16[256,2048]{1,0:T(8,128)(2,1)S(1)}, u32[]{:S(2)}, u32[]{:S(2)}) collective-permute-start(bf16[256,2048]{1,0:T(8,128)(2,1)} %get-tuple-element.277), channel_id=1, source_target_pairs={{0,2},{1,3},{2,0},{3,1},{4,6},{5,7},{6,4},{7,5},{8,10},{9,11},{10,... | collective-permute-start | bytes 3145736 | tf_op jit(solution)/shard_map/ppermute | solution.py:260
  967.0 36.2 %collective-permute-start.98 = (bf16[528,256]{1,0:T(8,128)(2,1)S(1)}, bf16[528,256]{1,0:T(8,128)(2,1)S(1)}, u32[]{:S(2)}, u32[]{:S(2)}) collective-permute-start(bf16[528,256]{1,0:T(8,128)(2,1)S(1)} %copy-done.78), channel_id=1, source_target_pairs={{0,2},{1,3},{2,0},{3,1},{4,6},{5,7},{6,4},{7,5},{8,10},{9,11},{10,... | collective-permute-start | bytes 811016 | tf_op jit(solution)/shard_map/ppermute | solution.py:260
  970.4 72.1 %collective-permute-start.91 = (bf16[256,2048]{1,0:T(8,128)(2,1)S(1)}, bf16[256,2048]{1,0:T(8,128)(2,1)S(1)}, u32[]{:S(2)}, u32[]{:S(2)}) collective-permute-start(bf16[256,2048]{1,0:T(8,128)(2,1)S(1)} %broadcast_select_fusion.8), channel_id=1, source_target_pairs={{0,2},{1,3},{2,0},{3,1},{4,6},{5,7},{6,4},{7,5},{8,10},{9,11},{10,... | collective-permute-start | bytes 3145736 | tf_op jit(solution)/shard_map/ppermute | solution.py:260
  1005.0 54.3 %collective-permute-start.97 = (bf16[256,1536]{1,0:T(8,128)(2,1)S(1)}, bf16[256,1536]{1,0:T(8,128)(2,1)S(1)}, u32[]{:S(2)}, u32[]{:S(2)}) collective-permute-start(bf16[256,1536]{1,0:T(8,128)(2,1)S(1)} %broadcast_select_fusion.22), channel_id=1, source_target_pairs={{0,2},{1,3},{2,0},{3,1},{4,6},{5,7},{6,4},{7,5},{8,10},{9,11},{10,... | collective-permute-start | bytes 2359304 | tf_op jit(solution)/shard_map/ppermute | solution.py:260
  (177 other events, 2619.4 us)

commit v4 on v3

--- a/solution.py
+++ b/solution.py
@@ -269,16 +269,16 @@
         got = swap(jnp.where(same, other, shard), core_bit)
         return [jnp.where(same, shard, got), jnp.where(same, got, other)]
 
-    def moved(parts, step):
+    def moved(parts, step, pair=True):
         got = [swap(v, order[step] * 2 * tensor_size) for v, order in zip(parts, orders)]
-        return list(lax.optimization_barrier(tuple(got)))
+        return list(lax.optimization_barrier(tuple(got))) if pair else got
 
     def joined(parts, got, axis):
         return [jnp.concatenate([v, w], axis=axis) for v, w in zip(parts, got)]
 
-    def doubled(parts, axis, begin, end):
+    def doubled(parts, axis, begin, end, pair=True):
         for step in range(begin, end):
-            parts = joined(parts, moved(parts, step), axis)
+            parts = joined(parts, moved(parts, step, pair), axis)
         return parts
 
     def tied(parts, *others):
@@ -287,12 +287,13 @@
     last = len(p_bits) - 1
 
 
-    def split_send(parts, step, axis):
+    def split_send(parts, step, axis, pair=True):
         halves_of = [jnp.split(v, 2, axis=axis) for v in parts]
         got = [
             swap(v[1], order[step] * 2 * tensor_size) for v, order in zip(halves_of, orders)
         ]
-        return [v[0] for v in halves_of], list(lax.optimization_barrier(tuple(got)))
+        got = list(lax.optimization_barrier(tuple(got))) if pair else got
+        return [v[0] for v in halves_of], got
 
     def added(kept, got):
         return [(v.astype(F32) + w.astype(F32)).astype(BF16) for v, w in zip(kept, got)]
@@ -370,6 +371,13 @@
         return jnp.stack([jnp.where(h == 0, kept, got), jnp.where(h == 0, got, kept)])
 
     streams = range(2)
+    pair_q = False
+    pair_o = True
+    pair_e = True
+    pair_c = False
+    send_c = True
+    send_e = False
+    send_o = False
     extra = 16
     qkv_shard = jnp.stack(
         [w.reshape(-1, heads, DH) for w in (query_weight, key_weight, value_weight)], axis=2
@@ -381,7 +389,7 @@
     qkv_other = swap(qkv_shard, half_bit)
     token_own, token_send = parted(tokens)
     token_other = swap(after(token_send, qkv_other), half_bit)
-    qkv_parts = doubled(near(qkv_shard, qkv_other), 0, 0, 1)
+    qkv_parts = doubled(near(qkv_shard, qkv_other), 0, 0, 1, pair_q)
     token_other = after(token_other, *qkv_parts)
     qkv_parts = tied(qkv_parts, token_other)
     output_other = swap(after(output_shard, token_other), half_bit)
@@ -389,11 +397,11 @@
     homes, _ = to_home(token_own, token_other)
     sent = [gather_far(homes[0])]
     sent.append(gather_far(after(homes[1], *sent[0])))
-    qkv_parts = doubled(qkv_parts, 0, 1, last)
-    qkv_got = moved(qkv_parts, last)
+    qkv_parts = doubled(qkv_parts, 0, 1, last, pair_q)
+    qkv_got = moved(qkv_parts, last, pair_q)
     full_qkv = jnp.concatenate([qkv_parts[0], qkv_got[0], qkv_parts[1], qkv_got[1]], axis=0)
     output_other = after(output_other, full_qkv, sent[0][-1])
-    output_parts = doubled(near(output_shard, output_other), 1, 0, last + 1)
+    output_parts = doubled(near(output_shard, output_other), 1, 0, last + 1, pair_o)
     segs = [segments_of(j) for j in streams]
 
     rows = [gather_near(sent[0])]
@@ -406,14 +414,15 @@
     partial = [reduce_near(dot_nn(context[0], full_output))]
     attended = [reduce_far(partial[0])]
     contract_other = swap(after(contract_weight, expand_other), half_bit)
-    expand_parts = doubled(near(expand_weight, expand_other), 0, 0, last)
-    sent1 = tied(sent[1], partial[0])
+    expand_other = after(expand_other, context[0])
+    expand_parts = doubled(near(expand_weight, expand_other), 0, 0, last, pair_e)
+    sent1 = tied(sent[1], context[0])
     pre = ()
     rows.append(after(gather_near(sent1), partial[0], *pre))
     qkv.append(dot_nn(rows[1], full_qkv).astype(BF16))
     pre = ()
     context.append(attention_forward(after(qkv[1], *pre), *segs[1]))
-    expand_got = moved(tied(expand_parts, context[1]), last)
+    expand_got = moved(tied(expand_parts, context[1]), last, pair_e)
 
     pre = ()
     partial.append(reduce_near(dot_nn(after(context[1], *pre), full_output)))
@@ -423,23 +432,22 @@
     normed = [first[0][0].astype(BF16)]
     sent = [gather_far(normed[0])]
     contract_other = after(contract_other, context[1])
-    pre = (contract_other, normed[0])
+    pre = (normed[0],)
     first.append(
         norm_forward(homes[1].astype(F32) + ready(attended[1], *pre), gains[0], shifts[0])
     )
     normed.append(first[1][0].astype(BF16))
     sent.append(gather_far(normed[1]))
     cotangent_own, cotangent_send = parted(cotangent)
-    cotangent_other = swap(after(cotangent_send, contract_other), half_bit)
     contract_parts = near(contract_weight, contract_other)
     expand_got = tied(expand_got, normed[1])
     full_expand = jnp.concatenate(
         [expand_parts[0], expand_got[0], expand_parts[1], expand_got[1]], axis=0
     )
-    contract_parts = doubled(tied(contract_parts, *expand_got), 1, 0, last)
+    contract_parts = doubled(tied(contract_parts, *expand_got), 1, 0, last, pair_c)
     normed_rows, active, slope, branch = [], [], [], []
     gate = tuple(contract_parts)
-    contract_got = moved(contract_parts, last)
+    contract_got = moved(contract_parts, last, pair_c)
 
     def feed(j, *gate):
         normed_rows.append(after(gather_near(sent[j]), *gate))
@@ -448,6 +456,7 @@
         slope.append(derivative.astype(BF16))
 
     feed(0, normed[1], *gate)
+    cotangent_other = swap(after(cotangent_send, contract_other, active[0]), half_bit)
     feed(1, active[0])
     contract_got = tied(contract_got, active[1])
     full_contract = jnp.concatenate(
@@ -457,14 +466,14 @@
     branch.append(dot_nn(after(active[0], gate), full_contract).astype(BF16))
     partial = [reduce_near(branch[0])]
     pairs = [reduce_far(partial[0])]
-    grads_home, grads_all = to_home(cotangent_own, after(cotangent_other, active[1]))
+    grads_home, grads_all = to_home(cotangent_own, cotangent_other)
     gate = (branch[0],)
     branch.append(dot_nn(after(active[1], *gate), full_contract).astype(BF16))
     partial.append(reduce_near(branch[1]))
     pairs.append(reduce_far(partial[1]))
 
     second, branch_grad, sent = [], [], []
-    gate = (partial[1], grads_all)
+    gate = (branch[1], grads_all)
     for j in streams:
         second.append(norm_forward(first[j][0] + ready(pairs[j], *gate), gains[1], shifts[1]))
         branch_grad.append(
@@ -472,6 +481,8 @@
         )
         gate = (branch_grad[j][0].astype(BF16),)
         sent.append(gather_far(gate[0]))
+        if j == 0:
+            gate = ()
     result_kept, result_got = sent_home([second[j][0].astype(BF16) for j in streams])
     branch_rows, hidden_grad, normed_part = [], [], []
     partial, pairs = [], []
@@ -493,20 +504,20 @@
             result_got = after(result_got, partial[0])
             gate = (contract_grad,)
             gate = (*gate, result_got)
-    contract_kept, contract_got = split_send(jnp.split(contract_grad, 2, axis=1), last, 1)
+    contract_kept, contract_got = split_send(jnp.split(contract_grad, 2, axis=1), last, 1, send_c)
     result = home_pair(result_kept, result_got)
     normed_grad = [branch_grad[0][0] + ready(pairs[0], contract_grad)]
     first_grad = [norm_backward(normed_grad[0], first[0][1], first[0][2], gains[0])]
     gate = first_grad[0][0].astype(BF16)
     sent = [gather_far(gate)]
-    expand_grad = dot_tn(after(normed_rows[0], gate, partial[1]), hidden_grad[0])
+    expand_grad = dot_tn(after(normed_rows[0], gate, normed_part[1]), hidden_grad[0])
     contract_sum = added(contract_kept, tied(contract_got, partial[1]))
     pre = tuple(contract_sum)
     expand_grad = expand_grad + dot_tn(after(normed_rows[1], *pre), hidden_grad[1])
     expand_grad = expand_grad.astype(BF16)
-    contract_kept, contract_got = split_send(contract_sum, last - 1, 1)
+    contract_kept, contract_got = split_send(contract_sum, last - 1, 1, send_c)
     expand_kept = jnp.split(expand_grad, 2, axis=0)
-    expand_kept, expand_got = split_send(expand_kept, last, 0)
+    expand_kept, expand_got = split_send(expand_kept, last, 0, send_e)
     normed_grad.append(branch_grad[1][0] + ready(pairs[1], expand_grad))
     first_grad.append(norm_backward(normed_grad[1], first[1][1], first[1][2], gains[0]))
     gate = first_grad[1][0].astype(BF16)
@@ -529,7 +540,7 @@
     qkv_grad = [attention_backward(qkv[0], context_grad, *segs[0])]
     attended_rows.append(gather_near(tied(sent[1], qkv_grad[0])))
     expand_sum = added(expand_kept, tied(expand_got, qkv_grad[0]))
-    expand_kept, expand_got = split_send(expand_sum, last - 1, 0)
+    expand_kept, expand_got = split_send(expand_sum, last - 1, 0, send_e)
     pre = tuple(expand_sum)
     tied_grad = after(qkv_grad[0], attended_rows[1], *pre)
     token_part = dot_nt(tied_grad, full_qkv).astype(BF16)
@@ -543,7 +554,7 @@
     output_grad = dot_tn(after(context[0], partial[0], *pre), attended_rows[0])
     output_grad = output_grad + dot_tn(context[1], attended_rows[1])
     output_grad = jnp.concatenate([output_grad, terms], axis=0).astype(BF16)
-    output_kept, output_got = split_send(jnp.split(output_grad, 2, axis=1), last, 1)
+    output_kept, output_got = split_send(jnp.split(output_grad, 2, axis=1), last, 1, send_o)
     pre = ()
     context_grad = dot_nt(after(attended_rows[1], output_grad, *pre), full_output)
     qkv_grad.append(attention_backward(qkv[1], context_grad.astype(BF16), *segs[1]))
@@ -551,7 +562,7 @@
         added(expand_kept, tied(expand_got, qkv_grad[1])), 0, last - 2
     )
     output_sum = added(output_kept, tied(output_got, qkv_grad[1]))
-    output_kept, output_got = split_send(output_sum, last - 1, 1)
+    output_kept, output_got = split_send(output_sum, last - 1, 1, send_o)
     token_sums = [(first_grad[0][0] + ready(pairs[0], qkv_grad[1])).astype(BF16)]
     contract_got = after(contract_got, qkv_grad[1])
     pre = (contract_got,)
@@ -570,14 +581,11 @@
         parts.append((part + dot_tn(rows[1][:, columns], qkv_grad[1])).astype(BF16))
         if i == 0:
             gate = (parts[0],)
-            expand_got = after(expand_got, parts[0])
-            gate = (*gate, expand_got)
-            output_got = tied(output_got, parts[0])
-            output_kept, output_got = reduce_rest(added(output_kept, output_got), 1, last - 2)
-            gate = (*gate, output_kept)
-    pre = (parts[1],)
+    expand_got = after(expand_got, parts[1])
+    pre = (parts[1], expand_got)
     token_sums.append((first_grad[1][0] + ready(pairs[1], *pre)).astype(BF16))
     tokens_kept, tokens_got = sent_home(token_sums)
+    output_kept, output_got = reduce_rest(added(output_kept, output_got), 1, last - 2)
     output_got = after(output_got, token_sums[1])
     output_grad = total_of(output_kept, output_got)
     tokens_grad = home_pair(tokens_kept, tokens_got).astype(F32)

time: 1070 us -> 1030 us (0.963)
  waiting for transfers between devices: 467 us -> 398 us
  local copies, waits for them, and re-layouts: 71.3 us -> 83.8 us
    ppermute x99, waiting for transfers between devices: 467 us -> 398 us  [swap(): return lax.ppermute(array, AXES, [(i, i ^ mask) for i in range(total)])]
    unnamed x242 -> x246, local copies, waits for them, and re-layouts: 37.8 us -> 43.3 us
  transfers between devices with their start and end apart: 99 -> 99, of which waited for: 49 -> 36; matrix products, arithmetic and copies ran while one was open for 35% -> 39% of each run, Pallas kernels for 8% -> 9%
where the time goes in v4:
time: 1030 us
  waiting for transfers between devices  398 us (39%)
  matrix products  254 us (25%)
  other arithmetic  126 us (12%)
  Pallas kernels  88.5 us (9%)
  local copies, waits for them, and re-layouts  83.8 us (8%)
  starting transfers between devices  71.6 us (7%)
    ppermute x99, waiting for transfers between devices, swap(): return lax.ppermute(array, AXES, [(i, i ^ mask) for i in range(total)])  398 us
    dot_general x10, matrix products, dot_tn(): lax.dot_general(left, right, (((0,), (0,)), ((), ())), preferred_element_...  86.5 us
    dot_general x8, matrix products, dot_nt(): lax.dot_general(left, right, (((1,), (1,)), ((), ())), preferred_element_...  85.6 us
    dot_general x8, matrix products, dot_nn(): return jnp.dot(left, right, preferred_element_type=F32)  82.1 us
    ppermute x99, starting transfers between devices, swap(): return lax.ppermute(array, AXES, [(i, i ^ mask) for i in range(total)])  71.6 us
    pallas_call x2, Pallas kernels, attention_backward(): pl.pallas_call(functools.partial(attention_backward_kernel, block=min(256...  46.4 us
    unnamed x246, local copies, waits for them, and re-layouts  43.3 us
    pallas_call x2, Pallas kernels, attention_forward(): pl.pallas_call(functools.partial(attention_forward_kernel, block=min(256,...  23.6 us
  transfers between devices with their start and end apart: 99, of which 36 were waited for; matrix products, arithmetic and copies ran while one was open for 39% of the time, Pallas kernels for 9%

profile of v4, /device:TPU:0, one launch (start us, length us, event | category | flops | bytes accessed | tf_op | source)
XLA Modules:
  0.0 1025.2 jit_solution(17390566894984470832)
XLA Ops:
  8.4 34.5 %collective-permute-done = bf16[256,1536]{1,0:T(8,128)(2,1)} collective-permute-done((bf16[256,1536]{1,0:T(8,128)(2,1)S(1)}, bf16[256,1536]{1,0:T(8,128)(2,1)}, u32[]{:S(2)}, u32[]{:S(2)}) %collective-permute-start) | collective-permute-done | bytes 786464 | tf_op jit(solution)/shard_map/ppermute | solution.py:260
  52.4 16.4 %collective-permute-done.4 = bf16[256,1536]{1,0:T(8,128)(2,1)S(1)} collective-permute-done((bf16[256,1536]{1,0:T(8,128)(2,1)S(1)}, bf16[256,1536]{1,0:T(8,128)(2,1)S(1)}, u32[]{:S(2)}, u32[]{:S(2)}) %collective-permute-start.4) | collective-permute-done | bytes 786464 | tf_op jit(solution)/shard_map/ppermute | solution.py:260
  71.3 29.1 %collective-permute-done.1 = bf16[256,2048]{1,0:T(8,128)(2,1)S(1)} collective-permute-done((bf16[256,2048]{1,0:T(8,128)(2,1)S(1)}, bf16[256,2048]{1,0:T(8,128)(2,1)S(1)}, u32[]{:S(2)}, u32[]{:S(2)}) %collective-permute-start.1) | collective-permute-done | bytes 1048608 | tf_op jit(solution)/shard_map/ppermute | solution.py:260
  116.8 23.3 %collective-permute-done.9 = bf16[512,1536]{1,0:T(8,128)(2,1)} collective-permute-done((bf16[512,1536]{1,0:T(8,128)(2,1)}, bf16[512,1536]{1,0:T(8,128)(2,1)}, u32[]{:S(2)}, u32[]{:S(2)}) %collective-permute-start.9) | collective-permute-done | bytes 1572896 | tf_op jit(solution)/shard_map/ppermute | solution.py:260
  159.8 12.5 %convolution_convert_fusion.3.qkv_ref = bf16[1024,1536]{1,0:T(8,128)(2,1)} fusion(bf16[2048,1536]{1,0:T(8,128)(2,1)} %copy-done.82, bf16[256,2048]{1,0:T(8,128)(2,1)} %collective-permute-done.8, bf16[256,2048]{1,0:T(8,128)(2,1)} %collective-permute-done.7, bf16[256,2048]{1,0:T(8,128)(2,1)} %collective-permute-done.6, bf16[256,2048]{1,0:T(8,128)(2,1)} %get-tuple-element.238), kind=kOutput, calls=%fused_computation.39 | convolution fusion | flops 6460801024 | bytes 13631488 | tf_op jit(solution)/shard_map/dot_general | solution.py:20
  172.3 11.8 %attention_forward.2 = bf16[1024,512]{1,0:T(8,128)(2,1)} custom-call(bf16[1024,1536]{1,0:T(8,128)(2,1)} %convolution_convert_fusion.3.qkv_ref, s32[1024,1]{1,0:T(8,128)} %copy.30.seg_col_ref, s32[1,1024]{1,0:T(1,128)} %bitcast.125), custom_call_target="tpu_custom_call" | custom-call | flops 65536 | bytes 65536 | tf_op jit(solution)/shard_map/attention_forward/pallas_call | solution.py:82
  184.0 13.1 %collective-permute-done.28 = bf16[256,2048]{1,0:T(8,128)(2,1)S(1)} collective-permute-done((bf16[256,2048]{1,0:T(8,128)(2,1)S(1)}, bf16[256,2048]{1,0:T(8,128)(2,1)S(1)}, u32[]{:S(2)}, u32[]{:S(2)}) %collective-permute-start.28) | collective-permute-done | bytes 1048608 | tf_op jit(solution)/shard_map/ppermute | solution.py:260
  233.1 11.8 %attention_forward.3 = bf16[1024,512]{1,0:T(8,128)(2,1)} custom-call(bf16[1024,1536]{1,0:T(8,128)(2,1)} %convolution_convert_fusion.2.qkv_ref, s32[1024,1]{1,0:T(8,128)} %copy.31.seg_col_ref, s32[1,1024]{1,0:T(1,128)} %bitcast.122), custom_call_target="tpu_custom_call" | custom-call | flops 65536 | bytes 65536 | tf_op jit(solution)/shard_map/attention_forward/pallas_call | solution.py:82
  268.4 20.2 %collective-permute-done.19 = bf16[256,2048]{1,0:T(8,128)(2,1)S(1)} collective-permute-done((bf16[256,2048]{1,0:T(8,128)(2,1)S(1)}, bf16[256,2048]{1,0:T(8,128)(2,1)S(1)}, u32[]{:S(2)}, u32[]{:S(2)}) %collective-permute-start.19) | collective-permute-done | bytes 1048608 | tf_op jit(solution)/shard_map/ppermute | solution.py:260
  292.1 19.0 %collective-permute-done.34 = bf16[512,2048]{1,0:T(8,128)(2,1)S(1)} collective-permute-done((bf16[512,2048]{1,0:T(8,128)(2,1)S(1)}, bf16[512,2048]{1,0:T(8,128)(2,1)S(1)}, u32[]{:S(2)}, u32[]{:S(2)}) %collective-permute-start.34) | collective-permute-done | bytes 2097184 | tf_op jit(solution)/shard_map/ppermute | solution.py:260
  321.7 15.4 %collective-permute-done.24 = bf16[256,2048]{1,0:T(8,128)(2,1)S(1)} collective-permute-done((bf16[256,2048]{1,0:T(8,128)(2,1)S(1)}, bf16[256,2048]{1,0:T(8,128)(2,1)S(1)}, u32[]{:S(2)}, u32[]{:S(2)}) %collective-permute-start.24) | collective-permute-done | bytes 1048608 | tf_op jit(solution)/shard_map/ppermute | solution.py:260
  346.2 12.0 %collective-permute-done.38 = bf16[256,2048]{1,0:T(8,128)(2,1)S(1)} collective-permute-done((bf16[256,2048]{1,0:T(8,128)(2,1)S(1)}, bf16[256,2048]{1,0:T(8,128)(2,1)S(1)}, u32[]{:S(2)}, u32[]{:S(2)}) %collective-permute-start.38) | collective-permute-done | bytes 1048608 | tf_op jit(solution)/shard_map/ppermute | solution.py:260
  358.2 15.4 %multiply_convert_fusion.3 = (bf16[1024,2048]{1,0:T(8,128)(2,1)}, f32[1024,2048]{1,0:T(8,128)}) fusion(bf16[1024,2048]{1,0:T(8,128)(2,1)S(1)} %pad_maximum_fusion.2, bf16[2048,2048]{1,0:T(8,128)(2,1)} %constant_dynamic-update-slice_fusion.8), kind=kOutput, calls=%fused_computation.9 | convolution fusion | flops 8608808960 | bytes 25165824 | tf_op jit(solution)/shard_map/dot_general | solution.py:20
  376.1 16.7 %multiply_convert_fusion.2 = (bf16[1024,2048]{1,0:T(8,128)(2,1)}, f32[1024,2048]{1,0:T(8,128)}) fusion(bf16[1024,2048]{1,0:T(8,128)(2,1)S(1)} %pad_maximum_fusion.3, bf16[2048,2048]{1,0:T(8,128)(2,1)} %constant_dynamic-update-slice_fusion.8), kind=kOutput, calls=%fused_computation.6 | convolution fusion | flops 8608808960 | bytes 25165824 | tf_op jit(solution)/shard_map/dot_general | solution.py:20
  437.0 15.2 %collective-permute-done.44 = bf16[256,2048]{1,0:T(8,128)(2,1)S(1)} collective-permute-done((bf16[256,2048]{1,0:T(8,128)(2,1)}, bf16[256,2048]{1,0:T(8,128)(2,1)S(1)}, u32[]{:S(2)}, u32[]{:S(2)}) %collective-permute-start.44) | collective-permute-done | bytes 1048608 | tf_op jit(solution)/shard_map/ppermute | solution.py:260
  452.2 21.9 %collective-permute-done.48 = bf16[256,2048]{1,0:T(8,128)(2,1)} collective-permute-done((bf16[256,2048]{1,0:T(8,128)(2,1)}, bf16[256,2048]{1,0:T(8,128)(2,1)}, u32[]{:S(2)}, u32[]{:S(2)}) %collective-permute-start.48) | collective-permute-done | bytes 1048608 | tf_op jit(solution)/shard_map/ppermute | solution.py:260
  496.7 14.8 %collective-permute-done.51 = bf16[256,2048]{1,0:T(8,128)(2,1)} collective-permute-done((bf16[256,2048]{1,0:T(8,128)(2,1)}, bf16[256,2048]{1,0:T(8,128)(2,1)}, u32[]{:S(2)}, u32[]{:S(2)}) %collective-permute-start.51) | collective-permute-done | bytes 1048608 | tf_op jit(solution)/shard_map/ppermute | solution.py:260
  516.4 16.7 %multiply_convert_fusion.1 = bf16[1024,2048]{1,0:T(8,128)(2,1)S(1)} fusion(bf16[1024,2048]{1,0:T(8,128)(2,1)S(1)} %pad_maximum_fusion.4, bf16[2048,2048]{1,0:T(8,128)(2,1)} %constant_dynamic-update-slice_fusion.14, f32[1024,2048]{1,0:T(8,128)} %get-tuple-element.281), kind=kOutput, calls=%fused_computation.4 | convolution fusion | flops 8631877632 | bytes 25165824 | tf_op jit(solution)/shard_map/dot_general | solution.py:28
  533.2 13.0 %convolution_convert_fusion.5 = bf16[1024,2048]{1,0:T(8,128)(2,1)S(1)} fusion(bf16[1024,2048]{1,0:T(8,128)(2,1)S(1)} %multiply_convert_fusion.1, bf16[2048,2048]{1,0:T(8,128)(2,1)} %constant_dynamic-update-slice_fusion.8), kind=kOutput, calls=%fused_computation.41 | convolution fusion | flops 8592031744 | bytes 16777216 | tf_op jit(solution)/shard_map/dot_general | solution.py:28
  559.5 11.9 %fusion.69 = f32[2048,2048]{1,0:T(8,128)} fusion(bf16[1024,2048]{1,0:T(8,128)(2,1)S(1)} %copy-done.106, bf16[1024,2048]{1,0:T(8,128)(2,1)S(1)} %pad_maximum_fusion.4), kind=kOutput, calls=%fused_computation.310 | convolution fusion | flops 8589934592 | bytes 25165824 | tf_op jit(solution)/shard_map/dot_general | solution.py:24
  571.4 16.4 %add_convert_fusion.1 = bf16[2048,2048]{1,0:T(8,128)(2,1)} fusion(f32[2048,2048]{1,0:T(8,128)} %fusion.69, bf16[1024,2048]{1,0:T(8,128)(2,1)} %get-tuple-element.124, bf16[256,2048]{1,0:T(8,128)(2,1)} %copy-done.81, bf16[256,2048]{1,0:T(8,128)(2,1)} %copy-done.80, bf16[256,2048]{1,0:T(8,128)(2,1)} %copy-done.79, bf16[256,2048]{1,0:T(8,128)(2,1)S(1)} %get-tuple-element.235), kind=kOutput, calls=%fused_computation.1 | convolution fusion | flops 8615100416 | bytes 33554432 | tf_op jit(solution)/shard_map/dot_general | solution.py:24
  597.6 18.5 %multiply_convert_fusion = bf16[1024,2048]{1,0:T(8,128)(2,1)} fusion(bf16[1024,2048]{1,0:T(8,128)(2,1)S(1)} %copy-done.39, bf16[2048,2048]{1,0:T(8,128)(2,1)} %constant_dynamic-update-slice_fusion.14, f32[1024,2048]{1,0:T(8,128)} %get-tuple-element.283), kind=kOutput, calls=%fused_computation.2 | convolution fusion | flops 8631877632 | bytes 25165824 | tf_op jit(solution)/shard_map/dot_general | solution.py:28
  616.1 12.9 %convolution_convert_fusion.4 = bf16[1024,2048]{1,0:T(8,128)(2,1)S(1)} fusion(bf16[1024,2048]{1,0:T(8,128)(2,1)} %multiply_convert_fusion, bf16[2048,2048]{1,0:T(8,128)(2,1)} %constant_dynamic-update-slice_fusion.8), kind=kOutput, calls=%fused_computation.40 | convolution fusion | flops 8592031744 | bytes 16777216 | tf_op jit(solution)/shard_map/dot_general | solution.py:28
  636.2 14.6 %fusion.70 = f32[2048,2048]{1,0:T(8,128)} fusion(bf16[1024,2048]{1,0:T(8,128)(2,1)S(1)} %copy-done.38, bf16[1024,2048]{1,0:T(8,128)(2,1)} %copy-done.107), kind=kOutput, calls=%fused_computation.311 | convolution fusion | flops 8589934592 | bytes 25165824 | tf_op jit(solution)/shard_map/dot_general | solution.py:24
  664.3 16.5 %add_convert_fusion = bf16[2048,2048]{1,0:T(8,128)(2,1)} fusion(f32[2048,2048]{1,0:T(8,128)} %fusion.70, bf16[1024,2048]{1,0:T(8,128)(2,1)} %copy-done.36, bf16[1024,2048]{1,0:T(8,128)(2,1)} %multiply_convert_fusion), kind=kOutput, calls=%fused_computation | convolution fusion | flops 8598323200 | bytes 33554432 | tf_op jit(solution)/shard_map/dot_general | solution.py:24
  706.7 23.0 %attention_backward.2 = bf16[1024,1536]{1,0:T(8,128)(2,1)} custom-call(bf16[1024,1536]{1,0:T(8,128)(2,1)} %convolution_convert_fusion.3.qkv_ref, bf16[1024,512]{1,0:T(8,128)(2,1)} %convolution_convert_fusion.11.grad_ref, s32[1024,1]{1,0:T(8,128)} %copy.30.seg_col_ref, s32[1,1024]{1,0:T(1,128)} %bitcast.126), custom_call_target="tpu_custom_call" | custom-call | flops 65536 | bytes 65536 | tf_op jit(solution)/shard_map/attention_backward/pallas_call | solution.py:102
  774.5 23.4 %attention_backward.3 = bf16[1024,1536]{1,0:T(8,128)(2,1)} custom-call(bf16[1024,1536]{1,0:T(8,128)(2,1)} %convolution_convert_fusion.2.qkv_ref, bf16[1024,512]{1,0:T(8,128)(2,1)} %convolution_convert_fusion.10.grad_ref, s32[1024,1]{1,0:T(8,128)} %copy.31.seg_col_ref, s32[1,1024]{1,0:T(1,128)} %bitcast.123), custom_call_target="tpu_custom_call" | custom-call | flops 65536 | bytes 65536 | tf_op jit(solution)/shard_map/attention_backward/pallas_call | solution.py:102
  873.8 17.0 %collective-permute-done.86 = bf16[256,2048]{1,0:T(8,128)(2,1)S(1)} collective-permute-done((bf16[256,2048]{1,0:T(8,128)(2,1)S(1)}, bf16[256,2048]{1,0:T(8,128)(2,1)S(1)}, u32[]{:S(2)}, u32[]{:S(2)}) %collective-permute-start.86) | collective-permute-done | bytes 1048608 | tf_op jit(solution)/shard_map/ppermute | solution.py:260
  890.8 18.6 %collective-permute-done.85 = bf16[256,2048]{1,0:T(8,128)(2,1)S(1)} collective-permute-done((bf16[256,2048]{1,0:T(8,128)(2,1)S(1)}, bf16[256,2048]{1,0:T(8,128)(2,1)S(1)}, u32[]{:S(2)}, u32[]{:S(2)}) %collective-permute-start.85) | collective-permute-done | bytes 1048608 | tf_op jit(solution)/shard_map/ppermute | solution.py:260
  945.4 19.6 %collective-permute-done.98 = bf16[528,256]{1,0:T(8,128)(2,1)S(1)} collective-permute-done((bf16[528,256]{1,0:T(8,128)(2,1)S(1)}, bf16[528,256]{1,0:T(8,128)(2,1)S(1)}, u32[]{:S(2)}, u32[]{:S(2)}) %collective-permute-start.98) | collective-permute-done | bytes 270368 | tf_op jit(solution)/shard_map/ppermute | solution.py:260
  967.4 36.9 %collective-permute-done.88 = bf16[256,2048]{1,0:T(8,128)(2,1)S(1)} collective-permute-done((bf16[256,2048]{1,0:T(8,128)(2,1)S(1)}, bf16[256,2048]{1,0:T(8,128)(2,1)S(1)}, u32[]{:S(2)}, u32[]{:S(2)}) %collective-permute-start.88) | collective-permute-done | bytes 1048608 | tf_op jit(solution)/shard_map/ppermute | solution.py:260
  1006.8 14.2 %collective-permute-done.94 = bf16[256,1536]{1,0:T(8,128)(2,1)S(1)} collective-permute-done((bf16[256,1536]{1,0:T(8,128)(2,1)S(1)}, bf16[256,1536]{1,0:T(8,128)(2,1)S(1)}, u32[]{:S(2)}, u32[]{:S(2)}) %collective-permute-start.94) | collective-permute-done | bytes 786464 | tf_op jit(solution)/shard_map/ppermute | solution.py:260
  (619 shorter events, 445.8 us)
Async XLA Ops:
  52.2 48.3 %collective-permute-start.1 = (bf16[256,2048]{1,0:T(8,128)(2,1)S(1)}, bf16[256,2048]{1,0:T(8,128)(2,1)S(1)}, u32[]{:S(2)}, u32[]{:S(2)}) collective-permute-start(bf16[256,2048]{1,0:T(8,128)(2,1)S(1)} %select_bitcast_fusion.5), channel_id=1, source_target_pairs={{0,2},{1,3},{2,0},{3,1},{4,6},{5,7},{6,4},{7,5},{8,10},{9,11},{10,... | collective-permute-start | bytes 3145736 | tf_op jit(solution)/shard_map/ppermute | solution.py:260
  52.3 50.6 %collective-permute-start.11 = (s32[1024]{0:T(1024)S(1)}, s32[1024]{0:T(1024)S(1)}, u32[]{:S(2)}, u32[]{:S(2)}) collective-permute-start(s32[1024]{0:T(1024)S(1)} %bitcast.136), channel_id=1, source_target_pairs={{0,4},{1,5},{2,6},{3,7},{4,0},{5,1},{6,2},{7,3},{8,12},{9,13},{10,... | collective-permute-start | bytes 12296 | tf_op jit(solution)/shard_map/ppermute | solution.py:260
  148.4 48.7 %collective-permute-start.28 = (bf16[256,2048]{1,0:T(8,128)(2,1)S(1)}, bf16[256,2048]{1,0:T(8,128)(2,1)S(1)}, u32[]{:S(2)}, u32[]{:S(2)}) collective-permute-start(bf16[256,2048]{1,0:T(8,128)(2,1)S(1)} %copy-done.32), channel_id=1, source_target_pairs={{0,2},{1,3},{2,0},{3,1},{4,6},{5,7},{6,4},{7,5},{8,10},{9,11},{10,... | collective-permute-start | bytes 3145736 | tf_op jit(solution)/shard_map/ppermute | solution.py:260
  155.6 52.5 %collective-permute-start.20 = (bf16[256,2048]{1,0:T(8,128)(2,1)}, bf16[256,2048]{1,0:T(8,128)(2,1)}, u32[]{:S(2)}, u32[]{:S(2)}) collective-permute-start(bf16[256,2048]{1,0:T(8,128)(2,1)} %get-tuple-element.100), channel_id=1, source_target_pairs={{0,1},{1,0},{2,3},{3,2},{4,5},{5,4},{6,7},{7,6},{8,9},{9,8},{10,11... | collective-permute-start | bytes 3145736 | tf_op jit(solution)/shard_map/ppermute | solution.py:260
  209.8 46.9 %collective-permute-start.29 = (bf16[2048,256]{1,0:T(8,128)(2,1)}, bf16[2048,256]{1,0:T(8,128)(2,1)}, u32[]{:S(2)}, u32[]{:S(2)}) collective-permute-start(bf16[2048,256]{1,0:T(8,128)(2,1)} %param.18), channel_id=1, source_target_pairs={{0,2},{1,3},{2,0},{3,1},{4,6},{5,7},{6,4},{7,5},{8,10},{9,11},{10,... | collective-permute-start | bytes 3145736 | tf_op jit(solution)/shard_map/ppermute | solution.py:260
  213.9 44.2 %collective-permute-start.32 = (bf16[256,2048]{1,0:T(8,128)(2,1)}, bf16[256,2048]{1,0:T(8,128)(2,1)S(1)}, u32[]{:S(2)}, u32[]{:S(2)}) collective-permute-start(bf16[256,2048]{1,0:T(8,128)(2,1)} %get-tuple-element.207), channel_id=1, source_target_pairs={{0,8},{1,9},{2,10},{3,11},{4,12},{5,13},{6,14},{7,15},{8,0},{9,1},... | collective-permute-start | bytes 3145736 | tf_op jit(solution)/shard_map/ppermute | solution.py:260
  214.7 43.5 %collective-permute-start.33 = (bf16[256,2048]{1,0:T(8,128)(2,1)S(1)}, bf16[256,2048]{1,0:T(8,128)(2,1)S(1)}, u32[]{:S(2)}, u32[]{:S(2)}) collective-permute-start(bf16[256,2048]{1,0:T(8,128)(2,1)S(1)} %get-tuple-element.253), channel_id=1, source_target_pairs={{0,16},{1,17},{2,18},{3,19},{4,20},{5,21},{6,22},{7,23},{8,24},{9,... | collective-permute-start | bytes 3145736 | tf_op jit(solution)/shard_map/ppermute | solution.py:260
  263.1 48.0 %collective-permute-start.34 = (bf16[512,2048]{1,0:T(8,128)(2,1)S(1)}, bf16[512,2048]{1,0:T(8,128)(2,1)S(1)}, u32[]{:S(2)}, u32[]{:S(2)}) collective-permute-start(bf16[512,2048]{1,0:T(8,128)(2,1)S(1)} %pad_maximum_fusion.9), channel_id=1, source_target_pairs={{0,16},{1,17},{2,18},{3,19},{4,20},{5,21},{6,22},{7,23},{8,24},{9,... | collective-permute-start | bytes 6291464 | tf_op jit(solution)/shard_map/ppermute | solution.py:260
  264.5 47.7 %collective-permute-start.35 = (bf16[512,2048]{1,0:T(8,128)(2,1)S(1)}, bf16[512,2048]{1,0:T(8,128)(2,1)S(1)}, u32[]{:S(2)}, u32[]{:S(2)}) collective-permute-start(bf16[512,2048]{1,0:T(8,128)(2,1)S(1)} %pad_maximum_fusion.10), channel_id=1, source_target_pairs={{0,8},{1,9},{2,10},{3,11},{4,12},{5,13},{6,14},{7,15},{8,0},{9,1},... | collective-permute-start | bytes 6291464 | tf_op jit(solution)/shard_map/ppermute | solution.py:260
  290.3 46.8 %collective-permute-start.24 = (bf16[256,2048]{1,0:T(8,128)(2,1)S(1)}, bf16[256,2048]{1,0:T(8,128)(2,1)S(1)}, u32[]{:S(2)}, u32[]{:S(2)}) collective-permute-start(bf16[256,2048]{1,0:T(8,128)(2,1)S(1)} %fusion.28), channel_id=1, source_target_pairs={{0,1},{1,0},{2,3},{3,2},{4,5},{5,4},{6,7},{7,6},{8,9},{9,8},{10,11... | collective-permute-start | bytes 3145736 | tf_op jit(solution)/shard_map/ppermute | solution.py:260
  292.1 52.0 %collective-permute-start.25 = (bf16[256,2048]{1,0:T(8,128)(2,1)S(1)}, bf16[256,2048]{1,0:T(8,128)(2,1)S(1)}, u32[]{:S(2)}, u32[]{:S(2)}) collective-permute-start(bf16[256,2048]{1,0:T(8,128)(2,1)S(1)} %fusion.28), channel_id=1, source_target_pairs={{0,4},{1,5},{2,6},{3,7},{4,0},{5,1},{6,2},{7,3},{8,12},{9,13},{10,... | collective-permute-start | bytes 3145736 | tf_op jit(solution)/shard_map/ppermute | solution.py:260
  316.0 42.1 %collective-permute-start.38 = (bf16[256,2048]{1,0:T(8,128)(2,1)S(1)}, bf16[256,2048]{1,0:T(8,128)(2,1)S(1)}, u32[]{:S(2)}, u32[]{:S(2)}) collective-permute-start(bf16[256,2048]{1,0:T(8,128)(2,1)S(1)} %fusion.29), channel_id=1, source_target_pairs={{0,1},{1,0},{2,3},{3,2},{4,5},{5,4},{6,7},{7,6},{8,9},{9,8},{10,11... | collective-permute-start | bytes 3145736 | tf_op jit(solution)/shard_map/ppermute | solution.py:260
  341.6 51.3 %collective-permute-start.42 = (bf16[2048,512]{1,0:T(8,128)(2,1)S(1)}, bf16[2048,512]{1,0:T(8,128)(2,1)S(1)}, u32[]{:S(2)}, u32[]{:S(2)}) collective-permute-start(bf16[2048,512]{1,0:T(8,128)(2,1)S(1)} %constant_dynamic-update-slice_fusion.6), channel_id=1, source_target_pairs={{0,8},{1,9},{2,10},{3,11},{4,12},{5,13},{6,14},{7,15},{8,0},{9,1},... | collective-permute-start | bytes 6291464 | tf_op jit(solution)/shard_map/ppermute | solution.py:260
  344.1 48.8 %collective-permute-start.41 = (bf16[2048,512]{1,0:T(8,128)(2,1)S(1)}, bf16[2048,512]{1,0:T(8,128)(2,1)S(1)}, u32[]{:S(2)}, u32[]{:S(2)}) collective-permute-start(bf16[2048,512]{1,0:T(8,128)(2,1)S(1)} %get-tuple-element.250), channel_id=1, source_target_pairs={{0,16},{1,17},{2,18},{3,19},{4,20},{5,21},{6,22},{7,23},{8,24},{9,... | collective-permute-start | bytes 6291464 | tf_op jit(solution)/shard_map/ppermute | solution.py:260
  373.6 49.0 %collective-permute-start.45 = (bf16[256,2048]{1,0:T(8,128)(2,1)S(1)}, bf16[256,2048]{1,0:T(8,128)(2,1)S(1)}, u32[]{:S(2)}, u32[]{:S(2)}) collective-permute-start(bf16[256,2048]{1,0:T(8,128)(2,1)S(1)} %copy-done.76), channel_id=1, source_target_pairs={{0,2},{1,3},{2,0},{3,1},{4,6},{5,7},{6,4},{7,5},{8,10},{9,11},{10,... | collective-permute-start | bytes 3145736 | tf_op jit(solution)/shard_map/ppermute | solution.py:260
  429.4 44.7 %collective-permute-start.48 = (bf16[256,2048]{1,0:T(8,128)(2,1)}, bf16[256,2048]{1,0:T(8,128)(2,1)}, u32[]{:S(2)}, u32[]{:S(2)}) collective-permute-start(bf16[256,2048]{1,0:T(8,128)(2,1)} %slice.498), channel_id=1, source_target_pairs={{0,1},{1,0},{2,3},{3,2},{4,5},{5,4},{6,7},{7,6},{8,9},{9,8},{10,11... | collective-permute-start | bytes 3145736 | tf_op jit(solution)/shard_map/ppermute | solution.py:260
  547.2 49.0 %collective-permute-start.50 = (bf16[256,2048]{1,0:T(8,128)(2,1)}, bf16[256,2048]{1,0:T(8,128)(2,1)S(1)}, u32[]{:S(2)}, u32[]{:S(2)}) collective-permute-start(bf16[256,2048]{1,0:T(8,128)(2,1)} %get-tuple-element.225), channel_id=1, source_target_pairs={{0,2},{1,3},{2,0},{3,1},{4,6},{5,7},{6,4},{7,5},{8,10},{9,11},{10,... | collective-permute-start | bytes 3145736 | tf_op jit(solution)/shard_map/ppermute | solution.py:260
  594.2 56.6 %collective-permute-start.62 = (bf16[2048,512]{1,0:T(8,128)(2,1)}, bf16[2048,512]{1,0:T(8,128)(2,1)S(1)}, u32[]{:S(2)}, u32[]{:S(2)}) collective-permute-start(bf16[2048,512]{1,0:T(8,128)(2,1)} %get-tuple-element.219), channel_id=1, source_target_pairs={{0,16},{1,17},{2,18},{3,19},{4,20},{5,21},{6,22},{7,23},{8,24},{9,... | collective-permute-start | bytes 6291464 | tf_op jit(solution)/shard_map/ppermute | solution.py:260
  595.5 55.3 %collective-permute-start.63 = (bf16[2048,512]{1,0:T(8,128)(2,1)}, bf16[2048,512]{1,0:T(8,128)(2,1)S(1)}, u32[]{:S(2)}, u32[]{:S(2)}) collective-permute-start(bf16[2048,512]{1,0:T(8,128)(2,1)} %get-tuple-element.218), channel_id=1, source_target_pairs={{0,8},{1,9},{2,10},{3,11},{4,12},{5,13},{6,14},{7,15},{8,0},{9,1},... | collective-permute-start | bytes 6291464 | tf_op jit(solution)/shard_map/ppermute | solution.py:260
  635.4 50.3 %collective-permute-start.59 = (bf16[256,2048]{1,0:T(8,128)(2,1)S(1)}, bf16[256,2048]{1,0:T(8,128)(2,1)}, u32[]{:S(2)}, u32[]{:S(2)}) collective-permute-start(bf16[256,2048]{1,0:T(8,128)(2,1)S(1)} %get-tuple-element.199), channel_id=1, source_target_pairs={{0,1},{1,0},{2,3},{3,2},{4,5},{5,4},{6,7},{7,6},{8,9},{9,8},{10,11... | collective-permute-start | bytes 3145736 | tf_op jit(solution)/shard_map/ppermute | solution.py:260
  636.1 59.5 %collective-permute-start.60 = (bf16[256,2048]{1,0:T(8,128)(2,1)S(1)}, bf16[256,2048]{1,0:T(8,128)(2,1)}, u32[]{:S(2)}, u32[]{:S(2)}) collective-permute-start(bf16[256,2048]{1,0:T(8,128)(2,1)S(1)} %get-tuple-element.199), channel_id=1, source_target_pairs={{0,4},{1,5},{2,6},{3,7},{4,0},{5,1},{6,2},{7,3},{8,12},{9,13},{10,... | collective-permute-start | bytes 3145736 | tf_op jit(solution)/shard_map/ppermute | solution.py:260
  685.8 47.6 %collective-permute-start.72 = (bf16[512,2048]{1,0:T(8,128)(2,1)}, bf16[512,2048]{1,0:T(8,128)(2,1)}, u32[]{:S(2)}, u32[]{:S(2)}) collective-permute-start(bf16[512,2048]{1,0:T(8,128)(2,1)} %get-tuple-element.215), channel_id=1, source_target_pairs={{0,16},{1,17},{2,18},{3,19},{4,20},{5,21},{6,22},{7,23},{8,24},{9,... | collective-permute-start | bytes 6291464 | tf_op jit(solution)/shard_map/ppermute | solution.py:260
  687.1 47.2 %collective-permute-start.73 = (bf16[512,2048]{1,0:T(8,128)(2,1)}, bf16[512,2048]{1,0:T(8,128)(2,1)}, u32[]{:S(2)}, u32[]{:S(2)}) collective-permute-start(bf16[512,2048]{1,0:T(8,128)(2,1)} %get-tuple-element.214), channel_id=1, source_target_pairs={{0,8},{1,9},{2,10},{3,11},{4,12},{5,13},{6,14},{7,15},{8,0},{9,1},... | collective-permute-start | bytes 6291464 | tf_op jit(solution)/shard_map/ppermute | solution.py:260
  755.8 48.7 %collective-permute-start.81 = (bf16[2048,256]{1,0:T(8,128)(2,1)}, bf16[2048,256]{1,0:T(8,128)(2,1)}, u32[]{:S(2)}, u32[]{:S(2)}) collective-permute-start(bf16[2048,256]{1,0:T(8,128)(2,1)} %get-tuple-element.245), channel_id=1, source_target_pairs={{0,2},{1,3},{2,0},{3,1},{4,6},{5,7},{6,4},{7,5},{8,10},{9,11},{10,... | collective-permute-start | bytes 3145736 | tf_op jit(solution)/shard_map/ppermute | solution.py:260
  772.6 48.0 %collective-permute-start.75 = (bf16[256,2048]{1,0:T(8,128)(2,1)}, bf16[256,2048]{1,0:T(8,128)(2,1)}, u32[]{:S(2)}, u32[]{:S(2)}) collective-permute-start(bf16[256,2048]{1,0:T(8,128)(2,1)} %slice.495), channel_id=1, source_target_pairs={{0,1},{1,0},{2,3},{3,2},{4,5},{5,4},{6,7},{7,6},{8,9},{9,8},{10,11... | collective-permute-start | bytes 3145736 | tf_op jit(solution)/shard_map/ppermute | solution.py:260
  843.2 47.5 %collective-permute-start.86 = (bf16[256,2048]{1,0:T(8,128)(2,1)S(1)}, bf16[256,2048]{1,0:T(8,128)(2,1)S(1)}, u32[]{:S(2)}, u32[]{:S(2)}) collective-permute-start(bf16[256,2048]{1,0:T(8,128)(2,1)S(1)} %get-tuple-element.243), channel_id=1, source_target_pairs={{0,2},{1,3},{2,0},{3,1},{4,6},{5,7},{6,4},{7,5},{8,10},{9,11},{10,... | collective-permute-start | bytes 3145736 | tf_op jit(solution)/shard_map/ppermute | solution.py:260
  861.9 47.5 %collective-permute-start.85 = (bf16[256,2048]{1,0:T(8,128)(2,1)S(1)}, bf16[256,2048]{1,0:T(8,128)(2,1)S(1)}, u32[]{:S(2)}, u32[]{:S(2)}) collective-permute-start(bf16[256,2048]{1,0:T(8,128)(2,1)S(1)} %slice.494), channel_id=1, source_target_pairs={{0,1},{1,0},{2,3},{3,2},{4,5},{5,4},{6,7},{7,6},{8,9},{9,8},{10,11... | collective-permute-start | bytes 3145736 | tf_op jit(solution)/shard_map/ppermute | solution.py:260
  870.2 47.8 %collective-permute-start.90 = (bf16[512,1536]{1,0:T(8,128)(2,1)}, bf16[512,1536]{1,0:T(8,128)(2,1)}, u32[]{:S(2)}, u32[]{:S(2)}) collective-permute-start(bf16[512,1536]{1,0:T(8,128)(2,1)} %split.156), channel_id=1, source_target_pairs={{0,8},{1,9},{2,10},{3,11},{4,12},{5,13},{6,14},{7,15},{8,0},{9,1},... | collective-permute-start | bytes 4718600 | tf_op jit(solution)/shard_map/ppermute | solution.py:260
  870.9 47.1 %collective-permute-start.89 = (bf16[512,1536]{1,0:T(8,128)(2,1)S(1)}, bf16[512,1536]{1,0:T(8,128)(2,1)}, u32[]{:S(2)}, u32[]{:S(2)}) collective-permute-start(bf16[512,1536]{1,0:T(8,128)(2,1)S(1)} %split.155), channel_id=1, source_target_pairs={{0,16},{1,17},{2,18},{3,19},{4,20},{5,21},{6,22},{7,23},{8,24},{9,... | collective-permute-start | bytes 4718600 | tf_op jit(solution)/shard_map/ppermute | solution.py:260
  873.8 54.1 %collective-permute-start.97 = (bf16[528,256]{1,0:T(8,128)(2,1)}, bf16[528,256]{1,0:T(8,128)(2,1)}, u32[]{:S(2)}, u32[]{:S(2)}) collective-permute-start(bf16[528,256]{1,0:T(8,128)(2,1)} %broadcast_select_fusion.28), channel_id=1, source_target_pairs={{0,4},{1,5},{2,6},{3,7},{4,0},{5,1},{6,2},{7,3},{8,12},{9,13},{10,... | collective-permute-start | bytes 811016 | tf_op jit(solution)/shard_map/ppermute | solution.py:260
  929.2 75.2 %collective-permute-start.88 = (bf16[256,2048]{1,0:T(8,128)(2,1)S(1)}, bf16[256,2048]{1,0:T(8,128)(2,1)S(1)}, u32[]{:S(2)}, u32[]{:S(2)}) collective-permute-start(bf16[256,2048]{1,0:T(8,128)(2,1)S(1)} %broadcast_select_fusion.8), channel_id=1, source_target_pairs={{0,2},{1,3},{2,0},{3,1},{4,6},{5,7},{6,4},{7,5},{8,10},{9,11},{10,... | collective-permute-start | bytes 3145736 | tf_op jit(solution)/shard_map/ppermute | solution.py:260
  966.9 54.1 %collective-permute-start.94 = (bf16[256,1536]{1,0:T(8,128)(2,1)S(1)}, bf16[256,1536]{1,0:T(8,128)(2,1)S(1)}, u32[]{:S(2)}, u32[]{:S(2)}) collective-permute-start(bf16[256,1536]{1,0:T(8,128)(2,1)S(1)} %broadcast_select_fusion.22), channel_id=1, source_target_pairs={{0,2},{1,3},{2,0},{3,1},{4,6},{5,7},{6,4},{7,5},{8,10},{9,11},{10,... | collective-permute-start | bytes 2359304 | tf_op jit(solution)/shard_map/ppermute | solution.py:260
  (179 other events, 2792.3 us)

commit v5 on v4

--- a/solution.py
+++ b/solution.py
@@ -373,7 +373,7 @@
     streams = range(2)
     pair_q = False
     pair_o = True
-    pair_e = True
+    pair_e = False
     pair_c = False
     send_c = True
     send_e = False
@@ -396,7 +396,7 @@
     expand_other = swap(after(expand_weight, token_other), half_bit)
     homes, _ = to_home(token_own, token_other)
     sent = [gather_far(homes[0])]
-    sent.append(gather_far(after(homes[1], *sent[0])))
+    sent.append(gather_far(homes[1]))
     qkv_parts = doubled(qkv_parts, 0, 1, last, pair_q)
     qkv_got = moved(qkv_parts, last, pair_q)
     full_qkv = jnp.concatenate([qkv_parts[0], qkv_got[0], qkv_parts[1], qkv_got[1]], axis=0)
@@ -481,8 +481,6 @@
         )
         gate = (branch_grad[j][0].astype(BF16),)
         sent.append(gather_far(gate[0]))
-        if j == 0:
-            gate = ()
     result_kept, result_got = sent_home([second[j][0].astype(BF16) for j in streams])
     branch_rows, hidden_grad, normed_part = [], [], []
     partial, pairs = [], []

time: 1030 us -> 1020 us (level)
    unnamed x246 -> x244, local copies, waits for them, and re-layouts: 43.3 us -> 41 us
  transfers between devices with their start and end apart: 99 -> 99, of which waited for: 36 -> 37; matrix products, arithmetic and copies ran while one was open for 39% -> 40% of each run, Pallas kernels for 9% -> 9%
where the time goes in v5:
time: 1020 us; the launch traced here: 1010 us
  waiting for transfers between devices  393 us (39%)
  matrix products  255 us (25%)
  other arithmetic  128 us (13%)
  Pallas kernels  89 us (9%)
  local copies, waits for them, and re-layouts  80 us (8%)
  starting transfers between devices  66.2 us (6%)
    ppermute x99, waiting for transfers between devices, swap(): return lax.ppermute(array, AXES, [(i, i ^ mask) for i in range(total)])  393 us
    dot_general x10, matrix products, dot_tn(): lax.dot_general(left, right, (((0,), (0,)), ((), ())), preferred_element_...  87.1 us
    dot_general x8, matrix products, dot_nt(): lax.dot_general(left, right, (((1,), (1,)), ((), ())), preferred_element_...  85.2 us
    dot_general x8, matrix products, dot_nn(): return jnp.dot(left, right, preferred_element_type=F32)  82.3 us
    ppermute x99, starting transfers between devices, swap(): return lax.ppermute(array, AXES, [(i, i ^ mask) for i in range(total)])  66.2 us
    pallas_call x2, Pallas kernels, attention_backward(): pl.pallas_call(functools.partial(attention_backward_kernel, block=min(256...  46.5 us
    unnamed x244, local copies, waits for them, and re-layouts  41 us
    pallas_call x2, Pallas kernels, attention_forward(): pl.pallas_call(functools.partial(attention_forward_kernel, block=min(256,...  23.6 us
  transfers between devices with their start and end apart: 99, of which 37 were waited for; matrix products, arithmetic and copies ran while one was open for 40% of the time, Pallas kernels for 9%

profile of v5, /device:TPU:0, one launch (start us, length us, event | category | flops | bytes accessed | tf_op | source)
XLA Modules:
  0.0 1013.0 jit_solution(7358378817673572143)
XLA Ops:
  8.4 34.5 %collective-permute-done = bf16[256,1536]{1,0:T(8,128)(2,1)} collective-permute-done((bf16[256,1536]{1,0:T(8,128)(2,1)S(1)}, bf16[256,1536]{1,0:T(8,128)(2,1)}, u32[]{:S(2)}, u32[]{:S(2)}) %collective-permute-start) | collective-permute-done | bytes 786464 | tf_op jit(solution)/shard_map/ppermute | solution.py:260
  52.4 16.4 %collective-permute-done.4 = bf16[256,1536]{1,0:T(8,128)(2,1)S(1)} collective-permute-done((bf16[256,1536]{1,0:T(8,128)(2,1)S(1)}, bf16[256,1536]{1,0:T(8,128)(2,1)S(1)}, u32[]{:S(2)}, u32[]{:S(2)}) %collective-permute-start.4) | collective-permute-done | bytes 786464 | tf_op jit(solution)/shard_map/ppermute | solution.py:260
  71.3 29.1 %collective-permute-done.1 = bf16[256,2048]{1,0:T(8,128)(2,1)S(1)} collective-permute-done((bf16[256,2048]{1,0:T(8,128)(2,1)S(1)}, bf16[256,2048]{1,0:T(8,128)(2,1)S(1)}, u32[]{:S(2)}, u32[]{:S(2)}) %collective-permute-start.1) | collective-permute-done | bytes 1048608 | tf_op jit(solution)/shard_map/ppermute | solution.py:260
  116.9 23.2 %collective-permute-done.9 = bf16[512,1536]{1,0:T(8,128)(2,1)} collective-permute-done((bf16[512,1536]{1,0:T(8,128)(2,1)}, bf16[512,1536]{1,0:T(8,128)(2,1)}, u32[]{:S(2)}, u32[]{:S(2)}) %collective-permute-start.9) | collective-permute-done | bytes 1572896 | tf_op jit(solution)/shard_map/ppermute | solution.py:260
  159.8 12.5 %convolution_convert_fusion.3.qkv_ref = bf16[1024,1536]{1,0:T(8,128)(2,1)} fusion(bf16[2048,1536]{1,0:T(8,128)(2,1)} %copy-done.81, bf16[256,2048]{1,0:T(8,128)(2,1)} %collective-permute-done.8, bf16[256,2048]{1,0:T(8,128)(2,1)} %collective-permute-done.7, bf16[256,2048]{1,0:T(8,128)(2,1)} %collective-permute-done.6, bf16[256,2048]{1,0:T(8,128)(2,1)} %get-tuple-element.226), kind=kOutput, calls=%fused_computation.39 | convolution fusion | flops 6460801024 | bytes 13631488 | tf_op jit(solution)/shard_map/dot_general | solution.py:20
  172.3 11.8 %attention_forward.2 = bf16[1024,512]{1,0:T(8,128)(2,1)} custom-call(bf16[1024,1536]{1,0:T(8,128)(2,1)} %convolution_convert_fusion.3.qkv_ref, s32[1024,1]{1,0:T(8,128)} %copy.30.seg_col_ref, s32[1,1024]{1,0:T(1,128)} %bitcast.131), custom_call_target="tpu_custom_call" | custom-call | flops 65536 | bytes 65536 | tf_op jit(solution)/shard_map/attention_forward/pallas_call | solution.py:82
  184.1 13.2 %collective-permute-done.28 = bf16[256,2048]{1,0:T(8,128)(2,1)S(1)} collective-permute-done((bf16[256,2048]{1,0:T(8,128)(2,1)S(1)}, bf16[256,2048]{1,0:T(8,128)(2,1)S(1)}, u32[]{:S(2)}, u32[]{:S(2)}) %collective-permute-start.28) | collective-permute-done | bytes 1048608 | tf_op jit(solution)/shard_map/ppermute | solution.py:260
  233.5 11.8 %attention_forward.3 = bf16[1024,512]{1,0:T(8,128)(2,1)} custom-call(bf16[1024,1536]{1,0:T(8,128)(2,1)} %convolution_convert_fusion.2.qkv_ref, s32[1024,1]{1,0:T(8,128)} %copy.31.seg_col_ref, s32[1,1024]{1,0:T(1,128)} %bitcast.128), custom_call_target="tpu_custom_call" | custom-call | flops 65536 | bytes 65536 | tf_op jit(solution)/shard_map/attention_forward/pallas_call | solution.py:82
  268.6 22.6 %collective-permute-done.19 = bf16[256,2048]{1,0:T(8,128)(2,1)S(1)} collective-permute-done((bf16[256,2048]{1,0:T(8,128)(2,1)S(1)}, bf16[256,2048]{1,0:T(8,128)(2,1)S(1)}, u32[]{:S(2)}, u32[]{:S(2)}) %collective-permute-start.19) | collective-permute-done | bytes 1048608 | tf_op jit(solution)/shard_map/ppermute | solution.py:260
  294.7 23.1 %collective-permute-done.27 = bf16[256,2048]{1,0:T(8,128)(2,1)S(1)} collective-permute-done((bf16[256,2048]{1,0:T(8,128)(2,1)S(1)}, bf16[256,2048]{1,0:T(8,128)(2,1)S(1)}, u32[]{:S(2)}, u32[]{:S(2)}) %collective-permute-start.27) | collective-permute-done | bytes 1048608 | tf_op jit(solution)/shard_map/ppermute | solution.py:260
  323.5 16.8 %collective-permute-done.24 = bf16[256,2048]{1,0:T(8,128)(2,1)S(1)} collective-permute-done((bf16[256,2048]{1,0:T(8,128)(2,1)S(1)}, bf16[256,2048]{1,0:T(8,128)(2,1)S(1)}, u32[]{:S(2)}, u32[]{:S(2)}) %collective-permute-start.24) | collective-permute-done | bytes 1048608 | tf_op jit(solution)/shard_map/ppermute | solution.py:260
  347.9 12.9 %collective-permute-done.38 = bf16[256,2048]{1,0:T(8,128)(2,1)S(1)} collective-permute-done((bf16[256,2048]{1,0:T(8,128)(2,1)S(1)}, bf16[256,2048]{1,0:T(8,128)(2,1)S(1)}, u32[]{:S(2)}, u32[]{:S(2)}) %collective-permute-start.38) | collective-permute-done | bytes 1048608 | tf_op jit(solution)/shard_map/ppermute | solution.py:260
  360.8 15.4 %multiply_convert_fusion.3 = (bf16[1024,2048]{1,0:T(8,128)(2,1)}, f32[1024,2048]{1,0:T(8,128)}) fusion(bf16[1024,2048]{1,0:T(8,128)(2,1)S(1)} %pad_maximum_fusion.2, bf16[2048,2048]{1,0:T(8,128)(2,1)} %constant_dynamic-update-slice_fusion.8), kind=kOutput, calls=%fused_computation.9 | convolution fusion | flops 8608808960 | bytes 25165824 | tf_op jit(solution)/shard_map/dot_general | solution.py:20
  378.0 16.8 %multiply_convert_fusion.2 = (bf16[1024,2048]{1,0:T(8,128)(2,1)}, f32[1024,2048]{1,0:T(8,128)}) fusion(bf16[1024,2048]{1,0:T(8,128)(2,1)S(1)} %pad_maximum_fusion.3, bf16[2048,2048]{1,0:T(8,128)(2,1)} %constant_dynamic-update-slice_fusion.8), kind=kOutput, calls=%fused_computation.6 | convolution fusion | flops 8608808960 | bytes 25165824 | tf_op jit(solution)/shard_map/dot_general | solution.py:20
  400.8 11.4 %convolution_convert_fusion.7 = bf16[1024,2048]{1,0:T(8,128)(2,1)S(1)} fusion(bf16[1024,2048]{1,0:T(8,128)(2,1)S(1)} %copy-done.104, bf16[2048,2048]{1,0:T(8,128)(2,1)} %constant_dynamic-update-slice_fusion.14), kind=kOutput, calls=%fused_computation.43 | convolution fusion | flops 8592031744 | bytes 16777216 | tf_op jit(solution)/shard_map/dot_general | solution.py:20
  442.4 12.7 %collective-permute-done.44 = bf16[256,2048]{1,0:T(8,128)(2,1)} collective-permute-done((bf16[256,2048]{1,0:T(8,128)(2,1)S(1)}, bf16[256,2048]{1,0:T(8,128)(2,1)}, u32[]{:S(2)}, u32[]{:S(2)}) %collective-permute-start.44) | collective-permute-done | bytes 1048608 | tf_op jit(solution)/shard_map/ppermute | solution.py:260
  461.5 16.0 %collective-permute-done.48 = bf16[256,2048]{1,0:T(8,128)(2,1)S(1)} collective-permute-done((bf16[256,2048]{1,0:T(8,128)(2,1)S(1)}, bf16[256,2048]{1,0:T(8,128)(2,1)S(1)}, u32[]{:S(2)}, u32[]{:S(2)}) %collective-permute-start.48) | collective-permute-done | bytes 1048608 | tf_op jit(solution)/shard_map/ppermute | solution.py:260
  504.1 16.3 %multiply_convert_fusion.1 = bf16[1024,2048]{1,0:T(8,128)(2,1)S(1)} fusion(bf16[1024,2048]{1,0:T(8,128)(2,1)S(1)} %pad_maximum_fusion.4, bf16[2048,2048]{1,0:T(8,128)(2,1)} %constant_dynamic-update-slice_fusion.14, f32[1024,2048]{1,0:T(8,128)} %get-tuple-element.267), kind=kOutput, calls=%fused_computation.4 | convolution fusion | flops 8631877632 | bytes 25165824 | tf_op jit(solution)/shard_map/dot_general | solution.py:28
  520.4 13.0 %convolution_convert_fusion.5 = bf16[1024,2048]{1,0:T(8,128)(2,1)S(1)} fusion(bf16[1024,2048]{1,0:T(8,128)(2,1)S(1)} %multiply_convert_fusion.1, bf16[2048,2048]{1,0:T(8,128)(2,1)} %constant_dynamic-update-slice_fusion.8), kind=kOutput, calls=%fused_computation.41 | convolution fusion | flops 8592031744 | bytes 16777216 | tf_op jit(solution)/shard_map/dot_general | solution.py:28
  545.5 11.9 %fusion.69 = f32[2048,2048]{1,0:T(8,128)} fusion(bf16[1024,2048]{1,0:T(8,128)(2,1)S(1)} %copy-done.105, bf16[1024,2048]{1,0:T(8,128)(2,1)S(1)} %pad_maximum_fusion.4), kind=kOutput, calls=%fused_computation.310 | convolution fusion | flops 8589934592 | bytes 25165824 | tf_op jit(solution)/shard_map/dot_general | solution.py:24
  557.5 16.5 %add_convert_fusion.1 = bf16[2048,2048]{1,0:T(8,128)(2,1)} fusion(f32[2048,2048]{1,0:T(8,128)} %fusion.69, bf16[1024,2048]{1,0:T(8,128)(2,1)} %get-tuple-element.115, bf16[256,2048]{1,0:T(8,128)(2,1)} %copy-done.80, bf16[256,2048]{1,0:T(8,128)(2,1)} %copy-done.79, bf16[256,2048]{1,0:T(8,128)(2,1)} %copy-done.78, bf16[256,2048]{1,0:T(8,128)(2,1)} %copy-done.56), kind=kOutput, calls=%fused_computation.1 | convolution fusion | flops 8615100416 | bytes 33554432 | tf_op jit(solution)/shard_map/dot_general | solution.py:24
  583.5 18.5 %multiply_convert_fusion = bf16[1024,2048]{1,0:T(8,128)(2,1)} fusion(bf16[1024,2048]{1,0:T(8,128)(2,1)S(1)} %copy-done.40, bf16[2048,2048]{1,0:T(8,128)(2,1)} %constant_dynamic-update-slice_fusion.14, f32[1024,2048]{1,0:T(8,128)} %get-tuple-element.269), kind=kOutput, calls=%fused_computation.2 | convolution fusion | flops 8631877632 | bytes 25165824 | tf_op jit(solution)/shard_map/dot_general | solution.py:28
  602.1 12.8 %convolution_convert_fusion.4 = bf16[1024,2048]{1,0:T(8,128)(2,1)S(1)} fusion(bf16[1024,2048]{1,0:T(8,128)(2,1)} %multiply_convert_fusion, bf16[2048,2048]{1,0:T(8,128)(2,1)} %constant_dynamic-update-slice_fusion.8), kind=kOutput, calls=%fused_computation.40 | convolution fusion | flops 8592031744 | bytes 16777216 | tf_op jit(solution)/shard_map/dot_general | solution.py:28
  624.8 14.7 %fusion.70 = f32[2048,2048]{1,0:T(8,128)} fusion(bf16[1024,2048]{1,0:T(8,128)(2,1)S(1)} %copy-done.39, bf16[1024,2048]{1,0:T(8,128)(2,1)} %copy-done.106), kind=kOutput, calls=%fused_computation.311 | convolution fusion | flops 8589934592 | bytes 25165824 | tf_op jit(solution)/shard_map/dot_general | solution.py:24
  651.1 16.5 %add_convert_fusion = bf16[2048,2048]{1,0:T(8,128)(2,1)} fusion(f32[2048,2048]{1,0:T(8,128)} %fusion.70, bf16[1024,2048]{1,0:T(8,128)(2,1)} %copy-done.37, bf16[1024,2048]{1,0:T(8,128)(2,1)} %multiply_convert_fusion), kind=kOutput, calls=%fused_computation | convolution fusion | flops 8598323200 | bytes 33554432 | tf_op jit(solution)/shard_map/dot_general | solution.py:24
  694.0 23.1 %attention_backward.2 = bf16[1024,1536]{1,0:T(8,128)(2,1)} custom-call(bf16[1024,1536]{1,0:T(8,128)(2,1)} %convolution_convert_fusion.3.qkv_ref, bf16[1024,512]{1,0:T(8,128)(2,1)} %convolution_convert_fusion.11.grad_ref, s32[1024,1]{1,0:T(8,128)} %copy.30.seg_col_ref, s32[1,1024]{1,0:T(1,128)} %bitcast.132), custom_call_target="tpu_custom_call" | custom-call | flops 65536 | bytes 65536 | tf_op jit(solution)/shard_map/attention_backward/pallas_call | solution.py:102
  761.4 23.4 %attention_backward.3 = bf16[1024,1536]{1,0:T(8,128)(2,1)} custom-call(bf16[1024,1536]{1,0:T(8,128)(2,1)} %convolution_convert_fusion.2.qkv_ref, bf16[1024,512]{1,0:T(8,128)(2,1)} %convolution_convert_fusion.10.grad_ref, s32[1024,1]{1,0:T(8,128)} %copy.31.seg_col_ref, s32[1,1024]{1,0:T(1,128)} %bitcast.129), custom_call_target="tpu_custom_call" | custom-call | flops 65536 | bytes 65536 | tf_op jit(solution)/shard_map/attention_backward/pallas_call | solution.py:102
  861.8 17.6 %collective-permute-done.86 = bf16[256,2048]{1,0:T(8,128)(2,1)S(1)} collective-permute-done((bf16[256,2048]{1,0:T(8,128)(2,1)S(1)}, bf16[256,2048]{1,0:T(8,128)(2,1)S(1)}, u32[]{:S(2)}, u32[]{:S(2)}) %collective-permute-start.86) | collective-permute-done | bytes 1048608 | tf_op jit(solution)/shard_map/ppermute | solution.py:260
  879.4 18.7 %collective-permute-done.85 = bf16[256,2048]{1,0:T(8,128)(2,1)S(1)} collective-permute-done((bf16[256,2048]{1,0:T(8,128)(2,1)S(1)}, bf16[256,2048]{1,0:T(8,128)(2,1)S(1)}, u32[]{:S(2)}, u32[]{:S(2)}) %collective-permute-start.85) | collective-permute-done | bytes 1048608 | tf_op jit(solution)/shard_map/ppermute | solution.py:260
  932.9 20.5 %collective-permute-done.98 = bf16[528,256]{1,0:T(8,128)(2,1)S(1)} collective-permute-done((bf16[528,256]{1,0:T(8,128)(2,1)S(1)}, bf16[528,256]{1,0:T(8,128)(2,1)S(1)}, u32[]{:S(2)}, u32[]{:S(2)}) %collective-permute-start.98) | collective-permute-done | bytes 270368 | tf_op jit(solution)/shard_map/ppermute | solution.py:260
  955.8 36.9 %collective-permute-done.88 = bf16[256,2048]{1,0:T(8,128)(2,1)S(1)} collective-permute-done((bf16[256,2048]{1,0:T(8,128)(2,1)S(1)}, bf16[256,2048]{1,0:T(8,128)(2,1)S(1)}, u32[]{:S(2)}, u32[]{:S(2)}) %collective-permute-start.88) | collective-permute-done | bytes 1048608 | tf_op jit(solution)/shard_map/ppermute | solution.py:260
  995.2 13.6 %collective-permute-done.94 = bf16[256,1536]{1,0:T(8,128)(2,1)S(1)} collective-permute-done((bf16[256,1536]{1,0:T(8,128)(2,1)S(1)}, bf16[256,1536]{1,0:T(8,128)(2,1)S(1)}, u32[]{:S(2)}, u32[]{:S(2)}) %collective-permute-start.94) | collective-permute-done | bytes 786464 | tf_op jit(solution)/shard_map/ppermute | solution.py:260
  (620 shorter events, 435.8 us)
Async XLA Ops:
  52.2 48.3 %collective-permute-start.1 = (bf16[256,2048]{1,0:T(8,128)(2,1)S(1)}, bf16[256,2048]{1,0:T(8,128)(2,1)S(1)}, u32[]{:S(2)}, u32[]{:S(2)}) collective-permute-start(bf16[256,2048]{1,0:T(8,128)(2,1)S(1)} %select_bitcast_fusion.5), channel_id=1, source_target_pairs={{0,2},{1,3},{2,0},{3,1},{4,6},{5,7},{6,4},{7,5},{8,10},{9,11},{10,... | collective-permute-start | bytes 3145736 | tf_op jit(solution)/shard_map/ppermute | solution.py:260
  52.3 50.6 %collective-permute-start.11 = (s32[1024]{0:T(1024)S(1)}, s32[1024]{0:T(1024)S(1)}, u32[]{:S(2)}, u32[]{:S(2)}) collective-permute-start(s32[1024]{0:T(1024)S(1)} %bitcast.141), channel_id=1, source_target_pairs={{0,4},{1,5},{2,6},{3,7},{4,0},{5,1},{6,2},{7,3},{8,12},{9,13},{10,... | collective-permute-start | bytes 12296 | tf_op jit(solution)/shard_map/ppermute | solution.py:260
  148.4 48.8 %collective-permute-start.28 = (bf16[256,2048]{1,0:T(8,128)(2,1)S(1)}, bf16[256,2048]{1,0:T(8,128)(2,1)S(1)}, u32[]{:S(2)}, u32[]{:S(2)}) collective-permute-start(bf16[256,2048]{1,0:T(8,128)(2,1)S(1)} %copy-done.33), channel_id=1, source_target_pairs={{0,2},{1,3},{2,0},{3,1},{4,6},{5,7},{6,4},{7,5},{8,10},{9,11},{10,... | collective-permute-start | bytes 3145736 | tf_op jit(solution)/shard_map/ppermute | solution.py:260
  155.6 52.6 %collective-permute-start.20 = (bf16[256,2048]{1,0:T(8,128)(2,1)}, bf16[256,2048]{1,0:T(8,128)(2,1)}, u32[]{:S(2)}, u32[]{:S(2)}) collective-permute-start(bf16[256,2048]{1,0:T(8,128)(2,1)} %get-tuple-element.95), channel_id=1, source_target_pairs={{0,1},{1,0},{2,3},{3,2},{4,5},{5,4},{6,7},{7,6},{8,9},{9,8},{10,11... | collective-permute-start | bytes 3145736 | tf_op jit(solution)/shard_map/ppermute | solution.py:260
  209.9 46.8 %collective-permute-start.29 = (bf16[2048,256]{1,0:T(8,128)(2,1)}, bf16[2048,256]{1,0:T(8,128)(2,1)}, u32[]{:S(2)}, u32[]{:S(2)}) collective-permute-start(bf16[2048,256]{1,0:T(8,128)(2,1)} %param.18), channel_id=1, source_target_pairs={{0,2},{1,3},{2,0},{3,1},{4,6},{5,7},{6,4},{7,5},{8,10},{9,11},{10,... | collective-permute-start | bytes 3145736 | tf_op jit(solution)/shard_map/ppermute | solution.py:260
  214.0 44.2 %collective-permute-start.32 = (bf16[256,2048]{1,0:T(8,128)(2,1)}, bf16[256,2048]{1,0:T(8,128)(2,1)S(1)}, u32[]{:S(2)}, u32[]{:S(2)}) collective-permute-start(bf16[256,2048]{1,0:T(8,128)(2,1)} %get-tuple-element.197), channel_id=1, source_target_pairs={{0,8},{1,9},{2,10},{3,11},{4,12},{5,13},{6,14},{7,15},{8,0},{9,1},... | collective-permute-start | bytes 3145736 | tf_op jit(solution)/shard_map/ppermute | solution.py:260
  214.8 45.9 %collective-permute-start.33 = (bf16[256,2048]{1,0:T(8,128)(2,1)S(1)}, bf16[256,2048]{1,0:T(8,128)(2,1)S(1)}, u32[]{:S(2)}, u32[]{:S(2)}) collective-permute-start(bf16[256,2048]{1,0:T(8,128)(2,1)S(1)} %get-tuple-element.241), channel_id=1, source_target_pairs={{0,16},{1,17},{2,18},{3,19},{4,20},{5,21},{6,22},{7,23},{8,24},{9,... | collective-permute-start | bytes 3145736 | tf_op jit(solution)/shard_map/ppermute | solution.py:260
  263.4 56.2 %collective-permute-start.34 = (bf16[512,2048]{1,0:T(8,128)(2,1)S(1)}, bf16[512,2048]{1,0:T(8,128)(2,1)S(1)}, u32[]{:S(2)}, u32[]{:S(2)}) collective-permute-start(bf16[512,2048]{1,0:T(8,128)(2,1)S(1)} %pad_maximum_fusion.9), channel_id=1, source_target_pairs={{0,16},{1,17},{2,18},{3,19},{4,20},{5,21},{6,22},{7,23},{8,24},{9,... | collective-permute-start | bytes 6291464 | tf_op jit(solution)/shard_map/ppermute | solution.py:260
  264.7 54.9 %collective-permute-start.35 = (bf16[512,2048]{1,0:T(8,128)(2,1)S(1)}, bf16[512,2048]{1,0:T(8,128)(2,1)S(1)}, u32[]{:S(2)}, u32[]{:S(2)}) collective-permute-start(bf16[512,2048]{1,0:T(8,128)(2,1)S(1)} %pad_maximum_fusion.10), channel_id=1, source_target_pairs={{0,8},{1,9},{2,10},{3,11},{4,12},{5,13},{6,14},{7,15},{8,0},{9,1},... | collective-permute-start | bytes 6291464 | tf_op jit(solution)/shard_map/ppermute | solution.py:260
  292.9 47.4 %collective-permute-start.24 = (bf16[256,2048]{1,0:T(8,128)(2,1)S(1)}, bf16[256,2048]{1,0:T(8,128)(2,1)S(1)}, u32[]{:S(2)}, u32[]{:S(2)}) collective-permute-start(bf16[256,2048]{1,0:T(8,128)(2,1)S(1)} %fusion.28), channel_id=1, source_target_pairs={{0,1},{1,0},{2,3},{3,2},{4,5},{5,4},{6,7},{7,6},{8,9},{9,8},{10,11... | collective-permute-start | bytes 3145736 | tf_op jit(solution)/shard_map/ppermute | solution.py:260
  294.7 51.8 %collective-permute-start.25 = (bf16[256,2048]{1,0:T(8,128)(2,1)S(1)}, bf16[256,2048]{1,0:T(8,128)(2,1)S(1)}, u32[]{:S(2)}, u32[]{:S(2)}) collective-permute-start(bf16[256,2048]{1,0:T(8,128)(2,1)S(1)} %fusion.28), channel_id=1, source_target_pairs={{0,4},{1,5},{2,6},{3,7},{4,0},{5,1},{6,2},{7,3},{8,12},{9,13},{10,... | collective-permute-start | bytes 3145736 | tf_op jit(solution)/shard_map/ppermute | solution.py:260
  344.8 50.1 %collective-permute-start.42 = (bf16[2048,512]{1,0:T(8,128)(2,1)S(1)}, bf16[2048,512]{1,0:T(8,128)(2,1)S(1)}, u32[]{:S(2)}, u32[]{:S(2)}) collective-permute-start(bf16[2048,512]{1,0:T(8,128)(2,1)S(1)} %constant_dynamic-update-slice_fusion.6), channel_id=1, source_target_pairs={{0,8},{1,9},{2,10},{3,11},{4,12},{5,13},{6,14},{7,15},{8,0},{9,1},... | collective-permute-start | bytes 6291464 | tf_op jit(solution)/shard_map/ppermute | solution.py:260
  346.5 48.3 %collective-permute-start.41 = (bf16[2048,512]{1,0:T(8,128)(2,1)S(1)}, bf16[2048,512]{1,0:T(8,128)(2,1)S(1)}, u32[]{:S(2)}, u32[]{:S(2)}) collective-permute-start(bf16[2048,512]{1,0:T(8,128)(2,1)S(1)} %get-tuple-element.238), channel_id=1, source_target_pairs={{0,16},{1,17},{2,18},{3,19},{4,20},{5,21},{6,22},{7,23},{8,24},{9,... | collective-permute-start | bytes 6291464 | tf_op jit(solution)/shard_map/ppermute | solution.py:260
  376.2 49.3 %collective-permute-start.45 = (bf16[256,2048]{1,0:T(8,128)(2,1)S(1)}, bf16[256,2048]{1,0:T(8,128)(2,1)S(1)}, u32[]{:S(2)}, u32[]{:S(2)}) collective-permute-start(bf16[256,2048]{1,0:T(8,128)(2,1)S(1)} %copy-done.75), channel_id=1, source_target_pairs={{0,2},{1,3},{2,0},{3,1},{4,6},{5,7},{6,4},{7,5},{8,10},{9,11},{10,... | collective-permute-start | bytes 3145736 | tf_op jit(solution)/shard_map/ppermute | solution.py:260
  534.5 49.0 %collective-permute-start.50 = (bf16[256,2048]{1,0:T(8,128)(2,1)}, bf16[256,2048]{1,0:T(8,128)(2,1)}, u32[]{:S(2)}, u32[]{:S(2)}) collective-permute-start(bf16[256,2048]{1,0:T(8,128)(2,1)} %get-tuple-element.215), channel_id=1, source_target_pairs={{0,2},{1,3},{2,0},{3,1},{4,6},{5,7},{6,4},{7,5},{8,10},{9,11},{10,... | collective-permute-start | bytes 3145736 | tf_op jit(solution)/shard_map/ppermute | solution.py:260
  579.8 59.8 %collective-permute-start.62 = (bf16[2048,512]{1,0:T(8,128)(2,1)}, bf16[2048,512]{1,0:T(8,128)(2,1)}, u32[]{:S(2)}, u32[]{:S(2)}) collective-permute-start(bf16[2048,512]{1,0:T(8,128)(2,1)} %get-tuple-element.209), channel_id=1, source_target_pairs={{0,16},{1,17},{2,18},{3,19},{4,20},{5,21},{6,22},{7,23},{8,24},{9,... | collective-permute-start | bytes 6291464 | tf_op jit(solution)/shard_map/ppermute | solution.py:260
  581.0 58.6 %collective-permute-start.63 = (bf16[2048,512]{1,0:T(8,128)(2,1)}, bf16[2048,512]{1,0:T(8,128)(2,1)}, u32[]{:S(2)}, u32[]{:S(2)}) collective-permute-start(bf16[2048,512]{1,0:T(8,128)(2,1)} %get-tuple-element.208), channel_id=1, source_target_pairs={{0,8},{1,9},{2,10},{3,11},{4,12},{5,13},{6,14},{7,15},{8,0},{9,1},... | collective-permute-start | bytes 6291464 | tf_op jit(solution)/shard_map/ppermute | solution.py:260
  622.8 49.8 %collective-permute-start.59 = (bf16[256,2048]{1,0:T(8,128)(2,1)S(1)}, bf16[256,2048]{1,0:T(8,128)(2,1)}, u32[]{:S(2)}, u32[]{:S(2)}) collective-permute-start(bf16[256,2048]{1,0:T(8,128)(2,1)S(1)} %get-tuple-element.189), channel_id=1, source_target_pairs={{0,1},{1,0},{2,3},{3,2},{4,5},{5,4},{6,7},{7,6},{8,9},{9,8},{10,11... | collective-permute-start | bytes 3145736 | tf_op jit(solution)/shard_map/ppermute | solution.py:260
  624.8 58.9 %collective-permute-start.60 = (bf16[256,2048]{1,0:T(8,128)(2,1)S(1)}, bf16[256,2048]{1,0:T(8,128)(2,1)}, u32[]{:S(2)}, u32[]{:S(2)}) collective-permute-start(bf16[256,2048]{1,0:T(8,128)(2,1)S(1)} %get-tuple-element.189), channel_id=1, source_target_pairs={{0,4},{1,5},{2,6},{3,7},{4,0},{5,1},{6,2},{7,3},{8,12},{9,13},{10,... | collective-permute-start | bytes 3145736 | tf_op jit(solution)/shard_map/ppermute | solution.py:260
  672.6 48.0 %collective-permute-start.72 = (bf16[512,2048]{1,0:T(8,128)(2,1)}, bf16[512,2048]{1,0:T(8,128)(2,1)}, u32[]{:S(2)}, u32[]{:S(2)}) collective-permute-start(bf16[512,2048]{1,0:T(8,128)(2,1)} %get-tuple-element.205), channel_id=1, source_target_pairs={{0,16},{1,17},{2,18},{3,19},{4,20},{5,21},{6,22},{7,23},{8,24},{9,... | collective-permute-start | bytes 6291464 | tf_op jit(solution)/shard_map/ppermute | solution.py:260
  674.6 47.3 %collective-permute-start.73 = (bf16[512,2048]{1,0:T(8,128)(2,1)}, bf16[512,2048]{1,0:T(8,128)(2,1)}, u32[]{:S(2)}, u32[]{:S(2)}) collective-permute-start(bf16[512,2048]{1,0:T(8,128)(2,1)} %get-tuple-element.204), channel_id=1, source_target_pairs={{0,8},{1,9},{2,10},{3,11},{4,12},{5,13},{6,14},{7,15},{8,0},{9,1},... | collective-permute-start | bytes 6291464 | tf_op jit(solution)/shard_map/ppermute | solution.py:260
  743.1 48.7 %collective-permute-start.81 = (bf16[2048,256]{1,0:T(8,128)(2,1)}, bf16[2048,256]{1,0:T(8,128)(2,1)}, u32[]{:S(2)}, u32[]{:S(2)}) collective-permute-start(bf16[2048,256]{1,0:T(8,128)(2,1)} %get-tuple-element.233), channel_id=1, source_target_pairs={{0,2},{1,3},{2,0},{3,1},{4,6},{5,7},{6,4},{7,5},{8,10},{9,11},{10,... | collective-permute-start | bytes 3145736 | tf_op jit(solution)/shard_map/ppermute | solution.py:260
  744.6 41.8 %collective-permute-start.78 = (bf16[256,2048]{1,0:T(8,128)(2,1)}, bf16[256,2048]{1,0:T(8,128)(2,1)S(1)}, u32[]{:S(2)}, u32[]{:S(2)}) collective-permute-start(bf16[256,2048]{1,0:T(8,128)(2,1)} %split.147), channel_id=1, source_target_pairs={{0,8},{1,9},{2,10},{3,11},{4,12},{5,13},{6,14},{7,15},{8,0},{9,1},... | collective-permute-start | bytes 3145736 | tf_op jit(solution)/shard_map/ppermute | solution.py:260
  745.1 42.0 %collective-permute-start.79 = (bf16[256,2048]{1,0:T(8,128)(2,1)}, bf16[256,2048]{1,0:T(8,128)(2,1)}, u32[]{:S(2)}, u32[]{:S(2)}) collective-permute-start(bf16[256,2048]{1,0:T(8,128)(2,1)} %split.148), channel_id=1, source_target_pairs={{0,16},{1,17},{2,18},{3,19},{4,20},{5,21},{6,22},{7,23},{8,24},{9,... | collective-permute-start | bytes 3145736 | tf_op jit(solution)/shard_map/ppermute | solution.py:260
  759.6 47.7 %collective-permute-start.75 = (bf16[256,2048]{1,0:T(8,128)(2,1)}, bf16[256,2048]{1,0:T(8,128)(2,1)}, u32[]{:S(2)}, u32[]{:S(2)}) collective-permute-start(bf16[256,2048]{1,0:T(8,128)(2,1)} %slice.495), channel_id=1, source_target_pairs={{0,1},{1,0},{2,3},{3,2},{4,5},{5,4},{6,7},{7,6},{8,9},{9,8},{10,11... | collective-permute-start | bytes 3145736 | tf_op jit(solution)/shard_map/ppermute | solution.py:260
  831.7 47.6 %collective-permute-start.86 = (bf16[256,2048]{1,0:T(8,128)(2,1)S(1)}, bf16[256,2048]{1,0:T(8,128)(2,1)S(1)}, u32[]{:S(2)}, u32[]{:S(2)}) collective-permute-start(bf16[256,2048]{1,0:T(8,128)(2,1)S(1)} %get-tuple-element.231), channel_id=1, source_target_pairs={{0,2},{1,3},{2,0},{3,1},{4,6},{5,7},{6,4},{7,5},{8,10},{9,11},{10,... | collective-permute-start | bytes 3145736 | tf_op jit(solution)/shard_map/ppermute | solution.py:260
  850.7 47.4 %collective-permute-start.85 = (bf16[256,2048]{1,0:T(8,128)(2,1)S(1)}, bf16[256,2048]{1,0:T(8,128)(2,1)S(1)}, u32[]{:S(2)}, u32[]{:S(2)}) collective-permute-start(bf16[256,2048]{1,0:T(8,128)(2,1)S(1)} %slice.494), channel_id=1, source_target_pairs={{0,1},{1,0},{2,3},{3,2},{4,5},{5,4},{6,7},{7,6},{8,9},{9,8},{10,11... | collective-permute-start | bytes 3145736 | tf_op jit(solution)/shard_map/ppermute | solution.py:260
  859.1 47.5 %collective-permute-start.90 = (bf16[512,1536]{1,0:T(8,128)(2,1)}, bf16[512,1536]{1,0:T(8,128)(2,1)}, u32[]{:S(2)}, u32[]{:S(2)}) collective-permute-start(bf16[512,1536]{1,0:T(8,128)(2,1)} %split.156), channel_id=1, source_target_pairs={{0,8},{1,9},{2,10},{3,11},{4,12},{5,13},{6,14},{7,15},{8,0},{9,1},... | collective-permute-start | bytes 4718600 | tf_op jit(solution)/shard_map/ppermute | solution.py:260
  860.4 46.3 %collective-permute-start.89 = (bf16[512,1536]{1,0:T(8,128)(2,1)S(1)}, bf16[512,1536]{1,0:T(8,128)(2,1)}, u32[]{:S(2)}, u32[]{:S(2)}) collective-permute-start(bf16[512,1536]{1,0:T(8,128)(2,1)S(1)} %split.155), channel_id=1, source_target_pairs={{0,16},{1,17},{2,18},{3,19},{4,20},{5,21},{6,22},{7,23},{8,24},{9,... | collective-permute-start | bytes 4718600 | tf_op jit(solution)/shard_map/ppermute | solution.py:260
  861.8 54.0 %collective-permute-start.97 = (bf16[528,256]{1,0:T(8,128)(2,1)}, bf16[528,256]{1,0:T(8,128)(2,1)}, u32[]{:S(2)}, u32[]{:S(2)}) collective-permute-start(bf16[528,256]{1,0:T(8,128)(2,1)} %broadcast_select_fusion.28), channel_id=1, source_target_pairs={{0,4},{1,5},{2,6},{3,7},{4,0},{5,1},{6,2},{7,3},{8,12},{9,13},{10,... | collective-permute-start | bytes 811016 | tf_op jit(solution)/shard_map/ppermute | solution.py:260
  917.1 75.7 %collective-permute-start.88 = (bf16[256,2048]{1,0:T(8,128)(2,1)S(1)}, bf16[256,2048]{1,0:T(8,128)(2,1)S(1)}, u32[]{:S(2)}, u32[]{:S(2)}) collective-permute-start(bf16[256,2048]{1,0:T(8,128)(2,1)S(1)} %broadcast_select_fusion.8), channel_id=1, source_target_pairs={{0,2},{1,3},{2,0},{3,1},{4,6},{5,7},{6,4},{7,5},{8,10},{9,11},{10,... | collective-permute-start | bytes 3145736 | tf_op jit(solution)/shard_map/ppermute | solution.py:260
  955.3 53.6 %collective-permute-start.94 = (bf16[256,1536]{1,0:T(8,128)(2,1)S(1)}, bf16[256,1536]{1,0:T(8,128)(2,1)S(1)}, u32[]{:S(2)}, u32[]{:S(2)}) collective-permute-start(bf16[256,1536]{1,0:T(8,128)(2,1)S(1)} %broadcast_select_fusion.22), channel_id=1, source_target_pairs={{0,2},{1,3},{2,0},{3,1},{4,6},{5,7},{6,4},{7,5},{8,10},{9,11},{10,... | collective-permute-start | bytes 2359304 | tf_op jit(solution)/shard_map/ppermute | solution.py:260
  (178 other events, 2885.0 us)
